TPU v7x, 128 devices: a whole 4x4x4 slice. The times are simulated.
128 devices in a mesh: gx: 32 (over y, x, core), gy: 4 (over z).
Axes of the slice: x: 4, y: 4, z: 4, core: 2. Of those that a mesh axis runs over, the one named last changes fastest.
Arguments:
- probes: float32 [16, 512, 128, 256], P(None, 'gx', 'gy'), may hold values from -6 to 6
- diffusivity: float32 [512, 128, 256], P('gx', 'gy'), may hold values from 0.5 to 2
- wind_speed: float32 [3], replicated, may hold values from 0.5 to 2
- sensor_cell: int32 [32, 4, 128], P('gx', 'gy'), may hold values from 0 to 131071
- sensor_owner: int32 [32, 4, 128, 1], P('gx', 'gy'), may hold values from 0 to 127; in each aligned block of 128 rows (0 to 127, 128 to 255, ..., all dimensions but the last counted through in order) at most 2 rows name the same one
- sensor_count: int32 [32, 4], P('gx', 'gy'), may hold values from 64 to 128
- goal_weight: float32 [32, 4, 128, 16], P('gx', 'gy'), may hold values from -0.6 to 0.6
Outputs:
- fields: float32 [16, 512, 128, 256], P(None, 'gx', 'gy')
- goal_block: float32 [2048, 16], P(('gx', 'gy'))
- ritz_gram: float32 [16, 16], replicated
Inputs may be any that keep to these rules, and one draw needn't show every extreme that they name: `sensor_owner`: among the rows of one device, no owner is named more than 2 times, a bound that some block reaches.
All inputs are finite; a program needn't handle non-finite values.
Results may differ from a plain program's by a relative error of at most 0.0003.
Values sent between devices are 32-bit elements; how exact they have to be, the bound alone decides.
No kernel may reach another device: no remote copies, remote signals or barrier semaphores. Data moves between devices by JAX's collectives and lax.ppermute only.
A program may use at most 192 MiB of HBM per device.

v0:
```python
import functools

import jax
import jax.numpy as jnp
from jax import lax
from jax.sharding import Mesh
from jax.sharding import PartitionSpec as P

STEPS = 2
SWEEPS = 4
GX_GY = ("gx_0", "gx_1", "gx_2", "gy")
GX = ("gx_0", "gx_1", "gx_2")


time_step = 2.0


def with_halo(x, sides, width):
    edges = {}
    for axis, dim in sides:
        peers, length = (lax.axis_size(axis), x.shape[dim])
        up = [(i, (i + 1) % peers) for i in range(peers - 1)]
        last = lax.slice_in_dim(x, length - width, length, axis=dim)
        leading = lax.slice_in_dim(x, 0, width, axis=dim)
        edges[dim] = (
            lax.ppermute(last, axis, up),
            lax.ppermute(leading, axis, [(b, a) for a, b in up]),
        )
    done = []
    for _, dim in sides:
        low, high = edges[dim]
        around = [(width, width) if d in done else (0, 0) for d in range(x.ndim)]
        x = jnp.concatenate([jnp.pad(low, around), x, jnp.pad(high, around)], axis=dim)
        done.append(dim)
    return x


def by_axis(x, axes):
    return functools.reduce(lax.psum, axes, x)


def relax(padded, source, diffusion, wind_speed):
    centre = padded[..., 1:-1, 1:-1, :]
    widths = [(0, 0)] * (centre.ndim - 1) + [(1, 1)]
    zpadded = jnp.pad(centre, widths)
    beside = padded[..., 2:, 1:-1, :] + padded[..., :-2, 1:-1, :]
    beside = beside + padded[..., 1:-1, 2:, :] + padded[..., 1:-1, :-2, :]
    beside = beside + zpadded[..., 2:] + zpadded[..., :-2]
    upwind = (
        wind_speed[0] * padded[..., :-2, 1:-1, :]
        + wind_speed[1] * padded[..., 1:-1, :-2, :]
        + wind_speed[2] * zpadded[..., :-2]
    )
    diagonal = 1.0 + time_step * (6.0 * diffusion + wind_speed[0] + wind_speed[1] + wind_speed[2])
    updated = (source + time_step * (diffusion * beside + upwind)) / diagonal
    return jnp.where(diffusion > 0.0, updated, 0.0)


def body(probes, diffusivity, wind_speed, sensor_cell, sensor_owner, sensor_count, goal_weight):
    state_field = probes
    for step_index in range(STEPS):
        source = state_field
        for sweep_index in range(SWEEPS):
            padded = with_halo(state_field, ((GX, 1), ("gy", 2)), 1)
            state_field = relax(padded, source, diffusivity, wind_speed)
    probe_count = state_field.shape[0]
    sensor_rows = sensor_cell.shape[2]
    goal_count = goal_weight.shape[3]
    device_count = lax.axis_size(GX) * lax.axis_size("gy")
    capacity = max(2, (sensor_rows + device_count - 1) // device_count)
    flattened = state_field.reshape(probe_count, -1)
    readings = jnp.take(flattened, sensor_cell.reshape(-1), axis=1)
    row_index = jnp.arange(sensor_rows, dtype=jnp.int32)
    active = (row_index < sensor_count.reshape(())).astype(jnp.float32)
    readings = readings.T * active[:, None]
    weights = goal_weight.reshape(sensor_rows, goal_count)
    owners = sensor_owner.reshape(sensor_rows)
    earlier = (owners[None, :] == owners[:, None]) & (row_index[None, :] < row_index[:, None])
    slot_rank = jnp.sum(earlier.astype(jnp.int32), axis=1)
    slot_index = owners * capacity + slot_rank
    placing = (
        jnp.arange(device_count * capacity, dtype=jnp.int32)[:, None] == slot_index[None, :]
    ).astype(jnp.float32)
    payload = jnp.concatenate([readings, weights], axis=1)
    outgoing = jnp.dot(placing, payload, precision=lax.Precision.HIGHEST).reshape(
        device_count, capacity, probe_count + goal_count
    )
    received = lax.all_to_all(outgoing, GX_GY, split_axis=0, concat_axis=0, tiled=True)
    goal_block = jnp.einsum(
        "scj,scp->jp",
        received[..., probe_count:],
        received[..., :probe_count],
        precision=lax.Precision.HIGHEST,
    )
    ritz_gram = by_axis(jnp.dot(goal_block.T, goal_block, precision=lax.Precision.HIGHEST), GX_GY)
    return (state_field, goal_block, ritz_gram)


def solution(mesh):
    torus = Mesh(mesh.devices.reshape(4, 4, 2, mesh.shape["gy"]), ("gx_0", "gx_1", "gx_2", "gy"))
    return jax.shard_map(
        body,
        mesh=torus,
        in_specs=(
            P(None, GX, "gy", None),
            P(GX, "gy", None),
            P(),
            P(GX, "gy", None),
            P(GX, "gy", None, None),
            P(GX, "gy"),
            P(GX, "gy", None, None),
        ),
        out_specs=(P(None, GX, "gy", None), P(GX_GY, None), P()),
        check_vma=False,
    )
```

profile of v0, /device:TPU:1, one launch (start us, length us, event | category | flops | bytes accessed | tf_op | source)
XLA Modules:
  0.0 479.0 jit_solution(9704484255742798876)
XLA Ops:
  1.9 4.5 collective-permute-start.1
  6.4 1.9 collective-permute-start
  8.4 2.6 fusion.147
  12.4 4.2 collective-permute-start.3
  16.6 1.4 fusion.150
  18.0 3.1 multiply_add_fusion
  23.6 9.0 %constant_dynamic-update-slice_fusion.1 = f32[16,18,32,256]{3,2,1,0:T(8,128)} fusion(f32[16,18,32,256]{3,2,1,0:T(8,128)} %constant_dynamic-update-slice_fusion.2, f32[16,16,32,256]{3,2,1,0:T(8,128)} %param.7), kind=kLoop, calls=%fused_computation.220 | loop fusion | bytes 16777216
  33.4 16.2 %fusion.122 = f32[16,16,32,256]{3,2,1,0:T(8,128)} fusion(f32[16,16,32,256]{3,2,1,0:T(8,128)S(1)} %bitcast.21, f32[16,18,32,256]{3,2,1,0:T(8,128)} %constant_dynamic-update-slice_fusion, f32[16,16,1,256]{3,2,1,0:T(1,128)S(1)} %copy.158, f32[16,16,1,256]{3,2,1,0:T(1,128)S(1)} %copy.157, f32[16,1,32,256]{3,2,1,0:T(8,128)S(1)} %collective-permute-done.1, ...), kind=kLoop, calls=%fused_computation.203 | loop fusion | flops 54525952 | bytes 28966924 | tf_op jit(solution)/shard_map/jit(_where)/select_n | solution.py:56
  49.7 1.3 fusion.146
  51.0 1.9 collective-permute-start.4
  52.9 4.0 collective-permute-start.5
  56.9 2.6 fusion.145
  61.0 4.3 collective-permute-start.7
  65.3 3.2 collective-permute-done.6
  68.7 1.5 collective-permute-done.7
  70.5 26.7 %fusion.121 = f32[16,16,32,256]{3,2,1,0:T(8,128)} fusion(f32[16,16,32,256]{3,2,1,0:T(8,128)S(1)} %bitcast.21, f32[16,16,32,256]{3,2,1,0:T(8,128)} %fusion.122, f32[16,1,32,256]{3,2,1,0:T(8,128)S(1)} %collective-permute-done.4, f32[16,1,32,256]{3,2,1,0:T(8,128)S(1)} %collective-permute-done.5, f32[16,16,1,256]{3,2,1,0:T(1,128)S(1)} %copy.122, ...), kind=kLoop, calls=%fused_computation.202 | loop fusion | flops 62914560 | bytes 27918348 | tf_op jit(solution)/shard_map/jit(_where)/select_n | solution.py:56
  97.2 1.3 fusion.144
  98.5 1.9 collective-permute-start.8
  100.4 4.4 collective-permute-start.9
  104.8 2.6 fusion.143
  108.9 4.9 %collective-permute-start.11 = (f32[16,16,1,256]{3,1,2,0:T(8,128)S(1)}, f32[16,16,1,256]{3,1,2,0:T(8,128)S(1)}, u32[]{:S(2)}, u32[]{:S(2)}) collective-permute-start(f32[16,16,1,256]{3,1,2,0:T(8,128)S(1)} %copy.125), channel_id=1, source_target_pairs={{0,1},{1,2},{2,3},{4,5},{5,6},{6,7},{8,9},{9,10},{10,11},{12,13},{... | collective-permute-start | bytes 786440 | tf_op jit(solution)/shard_map/ppermute | solution.py:26
  113.8 2.3 collective-permute-done.10
  116.4 1.5 collective-permute-done.11
  118.2 26.8 %fusion.120 = f32[16,16,32,256]{3,2,1,0:T(8,128)} fusion(f32[16,16,32,256]{3,2,1,0:T(8,128)S(1)} %bitcast.21, f32[16,16,32,256]{3,2,1,0:T(8,128)} %fusion.121, f32[16,1,32,256]{3,2,1,0:T(8,128)S(1)} %collective-permute-done.8, f32[16,1,32,256]{3,2,1,0:T(8,128)S(1)} %collective-permute-done.9, f32[16,16,1,256]{3,2,1,0:T(1,128)S(1)} %copy.126, ...), kind=kLoop, calls=%fused_computation.201 | loop fusion | flops 62914560 | bytes 27918348 | tf_op jit(solution)/shard_map/jit(_where)/select_n | solution.py:56
  145.1 1.3 fusion.142
  146.4 1.9 collective-permute-start.12
  148.3 4.7 collective-permute-start.13
  153.1 2.6 fusion.141
  157.1 4.8 collective-permute-start.15
  161.8 2.2 collective-permute-done.14
  164.3 1.5 collective-permute-done.15
  166.1 26.7 %fusion.119 = f32[16,16,32,256]{3,2,1,0:T(8,128)} fusion(f32[16,16,32,256]{3,2,1,0:T(8,128)S(1)} %bitcast.21, f32[16,16,32,256]{3,2,1,0:T(8,128)} %fusion.120, f32[16,1,32,256]{3,2,1,0:T(8,128)S(1)} %collective-permute-done.12, f32[16,1,32,256]{3,2,1,0:T(8,128)S(1)} %collective-permute-done.13, f32[16,16,1,256]{3,2,1,0:T(1,128)S(1)} %copy.130, ...), kind=kLoop, calls=%fused_computation.200 | loop fusion | flops 62914560 | bytes 27918348 | tf_op jit(solution)/shard_map/jit(_where)/select_n | solution.py:56
  194.1 1.9 collective-permute-start.16
  196.0 5.1 %collective-permute-start.17 = (f32[16,1,32,256]{3,2,1,0:T(8,128)S(1)}, f32[16,1,32,256]{3,2,1,0:T(8,128)S(1)}, u32[]{:S(2)}, u32[]{:S(2)}) collective-permute-start(f32[16,1,32,256]{3,2,1,0:T(8,128)S(1)} %get-tuple-element.20), channel_id=1, source_target_pairs={{0,4},{4,8},{8,12},{12,16},{16,20},{20,24},{24,28},{28,32},{32,36}... | collective-permute-start | bytes 1572872 | tf_op jit(solution)/shard_map/ppermute | solution.py:26
  201.1 2.6 fusion.139
  205.1 4.8 collective-permute-start.19
  209.9 1.8 collective-permute-done.18
  212.0 1.5 collective-permute-done.19
  213.8 30.8 %fusion.115 = f32[16,16,32,256]{3,2,1,0:T(8,128)} fusion(f32[16,16,32,256]{3,2,1,0:T(8,128)} %fusion.119, f32[16,1,32,256]{3,2,1,0:T(8,128)S(1)} %collective-permute-done.16, f32[16,1,32,256]{3,2,1,0:T(8,128)S(1)} %collective-permute-done.17, f32[16,16,1,256]{3,2,1,0:T(1,128)S(1)} %copy.134, f32[16,16,1,256]{3,2,1,0:T(1,128)S(1)} %copy.132, ...), kind=kLoop, calls=%fused_computation.196 | loop fusion | flops 62914560 | bytes 19529740 | tf_op jit(solution)/shard_map/jit(_where)/select_n | solution.py:56
  244.6 1.3 fusion.138
  245.9 1.9 collective-permute-start.20
  247.8 5.5 %collective-permute-start.21 = (f32[16,1,32,256]{3,2,1,0:T(8,128)S(1)}, f32[16,1,32,256]{3,2,1,0:T(8,128)S(1)}, u32[]{:S(2)}, u32[]{:S(2)}) collective-permute-start(f32[16,1,32,256]{3,2,1,0:T(8,128)S(1)} %get-tuple-element.16), channel_id=1, source_target_pairs={{0,4},{4,8},{8,12},{12,16},{16,20},{20,24},{24,28},{28,32},{32,36}... | collective-permute-start | bytes 1572872 | tf_op jit(solution)/shard_map/ppermute | solution.py:26
  253.3 2.6 fusion.137
  257.3 5.0 %collective-permute-start.23 = (f32[16,16,1,256]{3,1,2,0:T(8,128)S(1)}, f32[16,16,1,256]{3,1,2,0:T(8,128)S(1)}, u32[]{:S(2)}, u32[]{:S(2)}) collective-permute-start(f32[16,16,1,256]{3,1,2,0:T(8,128)S(1)} %copy.137), channel_id=1, source_target_pairs={{0,1},{1,2},{2,3},{4,5},{5,6},{6,7},{8,9},{9,10},{10,11},{12,13},{... | collective-permute-start | bytes 786440 | tf_op jit(solution)/shard_map/ppermute | solution.py:26
  262.3 1.5 collective-permute-done.22
  265.7 26.6 %fusion.118 = f32[16,16,32,256]{3,2,1,0:T(8,128)} fusion(f32[16,16,32,256]{3,2,1,0:T(8,128)S(1)} %bitcast.23, f32[16,16,32,256]{3,2,1,0:T(8,128)} %fusion.115, f32[16,1,32,256]{3,2,1,0:T(8,128)S(1)} %collective-permute-done.20, f32[16,1,32,256]{3,2,1,0:T(8,128)S(1)} %collective-permute-done.21, f32[16,16,1,256]{3,2,1,0:T(1,128)S(1)} %copy.138, ...), kind=kLoop, calls=%fused_computation.199 | loop fusion | flops 62914560 | bytes 27918348 | tf_op jit(solution)/shard_map/jit(_where)/select_n | solution.py:56
  293.6 1.9 collective-permute-start.24
  295.5 5.8 %collective-permute-start.25 = (f32[16,1,32,256]{3,2,1,0:T(8,128)S(1)}, f32[16,1,32,256]{3,2,1,0:T(8,128)S(1)}, u32[]{:S(2)}, u32[]{:S(2)}) collective-permute-start(f32[16,1,32,256]{3,2,1,0:T(8,128)S(1)} %get-tuple-element.12), channel_id=1, source_target_pairs={{0,4},{4,8},{8,12},{12,16},{16,20},{20,24},{24,28},{28,32},{32,36}... | collective-permute-start | bytes 1572872 | tf_op jit(solution)/shard_map/ppermute | solution.py:26
  301.3 2.6 fusion.135
  305.3 4.8 collective-permute-start.27
  313.6 27.4 %fusion.117 = f32[16,16,32,256]{3,2,1,0:T(8,128)} fusion(f32[16,16,32,256]{3,2,1,0:T(8,128)S(1)} %bitcast.23, f32[16,16,32,256]{3,2,1,0:T(8,128)} %fusion.118, f32[16,1,32,256]{3,2,1,0:T(8,128)S(1)} %collective-permute-done.24, f32[16,1,32,256]{3,2,1,0:T(8,128)S(1)} %collective-permute-done.25, f32[16,16,1,256]{3,2,1,0:T(1,128)S(1)} %copy.142, ...), kind=kLoop, calls=%fused_computation.198 | loop fusion | flops 62914560 | bytes 27918348 | tf_op jit(solution)/shard_map/jit(_where)/select_n | solution.py:56
  342.4 1.9 collective-permute-start.28
  344.3 5.8 %collective-permute-start.29 = (f32[16,1,32,256]{3,2,1,0:T(8,128)S(1)}, f32[16,1,32,256]{3,2,1,0:T(8,128)S(1)}, u32[]{:S(2)}, u32[]{:S(2)}) collective-permute-start(f32[16,1,32,256]{3,2,1,0:T(8,128)S(1)} %get-tuple-element.8), channel_id=1, source_target_pairs={{0,4},{4,8},{8,12},{12,16},{16,20},{20,24},{24,28},{28,32},{32,36}... | collective-permute-start | bytes 1572872 | tf_op jit(solution)/shard_map/ppermute | solution.py:26
  350.1 2.6 fusion.133
  354.1 4.8 collective-permute-start.31
  358.9 1.8 collective-permute-done.30
  362.4 26.8 %fusion.116 = f32[16,16,32,256]{3,2,1,0:T(8,128)} fusion(f32[16,16,32,256]{3,2,1,0:T(8,128)S(1)} %bitcast.23, f32[16,16,32,256]{3,2,1,0:T(8,128)} %fusion.117, f32[16,1,32,256]{3,2,1,0:T(8,128)S(1)} %collective-permute-done.28, f32[16,1,32,256]{3,2,1,0:T(8,128)S(1)} %collective-permute-done.29, f32[16,16,1,256]{3,2,1,0:T(1,128)S(1)} %copy.146, ...), kind=kLoop, calls=%fused_computation.197 | loop fusion | flops 62914560 | bytes 27918348 | tf_op jit(solution)/shard_map/jit(_where)/select_n | solution.py:56
  389.3 35.0 %copy.147 = f32[16,16,32,256]{0,3,2,1:T(8,128)} copy(f32[16,16,32,256]{3,2,1,0:T(8,128)} %fusion.116) | data formatting | bytes 16777216 | tf_op jit(solution)/shard_map/jit(_where)/select_n | solution.py:56
  424.3 1.8 gather_fusion
  426.3 23.9 %all_to_all.5 = f32[128,2,32]{2,1,0:T(2,128)S(1)} all-to-all(f32[128,2,32]{2,1,0:T(2,128)S(1)} %bitcast.24), channel_id=1, replica_groups=mesh['gx_0'=4,'gx_1'=4,'gx_2'=2,'gy'=4] {'gx_0','gx_1','gx_2','gy'}, dimensions={0} | all-to-all | bytes 65536 | tf_op jit(solution)/shard_map/all_to_all | solution.py:88
  451.0 6.9 %psum.28 = f32[16,16]{1,0:T(8,128)S(1)} all-reduce(f32[16,16]{1,0:T(8,128)S(1)} %fusion.151), channel_id=1, replica_groups=mesh['gx_0'=4,'gx_1'=4,'gx_2'=2,'gy'=4] {'gx_0'}, use_global_device_ids=true, to_apply=%region_1.2 | all-reduce | flops 256 | bytes 2048 | tf_op jit(solution)/shard_map/psum | solution.py:39
  458.0 6.5 %psum.29 = f32[16,16]{1,0:T(8,128)S(1)} all-reduce(f32[16,16]{1,0:T(8,128)S(1)} %psum.28), channel_id=1, replica_groups=mesh['gx_0'=4,'gx_1'=4,'gx_2'=2,'gy'=4] {'gx_1'}, use_global_device_ids=true, to_apply=%region_2.3 | all-reduce | flops 256 | bytes 2048 | tf_op jit(solution)/shard_map/psum | solution.py:39
  464.5 7.3 %psum.30 = f32[16,16]{1,0:T(8,128)S(1)} all-reduce(f32[16,16]{1,0:T(8,128)S(1)} %psum.29), channel_id=1, replica_groups=mesh['gx_0'=4,'gx_1'=4,'gx_2'=2,'gy'=4] {'gx_2'}, use_global_device_ids=true, to_apply=%region_3.4 | all-reduce | flops 256 | bytes 2048 | tf_op jit(solution)/shard_map/psum | solution.py:39
  471.8 7.2 %psum.31 = f32[16,16]{1,0:T(8,128)} all-reduce(f32[16,16]{1,0:T(8,128)S(1)} %psum.30), channel_id=1, replica_groups=mesh['gx_0'=4,'gx_1'=4,'gx_2'=2,'gy'=4] {'gy'}, use_global_device_ids=true, to_apply=%region_4.5 | all-reduce | flops 256 | bytes 2048 | tf_op jit(solution)/shard_map/psum | solution.py:39
  (100 shorter events, 28.9 us)
Async XLA Ops:
  1.9 20.8 %collective-permute-start.1 = (f32[16,1,32,256]{3,2,1,0:T(8,128)S(1)}, f32[16,1,32,256]{3,2,1,0:T(8,128)S(1)}, u32[]{:S(2)}, u32[]{:S(2)}) collective-permute-start(f32[16,1,32,256]{3,2,1,0:T(8,128)S(1)} %get-tuple-element.37), channel_id=1, source_target_pairs={{0,4},{4,8},{8,12},{12,16},{16,20},{20,24},{24,28},{28,32},{32,36}... | collective-permute-start | bytes 1572872 | tf_op jit(solution)/shard_map/ppermute | solution.py:26
  6.4 26.1 %collective-permute-start = (f32[16,1,32,256]{3,2,1,0:T(8,128)S(1)}, f32[16,1,32,256]{3,2,1,0:T(8,128)S(1)}, u32[]{:S(2)}, u32[]{:S(2)}) collective-permute-start(f32[16,1,32,256]{3,2,1,0:T(8,128)S(1)} %get-tuple-element.36), channel_id=1, source_target_pairs={{4,0},{8,4},{12,8},{16,12},{20,16},{24,20},{28,24},{32,28},{36,32}... | collective-permute-start | bytes 1572872 | tf_op jit(solution)/shard_map/ppermute | solution.py:27
  11.0 11.1 %collective-permute-start.2 = (f32[16,16,1,256]{3,1,2,0:T(8,128)S(1)}, f32[16,16,1,256]{3,1,2,0:T(8,128)S(1)}, u32[]{:S(2)}, u32[]{:S(2)}) collective-permute-start(f32[16,16,1,256]{3,1,2,0:T(8,128)S(1)} %copy.153), channel_id=1, source_target_pairs={{1,0},{2,1},{3,2},{5,4},{6,5},{7,6},{9,8},{10,9},{11,10},{13,12},{... | collective-permute-start | bytes 786440 | tf_op jit(solution)/shard_map/ppermute | solution.py:27
  12.4 10.1 %collective-permute-start.3 = (f32[16,16,1,256]{3,1,2,0:T(8,128)S(1)}, f32[16,16,1,256]{3,1,2,0:T(8,128)S(1)}, u32[]{:S(2)}, u32[]{:S(2)}) collective-permute-start(f32[16,16,1,256]{3,1,2,0:T(8,128)S(1)} %copy.154), channel_id=1, source_target_pairs={{0,1},{1,2},{2,3},{4,5},{5,6},{6,7},{8,9},{9,10},{10,11},{12,13},{... | collective-permute-start | bytes 786440 | tf_op jit(solution)/shard_map/ppermute | solution.py:26
  22.8 10.7 %slice-start = ((s8[8388608]{0:T(1024)(128)(4,1)}), s8[4194304]{0:T(1024)(128)(4,1)S(1)}, s32[]{:S(2)}) async-start(s8[8388608]{0:T(1024)(128)(4,1)} %bitcast.20), calls=%async_computation.1 | async-start | bytes 8388608
  23.6 9.8 %slice-start.1 = ((s8[8388608]{0:T(1024)(128)(4,1)}), s8[4194304]{0:T(1024)(128)(4,1)S(1)}, s32[]{:S(2)}) async-start(s8[8388608]{0:T(1024)(128)(4,1)} %bitcast.20), calls=%async_computation.2 | async-start | bytes 8388608
  23.6 9.8 %copy-start = (f32[16,32,256]{2,1,0:T(8,128)S(1)}, f32[16,32,256]{2,1,0:T(8,128)}, u32[]{:S(2)}) copy-start(f32[16,32,256]{2,1,0:T(8,128)} %param.8) | copy-start | bytes 1572868
  51.0 19.5 %collective-permute-start.4 = (f32[16,1,32,256]{3,2,1,0:T(8,128)S(1)}, f32[16,1,32,256]{3,2,1,0:T(8,128)S(1)}, u32[]{:S(2)}, u32[]{:S(2)}) collective-permute-start(f32[16,1,32,256]{3,2,1,0:T(8,128)S(1)} %get-tuple-element.33), channel_id=1, source_target_pairs={{4,0},{8,4},{12,8},{16,12},{20,16},{24,20},{28,24},{32,28},{36,32}... | collective-permute-start | bytes 1572872 | tf_op jit(solution)/shard_map/ppermute | solution.py:27
  52.9 17.6 %collective-permute-start.5 = (f32[16,1,32,256]{3,2,1,0:T(8,128)S(1)}, f32[16,1,32,256]{3,2,1,0:T(8,128)S(1)}, u32[]{:S(2)}, u32[]{:S(2)}) collective-permute-start(f32[16,1,32,256]{3,2,1,0:T(8,128)S(1)} %get-tuple-element.32), channel_id=1, source_target_pairs={{0,4},{4,8},{8,12},{12,16},{16,20},{20,24},{24,28},{28,32},{32,36}... | collective-permute-start | bytes 1572872 | tf_op jit(solution)/shard_map/ppermute | solution.py:26
  59.6 8.8 %collective-permute-start.6 = (f32[16,16,1,256]{3,1,2,0:T(8,128)S(1)}, f32[16,16,1,256]{3,1,2,0:T(8,128)S(1)}, u32[]{:S(2)}, u32[]{:S(2)}) collective-permute-start(f32[16,16,1,256]{3,1,2,0:T(8,128)S(1)} %copy.119), channel_id=1, source_target_pairs={{1,0},{2,1},{3,2},{5,4},{6,5},{7,6},{9,8},{10,9},{11,10},{13,12},{... | collective-permute-start | bytes 786440 | tf_op jit(solution)/shard_map/ppermute | solution.py:27
  61.0 9.3 %collective-permute-start.7 = (f32[16,16,1,256]{3,1,2,0:T(8,128)S(1)}, f32[16,16,1,256]{3,1,2,0:T(8,128)S(1)}, u32[]{:S(2)}, u32[]{:S(2)}) collective-permute-start(f32[16,16,1,256]{3,1,2,0:T(8,128)S(1)} %copy.121), channel_id=1, source_target_pairs={{0,1},{1,2},{2,3},{4,5},{5,6},{6,7},{8,9},{9,10},{10,11},{12,13},{... | collective-permute-start | bytes 786440 | tf_op jit(solution)/shard_map/ppermute | solution.py:26
  98.5 19.7 %collective-permute-start.8 = (f32[16,1,32,256]{3,2,1,0:T(8,128)S(1)}, f32[16,1,32,256]{3,2,1,0:T(8,128)S(1)}, u32[]{:S(2)}, u32[]{:S(2)}) collective-permute-start(f32[16,1,32,256]{3,2,1,0:T(8,128)S(1)} %get-tuple-element.29), channel_id=1, source_target_pairs={{4,0},{8,4},{12,8},{16,12},{20,16},{24,20},{28,24},{32,28},{36,32}... | collective-permute-start | bytes 1572872 | tf_op jit(solution)/shard_map/ppermute | solution.py:27
  100.4 17.8 %collective-permute-start.9 = (f32[16,1,32,256]{3,2,1,0:T(8,128)S(1)}, f32[16,1,32,256]{3,2,1,0:T(8,128)S(1)}, u32[]{:S(2)}, u32[]{:S(2)}) collective-permute-start(f32[16,1,32,256]{3,2,1,0:T(8,128)S(1)} %get-tuple-element.28), channel_id=1, source_target_pairs={{0,4},{4,8},{8,12},{12,16},{16,20},{20,24},{24,28},{28,32},{32,36}... | collective-permute-start | bytes 1572872 | tf_op jit(solution)/shard_map/ppermute | solution.py:26
  107.5 8.6 %collective-permute-start.10 = (f32[16,16,1,256]{3,1,2,0:T(8,128)S(1)}, f32[16,16,1,256]{3,1,2,0:T(8,128)S(1)}, u32[]{:S(2)}, u32[]{:S(2)}) collective-permute-start(f32[16,16,1,256]{3,1,2,0:T(8,128)S(1)} %copy.123), channel_id=1, source_target_pairs={{1,0},{2,1},{3,2},{5,4},{6,5},{7,6},{9,8},{10,9},{11,10},{13,12},{... | collective-permute-start | bytes 786440 | tf_op jit(solution)/shard_map/ppermute | solution.py:27
  108.9 9.1 %collective-permute-start.11 = (f32[16,16,1,256]{3,1,2,0:T(8,128)S(1)}, f32[16,16,1,256]{3,1,2,0:T(8,128)S(1)}, u32[]{:S(2)}, u32[]{:S(2)}) collective-permute-start(f32[16,16,1,256]{3,1,2,0:T(8,128)S(1)} %copy.125), channel_id=1, source_target_pairs={{0,1},{1,2},{2,3},{4,5},{5,6},{6,7},{8,9},{9,10},{10,11},{12,13},{... | collective-permute-start | bytes 786440 | tf_op jit(solution)/shard_map/ppermute | solution.py:26
  146.4 19.7 %collective-permute-start.12 = (f32[16,1,32,256]{3,2,1,0:T(8,128)S(1)}, f32[16,1,32,256]{3,2,1,0:T(8,128)S(1)}, u32[]{:S(2)}, u32[]{:S(2)}) collective-permute-start(f32[16,1,32,256]{3,2,1,0:T(8,128)S(1)} %get-tuple-element.25), channel_id=1, source_target_pairs={{4,0},{8,4},{12,8},{16,12},{20,16},{24,20},{28,24},{32,28},{36,32}... | collective-permute-start | bytes 1572872 | tf_op jit(solution)/shard_map/ppermute | solution.py:27
  148.3 17.8 %collective-permute-start.13 = (f32[16,1,32,256]{3,2,1,0:T(8,128)S(1)}, f32[16,1,32,256]{3,2,1,0:T(8,128)S(1)}, u32[]{:S(2)}, u32[]{:S(2)}) collective-permute-start(f32[16,1,32,256]{3,2,1,0:T(8,128)S(1)} %get-tuple-element.24), channel_id=1, source_target_pairs={{0,4},{4,8},{8,12},{12,16},{16,20},{20,24},{24,28},{28,32},{32,36}... | collective-permute-start | bytes 1572872 | tf_op jit(solution)/shard_map/ppermute | solution.py:26
  155.7 8.3 %collective-permute-start.14 = (f32[16,16,1,256]{3,1,2,0:T(8,128)S(1)}, f32[16,16,1,256]{3,1,2,0:T(8,128)S(1)}, u32[]{:S(2)}, u32[]{:S(2)}) collective-permute-start(f32[16,16,1,256]{3,1,2,0:T(8,128)S(1)} %copy.127), channel_id=1, source_target_pairs={{1,0},{2,1},{3,2},{5,4},{6,5},{7,6},{9,8},{10,9},{11,10},{13,12},{... | collective-permute-start | bytes 786440 | tf_op jit(solution)/shard_map/ppermute | solution.py:27
  157.1 8.7 %collective-permute-start.15 = (f32[16,16,1,256]{3,1,2,0:T(8,128)S(1)}, f32[16,16,1,256]{3,1,2,0:T(8,128)S(1)}, u32[]{:S(2)}, u32[]{:S(2)}) collective-permute-start(f32[16,16,1,256]{3,1,2,0:T(8,128)S(1)} %copy.129), channel_id=1, source_target_pairs={{0,1},{1,2},{2,3},{4,5},{5,6},{6,7},{8,9},{9,10},{10,11},{12,13},{... | collective-permute-start | bytes 786440 | tf_op jit(solution)/shard_map/ppermute | solution.py:26
  194.1 19.7 %collective-permute-start.16 = (f32[16,1,32,256]{3,2,1,0:T(8,128)S(1)}, f32[16,1,32,256]{3,2,1,0:T(8,128)S(1)}, u32[]{:S(2)}, u32[]{:S(2)}) collective-permute-start(f32[16,1,32,256]{3,2,1,0:T(8,128)S(1)} %get-tuple-element.21), channel_id=1, source_target_pairs={{4,0},{8,4},{12,8},{16,12},{20,16},{24,20},{28,24},{32,28},{36,32}... | collective-permute-start | bytes 1572872 | tf_op jit(solution)/shard_map/ppermute | solution.py:27
  196.0 17.8 %collective-permute-start.17 = (f32[16,1,32,256]{3,2,1,0:T(8,128)S(1)}, f32[16,1,32,256]{3,2,1,0:T(8,128)S(1)}, u32[]{:S(2)}, u32[]{:S(2)}) collective-permute-start(f32[16,1,32,256]{3,2,1,0:T(8,128)S(1)} %get-tuple-element.20), channel_id=1, source_target_pairs={{0,4},{4,8},{8,12},{12,16},{16,20},{20,24},{24,28},{28,32},{32,36}... | collective-permute-start | bytes 1572872 | tf_op jit(solution)/shard_map/ppermute | solution.py:26
  203.8 7.9 %collective-permute-start.18 = (f32[16,16,1,256]{3,1,2,0:T(8,128)S(1)}, f32[16,16,1,256]{3,1,2,0:T(8,128)S(1)}, u32[]{:S(2)}, u32[]{:S(2)}) collective-permute-start(f32[16,16,1,256]{3,1,2,0:T(8,128)S(1)} %copy.131), channel_id=1, source_target_pairs={{1,0},{2,1},{3,2},{5,4},{6,5},{7,6},{9,8},{10,9},{11,10},{13,12},{... | collective-permute-start | bytes 786440 | tf_op jit(solution)/shard_map/ppermute | solution.py:27
  205.1 8.4 %collective-permute-start.19 = (f32[16,16,1,256]{3,1,2,0:T(8,128)S(1)}, f32[16,16,1,256]{3,1,2,0:T(8,128)S(1)}, u32[]{:S(2)}, u32[]{:S(2)}) collective-permute-start(f32[16,16,1,256]{3,1,2,0:T(8,128)S(1)} %copy.133), channel_id=1, source_target_pairs={{0,1},{1,2},{2,3},{4,5},{5,6},{6,7},{8,9},{9,10},{10,11},{12,13},{... | collective-permute-start | bytes 786440 | tf_op jit(solution)/shard_map/ppermute | solution.py:26
  213.5 52.2 %slice-start.2 = ((s8[8388608]{0:T(1024)(128)(4,1)}), s8[4194304]{0:T(1024)(128)(4,1)S(1)}, s32[]{:S(2)}) async-start(s8[8388608]{0:T(1024)(128)(4,1)} %bitcast.22), calls=%async_computation.3 | async-start | bytes 8388608
  213.8 48.5 %copy-start.3 = (s32[1,1,128]{2,1,0:T(1,128)S(1)}, s32[1,1,128]{2,1,0:T(1,128)}, u32[]{:S(2)}) copy-start(s32[1,1,128]{2,1,0:T(1,128)} %param.10) | copy-start | bytes 1540
  213.8 51.9 %slice-start.3 = ((s8[8388608]{0:T(1024)(128)(4,1)}), s8[4194304]{0:T(1024)(128)(4,1)S(1)}, s32[]{:S(2)}) async-start(s8[8388608]{0:T(1024)(128)(4,1)} %bitcast.22), calls=%async_computation.4 | async-start | bytes 8388608
  245.9 19.7 %collective-permute-start.20 = (f32[16,1,32,256]{3,2,1,0:T(8,128)S(1)}, f32[16,1,32,256]{3,2,1,0:T(8,128)S(1)}, u32[]{:S(2)}, u32[]{:S(2)}) collective-permute-start(f32[16,1,32,256]{3,2,1,0:T(8,128)S(1)} %get-tuple-element.17), channel_id=1, source_target_pairs={{4,0},{8,4},{12,8},{16,12},{20,16},{24,20},{28,24},{32,28},{36,32}... | collective-permute-start | bytes 1572872 | tf_op jit(solution)/shard_map/ppermute | solution.py:27
  247.8 17.8 %collective-permute-start.21 = (f32[16,1,32,256]{3,2,1,0:T(8,128)S(1)}, f32[16,1,32,256]{3,2,1,0:T(8,128)S(1)}, u32[]{:S(2)}, u32[]{:S(2)}) collective-permute-start(f32[16,1,32,256]{3,2,1,0:T(8,128)S(1)} %get-tuple-element.16), channel_id=1, source_target_pairs={{0,4},{4,8},{8,12},{12,16},{16,20},{20,24},{24,28},{28,32},{32,36}... | collective-permute-start | bytes 1572872 | tf_op jit(solution)/shard_map/ppermute | solution.py:26
  256.0 7.9 %collective-permute-start.22 = (f32[16,16,1,256]{3,1,2,0:T(8,128)S(1)}, f32[16,16,1,256]{3,1,2,0:T(8,128)S(1)}, u32[]{:S(2)}, u32[]{:S(2)}) collective-permute-start(f32[16,16,1,256]{3,1,2,0:T(8,128)S(1)} %copy.135), channel_id=1, source_target_pairs={{1,0},{2,1},{3,2},{5,4},{6,5},{7,6},{9,8},{10,9},{11,10},{13,12},{... | collective-permute-start | bytes 786440 | tf_op jit(solution)/shard_map/ppermute | solution.py:27
  257.3 8.0 %collective-permute-start.23 = (f32[16,16,1,256]{3,1,2,0:T(8,128)S(1)}, f32[16,16,1,256]{3,1,2,0:T(8,128)S(1)}, u32[]{:S(2)}, u32[]{:S(2)}) collective-permute-start(f32[16,16,1,256]{3,1,2,0:T(8,128)S(1)} %copy.137), channel_id=1, source_target_pairs={{0,1},{1,2},{2,3},{4,5},{5,6},{6,7},{8,9},{9,10},{10,11},{12,13},{... | collective-permute-start | bytes 786440 | tf_op jit(solution)/shard_map/ppermute | solution.py:26
  265.6 44.4 %copy-start.4 = (s32[1,1,128,1]{2,3,1,0:T(1,128)S(1)}, s32[1,1,128,1]{2,3,1,0:T(1,128)}, u32[]{:S(2)}) copy-start(s32[1,1,128,1]{2,3,1,0:T(1,128)} %param.11) | copy-start | bytes 1540
  293.6 20.0 %collective-permute-start.24 = (f32[16,1,32,256]{3,2,1,0:T(8,128)S(1)}, f32[16,1,32,256]{3,2,1,0:T(8,128)S(1)}, u32[]{:S(2)}, u32[]{:S(2)}) collective-permute-start(f32[16,1,32,256]{3,2,1,0:T(8,128)S(1)} %get-tuple-element.13), channel_id=1, source_target_pairs={{4,0},{8,4},{12,8},{16,12},{20,16},{24,20},{28,24},{32,28},{36,32}... | collective-permute-start | bytes 1572872 | tf_op jit(solution)/shard_map/ppermute | solution.py:27
  295.5 18.1 %collective-permute-start.25 = (f32[16,1,32,256]{3,2,1,0:T(8,128)S(1)}, f32[16,1,32,256]{3,2,1,0:T(8,128)S(1)}, u32[]{:S(2)}, u32[]{:S(2)}) collective-permute-start(f32[16,1,32,256]{3,2,1,0:T(8,128)S(1)} %get-tuple-element.12), channel_id=1, source_target_pairs={{0,4},{4,8},{8,12},{12,16},{16,20},{20,24},{24,28},{28,32},{32,36}... | collective-permute-start | bytes 1572872 | tf_op jit(solution)/shard_map/ppermute | solution.py:26
  303.9 7.9 %collective-permute-start.26 = (f32[16,16,1,256]{3,1,2,0:T(8,128)S(1)}, f32[16,16,1,256]{3,1,2,0:T(8,128)S(1)}, u32[]{:S(2)}, u32[]{:S(2)}) collective-permute-start(f32[16,16,1,256]{3,1,2,0:T(8,128)S(1)} %copy.139), channel_id=1, source_target_pairs={{1,0},{2,1},{3,2},{5,4},{6,5},{7,6},{9,8},{10,9},{11,10},{13,12},{... | collective-permute-start | bytes 786440 | tf_op jit(solution)/shard_map/ppermute | solution.py:27
  305.3 8.0 %collective-permute-start.27 = (f32[16,16,1,256]{3,1,2,0:T(8,128)S(1)}, f32[16,16,1,256]{3,1,2,0:T(8,128)S(1)}, u32[]{:S(2)}, u32[]{:S(2)}) collective-permute-start(f32[16,16,1,256]{3,1,2,0:T(8,128)S(1)} %copy.141), channel_id=1, source_target_pairs={{0,1},{1,2},{2,3},{4,5},{5,6},{6,7},{8,9},{9,10},{10,11},{12,13},{... | collective-permute-start | bytes 786440 | tf_op jit(solution)/shard_map/ppermute | solution.py:26
  342.4 20.0 %collective-permute-start.28 = (f32[16,1,32,256]{3,2,1,0:T(8,128)S(1)}, f32[16,1,32,256]{3,2,1,0:T(8,128)S(1)}, u32[]{:S(2)}, u32[]{:S(2)}) collective-permute-start(f32[16,1,32,256]{3,2,1,0:T(8,128)S(1)} %get-tuple-element.9), channel_id=1, source_target_pairs={{4,0},{8,4},{12,8},{16,12},{20,16},{24,20},{28,24},{32,28},{36,32}... | collective-permute-start | bytes 1572872 | tf_op jit(solution)/shard_map/ppermute | solution.py:27
  344.3 18.1 %collective-permute-start.29 = (f32[16,1,32,256]{3,2,1,0:T(8,128)S(1)}, f32[16,1,32,256]{3,2,1,0:T(8,128)S(1)}, u32[]{:S(2)}, u32[]{:S(2)}) collective-permute-start(f32[16,1,32,256]{3,2,1,0:T(8,128)S(1)} %get-tuple-element.8), channel_id=1, source_target_pairs={{0,4},{4,8},{8,12},{12,16},{16,20},{20,24},{24,28},{28,32},{32,36}... | collective-permute-start | bytes 1572872 | tf_op jit(solution)/shard_map/ppermute | solution.py:26
  352.8 7.9 %collective-permute-start.30 = (f32[16,16,1,256]{3,1,2,0:T(8,128)S(1)}, f32[16,16,1,256]{3,1,2,0:T(8,128)S(1)}, u32[]{:S(2)}, u32[]{:S(2)}) collective-permute-start(f32[16,16,1,256]{3,1,2,0:T(8,128)S(1)} %copy.143), channel_id=1, source_target_pairs={{1,0},{2,1},{3,2},{5,4},{6,5},{7,6},{9,8},{10,9},{11,10},{13,12},{... | collective-permute-start | bytes 786440 | tf_op jit(solution)/shard_map/ppermute | solution.py:27
  354.1 8.0 %collective-permute-start.31 = (f32[16,16,1,256]{3,1,2,0:T(8,128)S(1)}, f32[16,16,1,256]{3,1,2,0:T(8,128)S(1)}, u32[]{:S(2)}, u32[]{:S(2)}) collective-permute-start(f32[16,16,1,256]{3,1,2,0:T(8,128)S(1)} %copy.145), channel_id=1, source_target_pairs={{0,1},{1,2},{2,3},{4,5},{5,6},{6,7},{8,9},{9,10},{10,11},{12,13},{... | collective-permute-start | bytes 786440 | tf_op jit(solution)/shard_map/ppermute | solution.py:26
  389.3 36.8 %copy-start.2 = (f32[1,1,128,16]{2,3,1,0:T(8,128)S(1)}, f32[1,1,128,16]{2,3,1,0:T(8,128)}, u32[]{:S(2)}) copy-start(f32[1,1,128,16]{2,3,1,0:T(8,128)} %param.13) | copy-start | bytes 24580
  450.8 28.2 %copy-start.1 = (f32[16,16]{1,0:T(8,128)}, f32[16,16]{1,0:T(8,128)S(1)}, u32[]{:S(2)}) copy-start(f32[16,16]{1,0:T(8,128)S(1)} %convolution_bitcast_fusion) | copy-start | bytes 3076
where the time goes:
time: 482 us; the launch traced here: 479 us
  other arithmetic  213 us (44%)
  starting transfers between devices  103 us (21%)
  local copies, waits for them, and re-layouts  85.3 us (18%)
  blocking collectives  51.9 us (11%)
  waiting for transfers between devices  23.5 us (5%)
    select_n x8, other arithmetic, relax(): return jnp.where(diffusion > 0.0, updated, 0.0)  208 us
    ppermute x16, starting transfers between devices, with_halo(): lax.ppermute(last, axis, up)  77.2 us
    select_n x1, local copies, waits for them, and re-layouts, relax(): return jnp.where(diffusion > 0.0, updated, 0.0)  35 us
    psum x4, blocking collectives, by_axis(): return functools.reduce(lax.psum, axes, x)  28 us
    ppermute x16, starting transfers between devices, with_halo(): lax.ppermute(leading, axis, [(b, a) for a, b in up])  25.7 us
    all_to_all x1, blocking collectives, body(): lax.all_to_all(outgoing, GX_GY, split_axis=0, concat_axis=0, tiled=True)  23.9 us
    slice x16, local copies, waits for them, and re-layouts, with_halo(): leading = lax.slice_in_dim(x, 0, width, axis=dim)  22.6 us
    ppermute x16, waiting for transfers between devices, with_halo(): lax.ppermute(leading, axis, [(b, a) for a, b in up])  13.7 us
  transfers between devices with their start and end apart: 32, of which 14 were waited for; matrix products, arithmetic and copies ran while one was open for 9% of the time, Pallas kernels for 0%

commit v1 on v0

v1 whole, which is shorter than its diff:
```python
import functools

import jax
import jax.numpy as jnp
from jax import lax
from jax.experimental import pallas as pl
from jax.experimental.pallas import tpu as pltpu
from jax.sharding import Mesh
from jax.sharding import PartitionSpec as P

SWEEPS = 4
H = SWEEPS
ALL = ("gx_0", "gx_1", "gx_2", "gy")
GX = ("gx_0", "gx_1", "gx_2")
G = 8
TAU = 2.0
F32 = jnp.float32
ANY = pl.BlockSpec(memory_space=pl.ANY)
SMEM = pl.BlockSpec(memory_space=pltpu.SMEM)
VMEM = pl.BlockSpec(memory_space=pltpu.VMEM)
DMA = pltpu.SemaphoreType.DMA
NX, NY, NZ = 16, 32, 256
TILES = NY // 8


def both(pairs):
    return pairs + [(b, a) for a, b in pairs]


def near(x):
    return pltpu.with_memory_space_constraint(x, pltpu.VMEM)


def kernel(body, name, operands, outs, scratch, in_specs, microseconds, mib, aliases=None):
    placed = [near(x) if spec is VMEM else x for x, spec in zip(operands, in_specs)]
    out_shape = [pltpu.VMEM(dims, F32) if spec is VMEM else jax.ShapeDtypeStruct(dims, F32) for dims, spec in outs]
    return pl.pallas_call(
        body,
        in_specs=in_specs,
        out_specs=[spec for _, spec in outs],
        out_shape=out_shape,
        scratch_shapes=scratch,
        input_output_aliases=aliases or {},
        compiler_params=pltpu.CompilerParams(vmem_limit_bytes=mib * 1024 * 1024),
        cost_estimate=pl.CostEstimate(flops=0, transcendentals=0, bytes_accessed=int(microseconds * 3.5e6)),
        name=name,
    )(*placed)


def sorting(inverse):
    row = lax.broadcasted_iota(jnp.int32, (NZ, NZ), 0)
    col = lax.broadcasted_iota(jnp.int32, (NZ, NZ), 1)
    if inverse:
        row, col = col, row
    source = jnp.where(col < NZ // 2, 2 * col, 2 * col - (NZ - 1))
    return (row == source).astype(F32).astype(jnp.bfloat16)


def reorder(v, matrix):
    high = v.astype(jnp.bfloat16)
    rest = v - high.astype(F32)
    mid = rest.astype(jnp.bfloat16)
    low = (rest - mid.astype(F32)).astype(jnp.bfloat16)
    dot = functools.partial(jnp.dot, preferred_element_type=F32)
    return dot(high, matrix) + (dot(mid, matrix) + dot(low, matrix))


def copy_all(pairs, sems):
    made = [pltpu.make_async_copy(a, b, sems.at[i]) for i, (a, b) in enumerate(pairs)]
    for c in made:
        c.start()
    for c in made:
        c.wait()


def face_pairs(field, place, x0, y0, b_out, c_out, d_out):
    return [
        (field.at[pl.ds(x0 + place[0], H), pl.ds(y0, NY)], b_out.at[:, pl.ds(0, NY)]),
        (field.at[pl.ds(x0, NX), pl.ds(y0 + place[2], H)], c_out.at[:, pl.ds(0, H)]),
        (field.at[pl.ds(x0, NX), pl.ds(y0 + place[3], H)], d_out.at[:, pl.ds(0, H)]),
    ]


def face_outs(extra):
    more = 1 if extra else 0
    faces = [(H, NY + TILES * more, G, NZ), (NX, H + more, G, NZ), (NX, H + more, G, NZ)]
    return [(dims, VMEM) for dims in faces]


PLANES = 4


def pack_kernel(g, place, probes, *rest):
    a_in = rest[0] if g == 0 else None
    s_out, b_out, c_out, d_out, raw, mat, sem_in, sem_f = rest[-8:]

    def load(i):
        src = probes.at[pl.ds(g * G, G), pl.ds(i * PLANES, PLANES)]
        return pltpu.make_async_copy(src, raw.at[:, pl.ds(i * PLANES, PLANES)], sem_in.at[i])

    for i in range(NX // PLANES):
        load(i).start()
    mat[...] = sorting(False)

    def planes(i, carry):
        load(i).wait()
        rows = [jnp.swapaxes(raw[:, i * PLANES + k], 0, 1).reshape(NY * G, NZ) for k in range(PLANES)]
        rows = reorder(jnp.concatenate(rows, axis=0), mat[...])
        s_out[pl.ds(i * PLANES, PLANES)] = rows.reshape(PLANES, NY, G, NZ)
        return carry

    lax.fori_loop(0, NX // PLANES, planes, 0)
    pairs = face_pairs(s_out, place, 0, 0, b_out, c_out, d_out)
    if g == 0:
        pairs += [
            (a_in.at[pl.ds(place[0], H)], b_out.at[:, pl.ds(NY, TILES)]),
            (a_in.at[:, pl.ds(place[10], 1)], c_out.at[:, pl.ds(H, 1)]),
            (a_in.at[:, pl.ds(place[11], 1)], d_out.at[:, pl.ds(H, 1)]),
        ]
    copy_all(pairs, sem_f)


def pack(g, place, probes, a):
    more = [a] if g == 0 else []
    return kernel(
        functools.partial(pack_kernel, g),
        f"pack{g}",
        [place, probes] + more,
        [((NX, NY, G, NZ), VMEM)] + face_outs(g == 0),
        [
            pltpu.VMEM((G, NX, NY, NZ), F32),
            pltpu.VMEM((NZ, NZ), jnp.bfloat16),
            DMA((NX // PLANES,)),
            DMA((6,)),
        ],
        [SMEM, ANY] + [VMEM] * len(more),
        6,
        12,
    )


def corner_kernel(place, field, c_in, d_in, *rest):
    a_out, e_out, sems = rest[-3:]
    inner, outer = pl.ds(place[1], H), pl.ds(place[0], H)
    rows = pl.ds(0, H)
    pairs = [
        (field.at[inner], a_out.at[:, pl.ds(H, NY)]),
        (c_in.at[inner, rows], a_out.at[:, pl.ds(place[4], H)]),
        (d_in.at[inner, rows], a_out.at[:, pl.ds(place[5], H)]),
        (c_in.at[outer, rows], e_out.at[:, pl.ds(place[6], H)]),
        (d_in.at[outer, rows], e_out.at[:, pl.ds(place[7], H)]),
    ]
    if len(rest) > 3:
        tile, base = pl.ds(H, 1), NY + 2 * H
        pairs += [
            (rest[0].at[inner], a_out.at[:, pl.ds(base + 1, TILES)]),
            (c_in.at[inner, tile], a_out.at[:, pl.ds(base + place[12], 1)]),
            (d_in.at[inner, tile], a_out.at[:, pl.ds(base + place[13], 1)]),
            (c_in.at[outer, tile], e_out.at[:, pl.ds(2 * H + place[14], 1)]),
            (d_in.at[outer, tile], e_out.at[:, pl.ds(2 * H + place[15], 1)]),
        ]
    copy_all(pairs, sems)


def corners(place, field, c_in, d_in, a=None):
    more = [] if a is None else [a]
    n = len(more)
    return kernel(
        corner_kernel,
        "corners",
        [place, field, c_in, d_in] + more,
        [((H, NY + 2 * H + (TILES + 2) * n, G, NZ), VMEM), ((H, 2 * H + 2 * n, G, NZ), VMEM)],
        [DMA((10,))],
        [SMEM] + [VMEM] * (3 + n),
        1,
        2,
    )


def coefficient_kernel(place, wind, a_own, a_in, b_in, c_in, d_in, e_in, out, wide, mat, sems):
    base = NY + 2 * H
    outer, own, tile = pl.ds(place[8], H), pl.ds(1, TILES), pl.ds(H, 1)
    copy_all(
        [
            (a_own, wide.at[pl.ds(H, NX), own]),
            (a_in.at[:, pl.ds(base, TILES + 2)], wide.at[pl.ds(place[9], H)]),
            (b_in.at[:, pl.ds(NY, TILES)], wide.at[outer, own]),
            (c_in.at[:, tile], wide.at[pl.ds(H, NX), pl.ds(place[12], 1)]),
            (d_in.at[:, tile], wide.at[pl.ds(H, NX), pl.ds(place[13], 1)]),
            (e_in.at[:, pl.ds(2 * H, 1)], wide.at[outer, pl.ds(0, 1)]),
            (e_in.at[:, pl.ds(2 * H + 1, 1)], wide.at[outer, pl.ds(TILES + 1, 1)]),
        ],
        sems,
    )
    mat[...] = sorting(False)
    w = [wind[i] for i in range(3)]
    count = 8 * (TILES + 2)

    def planes(i, carry):
        x = pl.ds(i * H, H)
        a = reorder(wide[x].reshape(H * count, NZ), mat[...])
        inverse = 1.0 / (1.0 + TAU * (6.0 * a + (w[0] + w[1] + w[2])))
        inverse = jnp.where(a > 0.0, inverse, 0.0)
        spread = TAU * a * inverse
        lane = lax.broadcasted_iota(jnp.int32, a.shape, 1)
        parts = [
            spread,
            spread + (TAU * w[0]) * inverse,
            spread + (TAU * w[1]) * inverse,
            jnp.where(lane == 0, 0.0, spread + (TAU * w[2]) * inverse),
            inverse,
        ]
        for k, part in enumerate(parts):
            out[k, x] = part.reshape(H, count, NZ)
        return carry

    lax.fori_loop(0, (NX + 2 * H) // H, planes, 0)


def coefficients(place, wind, a_own, state):
    wide = (NX + 2 * H, TILES + 2, 8, NZ)
    return kernel(
        coefficient_kernel,
        "coefficients",
        [place, wind, a_own] + state[1:6],
        [((5, NX + 2 * H, 8 * (TILES + 2), NZ), VMEM)],
        [pltpu.VMEM(wide, F32), pltpu.VMEM((NZ, NZ), jnp.bfloat16), DMA((7,))],
        [SMEM, SMEM] + [VMEM] * 6,
        3,
        6,
    )[0]


SHIFT = 8 - H


def sweep(number, src, dst, scaled, coef):
    nx, ny = src.shape[:2]
    last = lax.broadcasted_iota(jnp.int32, (G, 128), 1) == 127
    block = 2

    def row(ref, x, y, z):
        return ref[x, y, :, z * 128 : (z + 1) * 128]

    def rows(ref, x, y):
        return [row(ref, x, y, z) for z in (0, 1)]

    def spread(k, x, y, z):
        y = y + SHIFT
        return jnp.broadcast_to(coef[k, x, y : y + 1, z * 128 : (z + 1) * 128], (G, 128))

    def planes(i, carry):
        xs = [number + block * i + k for k in range(block)]
        below = [rows(src, x, number - 1) for x in xs]
        here = [rows(src, x, number) for x in xs]
        for y in range(number, ny - number):
            above = [rows(src, x, y + 1) for x in xs]
            beside = [rows(src, xs[0] - 1, y)] + here + [rows(src, xs[-1] + 1, y)]
            for k, x in enumerate(xs):
                even, odd = here[k]
                up = [odd, jnp.where(last, 0.0, pltpu.roll(even, 127, 1))]
                down = [pltpu.roll(odd, 1, 1), even]
                for z in (0, 1):
                    if number == 1:
                        part = here[k][z] * spread(4, x, y, z)
                        scaled[x, y, :, z * 128 : (z + 1) * 128] = part
                    else:
                        part = row(scaled, x, y, z)
                    part = part + spread(0, x, y, z) * (beside[k + 2][z] + (above[k][z] + up[z]))
                    other = spread(1, x, y, z) * beside[k][z] + spread(2, x, y, z) * below[k][z]
                    dst[x, y, :, z * 128 : (z + 1) * 128] = (part + spread(3, x, y, z) * down[z]) + other
            below, here = here, above
        return carry

    lax.fori_loop(0, (nx - 2 * number) // block, planes, 0)


def gather_state(place, field, a_in, b_in, c_in, d_in, e_in, u, sems):
    outer, own_x, own_y, rows = pl.ds(place[8], H), pl.ds(H, NX), pl.ds(H, NY), pl.ds(0, H)
    copy_all(
        [
            (field, u.at[own_x, own_y]),
            (a_in.at[:, pl.ds(0, NY + 2 * H)], u.at[pl.ds(place[9], H)]),
            (b_in.at[:, pl.ds(0, NY)], u.at[outer, own_y]),
            (c_in.at[:, rows], u.at[own_x, pl.ds(place[4], H)]),
            (d_in.at[:, rows], u.at[own_x, pl.ds(place[5], H)]),
            (e_in.at[:, rows], u.at[outer, rows]),
            (e_in.at[:, pl.ds(H, H)], u.at[outer, pl.ds(H + NY, H)]),
        ],
        sems,
    )


def sweeps(u, v, scaled, coef):
    for number in range(1, SWEEPS + 1):
        sweep(number, u, v, scaled, coef)
        u, v = v, u


def step_kernel(place, field, a_in, b_in, c_in, d_in, e_in, coef, s_out, b_out, c_out, d_out, u, v, scaled, sems):
    gather_state(place, field, a_in, b_in, c_in, d_in, e_in, u, sems)
    sweeps(u, v, scaled, coef)
    own = u.at[pl.ds(H, NX), pl.ds(H, NY)]
    copy_all(face_pairs(u, place, H, H, b_out, c_out, d_out) + [(own, s_out)], sems)


STATE_SCRATCH = [pltpu.VMEM((NX + 2 * H, NY + 2 * H, G, NZ), F32)] * 3


def step(g, place, state):
    return kernel(
        step_kernel,
        f"step{g}",
        [place, *state],
        [((NX, NY, G, NZ), VMEM)] + face_outs(False),
        STATE_SCRATCH + [DMA((8,))],
        [SMEM] + [VMEM] * 7,
        12,
        24,
    )


def read_sensors(cells, u, out):
    lane = lax.broadcasted_iota(jnp.int32, (G, 128), 1)

    def one(s, found):
        cell = cells[s]
        x, y, z = cell // (NY * NZ), (cell // NZ) % NY, cell % NZ
        half = pl.multiple_of((z % 2) * 128, 128)
        value = pltpu.roll(u[x + H, y + H, :, pl.ds(half, 128)], (s - z // 2 + 128) % 128, 1)
        return jnp.where(lane == s, value, found)

    out[...] = lax.fori_loop(0, 128, one, jnp.zeros((G, 128), F32), unroll=8)


def last_kernel(g, place, cells, field, a_in, b_in, c_in, d_in, e_in, coef, *rest):
    out, reading, u, v, scaled, stage, mat, sems, sem_out = rest[-9:]
    gather_state(place, field, a_in, b_in, c_in, d_in, e_in, u, sems)
    mat[...] = sorting(True)
    sweeps(u, v, scaled, coef)

    def store(i):
        dst = out.at[pl.ds(g * G, G), pl.ds(i * PLANES, PLANES)]
        return pltpu.make_async_copy(stage.at[:, pl.ds(i * PLANES, PLANES)], dst, sem_out.at[i])

    def planes(i, carry):
        rows = u[pl.ds(i * PLANES + H, PLANES), pl.ds(H, NY)].reshape(PLANES * NY * G, NZ)
        rows = reorder(rows, mat[...]).reshape(PLANES, NY, G, NZ)
        for k in range(PLANES):
            stage[:, i * PLANES + k] = jnp.swapaxes(rows[k], 0, 1)
        store(i).start()
        return carry

    lax.fori_loop(0, NX // PLANES, planes, 0)
    read_sensors(cells, u, reading)
    for i in range(NX // PLANES):
        store(i).wait()


def last_step(g, place, cells, state, fields=None):
    more = [] if fields is None else [fields]
    return kernel(
        functools.partial(last_kernel, g),
        f"last{g}",
        [place, cells, *state] + more,
        [((2 * G, NX, NY, NZ), ANY), ((G, 128), VMEM)],
        STATE_SCRATCH
        + [
            pltpu.VMEM((G, NX, NY, NZ), F32),
            pltpu.VMEM((NZ, NZ), jnp.bfloat16),
            DMA((8,)),
            DMA((NX // PLANES,)),
        ],
        [SMEM, SMEM] + [VMEM] * 7 + [ANY] * len(more),
        16,
        30,
        {9: 0} if more else {},
    )


def readings_exchange(readings, sensor_owner, sensor_count, goal_weight):
    probe_count, sensor_rows = readings.shape
    goal_count = goal_weight.shape[3]
    device_count = lax.axis_size(ALL)
    capacity = max(2, (sensor_rows + device_count - 1) // device_count)
    row_index = jnp.arange(sensor_rows, dtype=jnp.int32)
    active = (row_index < sensor_count.reshape(())).astype(F32)
    readings = readings.T * active[:, None]
    weights = goal_weight.reshape(sensor_rows, goal_count)
    owners = sensor_owner.reshape(sensor_rows)
    earlier = (owners[None, :] == owners[:, None]) & (row_index[None, :] < row_index[:, None])
    slot_rank = jnp.sum(earlier.astype(jnp.int32), axis=1)
    slot_index = owners * capacity + slot_rank
    slots = jnp.arange(device_count * capacity, dtype=jnp.int32)
    placing = (slots[:, None] == slot_index[None, :]).astype(F32)
    payload = jnp.concatenate([readings, weights], axis=1)
    outgoing = jnp.dot(placing, payload, precision=lax.Precision.HIGHEST)
    outgoing = outgoing.reshape(device_count, capacity, probe_count + goal_count)
    received = lax.all_to_all(outgoing, ALL, split_axis=0, concat_axis=0, tiled=True)
    received = received.reshape(device_count * capacity, probe_count + goal_count)
    goal_block = jnp.dot(
        received[:, probe_count:].T, received[:, :probe_count], precision=lax.Precision.HIGHEST
    )
    own = jnp.dot(goal_block.T, goal_block, precision=lax.Precision.HIGHEST)
    terms = jnp.broadcast_to(own.reshape(1, -1), (device_count, own.size))
    terms = lax.all_to_all(terms, ALL, split_axis=0, concat_axis=0, tiled=True)
    return goal_block, jnp.sum(terms, axis=0).reshape(own.shape)


def body(probes, diffusivity, wind_speed, sensor_cell, sensor_owner, sensor_count, goal_weight):
    core = lax.axis_index("gx_2")
    odd = lax.axis_index("gy") % 2

    def either(flag, zero, one):
        return jnp.where(flag == 0, zero, one)

    place = jnp.stack(
        [
            either(core, 0, NX - H),
            either(core, NX - H, 0),
            either(odd, NY - H, 0),
            either(odd, 0, NY - H),
            either(odd, NY + H, 0),
            either(odd, 0, NY + H),
            either(odd, H, 0),
            either(odd, 0, H),
            either(core, 0, NX + H),
            either(core, NX + H, 0),
            either(odd, TILES - 1, 0),
            either(odd, 0, TILES - 1),
            either(odd, TILES + 1, 0),
            either(odd, 0, TILES + 1),
            either(odd, 1, 0),
            either(odd, 0, 1),
        ]
    ).astype(jnp.int32)
    peers_x, peers_y = lax.axis_size(GX), lax.axis_size("gy")
    inner = both([(i, i + 1) for i in range(0, peers_x - 1, 2)])
    outer = both([(i, i + 1) for i in range(1, peers_x - 1, 2)])
    first = both([(i, i + 1) for i in range(0, peers_y - 1, 2)])
    second = both([(i, i + 1) for i in range(1, peers_y - 1, 2)])

    def rows(c, d):
        return lax.ppermute(c, "gy", first), lax.ppermute(d, "gy", second)

    def planes(b):
        return lax.ppermute(b, GX, outer)

    def after(values, others):
        return lax.optimization_barrier((tuple(values), tuple(others)))[0]

    def finish(field, c, d, own=None):
        a, e = corners(place, field, c, d, own)
        return lax.ppermute(a, GX, inner), lax.ppermute(e, GX, outer), (a, e)

    probes = pltpu.with_memory_space_constraint(probes, pltpu.HBM)
    a_own = diffusivity.reshape(NX, TILES, 8, NZ)
    cells = sensor_cell.reshape(-1)
    made = [pack(0, place, probes, a_own), pack(1, place, probes, a_own)]
    c, d = rows(*made[0][2:])
    b = planes(made[0][1])
    c, d, b, *made[1] = after((c, d, b, *made[1]), ())
    coef = fields = None
    readings = []
    for turn in range(4):
        g, field = turn % 2, made[turn][0]
        a, e, sent = finish(field, c, d, a_own if turn == 0 else None)
        state = [field, a, b, c, d, e]
        if turn < 3:
            c, d = rows(*after(made[turn + 1][2:], sent))
            b = planes(*after(made[turn + 1][1:2], (e,)))
        if turn == 0:
            coef = coefficients(place, wind_speed, a_own, state)
        if turn < 2:
            c, d, b, *out = after((c, d, b, *step(g, place, state + [coef])), ())
            made.append(out)
        else:
            fields, reading = last_step(g, place, cells, state + [coef], fields)
            readings.append(reading)
            if turn == 2:
                c, d, b, fields = after((c, d, b, fields), ())
    readings = jnp.concatenate(readings, axis=0)
    goal_block, ritz_gram = readings_exchange(readings, sensor_owner, sensor_count, goal_weight)
    return fields, goal_block, ritz_gram


def solution(mesh):
    torus = Mesh(mesh.devices.reshape(4, 4, 2, mesh.shape["gy"]), ALL)
    return jax.shard_map(
        body,
        mesh=torus,
        in_specs=(
            P(None, GX, "gy", None),
            P(GX, "gy", None),
            P(),
            P(GX, "gy", None),
            P(GX, "gy", None, None),
            P(GX, "gy"),
            P(GX, "gy", None, None),
        ),
        out_specs=(P(None, GX, "gy", None), P(ALL, None), P()),
        check_vma=False,
    )
```

time: 482 us -> 205 us (0.43)
  other arithmetic: 213 us -> 0.34 us
  Pallas kernels: 0 us -> 86.8 us
  local copies, waits for them, and re-layouts: 85.3 us -> 2.01 us
  starting transfers between devices: 103 us -> 43.1 us
  blocking collectives: 51.9 us -> 43.6 us
    select_n x9 -> x0, other arithmetic: 208 us -> none  [the longest x8 208 us: relax(): return jnp.where(diffusion > 0.0, updated, 0.0)]
    pallas_call x0 -> x11, Pallas kernels: none -> 86.8 us  [kernel(): pl.pallas_call(body, in_specs=in_specs, out_specs=[spec for _, spec in ou...]
    ppermute x32 -> x20, starting transfers between devices: 103 us -> 43.1 us  [the longest x8 15 us: finish(): return (lax.ppermute(a, GX, inner), lax.ppermute(e, GX, outer), (a, e))]
    select_n x1 -> x0, local copies, waits for them, and re-layouts: 35 us -> none  [relax(): return jnp.where(diffusion > 0.0, updated, 0.0)]
    slice x32 -> x0, local copies, waits for them, and re-layouts: 33.5 us -> none  [the longest x16 22.6 us: with_halo(): leading = lax.slice_in_dim(x, 0, width, axis=dim)]
    psum x4 -> x0, blocking collectives: 28 us -> none  [by_axis(): return functools.reduce(lax.psum, axes, x)]
    all_to_all x1 -> x2, blocking collectives: 23.9 us -> 43.6 us  [the longest x1 29.5 us: readings_exchange(): lax.all_to_all(outgoing, ALL, split_axis=0, concat_axis=0, tiled=True)]
    unnamed x24 -> x12, local copies, waits for them, and re-layouts: 10.4 us -> 1.06 us
  transfers between devices with their start and end apart: 32 -> 20, of which waited for: 14 -> 5; matrix products, arithmetic and copies ran while one was open for 9% -> 0% of each run, Pallas kernels for 0% -> 29%
where the time goes in v1:
time: 205 us; the launch traced here: 204 us
  Pallas kernels  86.8 us (42%)
  blocking collectives  43.6 us (21%)
  starting transfers between devices  43.1 us (21%)
  waiting for transfers between devices  26 us (13%)
    pallas_call x11, Pallas kernels, kernel(): pl.pallas_call(body, in_specs=in_specs, out_specs=[spec for _, spec in ou...  86.8 us
    all_to_all x1, blocking collectives, readings_exchange(): lax.all_to_all(outgoing, ALL, split_axis=0, concat_axis=0, tiled=True)  29.5 us
    ppermute x8, waiting for transfers between devices, finish(): return (lax.ppermute(a, GX, inner), lax.ppermute(e, GX, outer), (a, e))  18.4 us
    ppermute x8, starting transfers between devices, finish(): return (lax.ppermute(a, GX, inner), lax.ppermute(e, GX, outer), (a, e))  15 us
    ppermute x8, starting transfers between devices, rows(): return (lax.ppermute(c, 'gy', first), lax.ppermute(d, 'gy', second))  14.4 us
    all_to_all x1, blocking collectives, readings_exchange(): terms = lax.all_to_all(terms, ALL, split_axis=0, concat_axis=0, tiled=True)  14.1 us
    ppermute x4, starting transfers between devices, planes(): return lax.ppermute(b, GX, outer)  13.7 us
    ppermute x8, waiting for transfers between devices, rows(): return (lax.ppermute(c, 'gy', first), lax.ppermute(d, 'gy', second))  7.58 us
  transfers between devices with their start and end apart: 20, of which 5 were waited for; matrix products, arithmetic and copies ran while one was open for 0% of the time, Pallas kernels for 29%

profile of v1, /device:TPU:1, one launch (start us, length us, event | category | flops | bytes accessed | tf_op | source)
XLA Modules:
  0.0 204.3 jit_solution(12917412321334380205)
XLA Ops:
  0.7 0.1 stack.67.place
  0.8 0.0 copy-start
  0.8 1.0 copy-done
  1.8 4.8 %pack0.1 = (f32[16,32,8,256]{3,2,1,0:T(8,128)S(1)}, f32[4,36,8,256]{3,2,1,0:T(8,128)S(1)}, f32[16,5,8,256]{3,2,1,0:T(8,128)S(1)}, f32[16,5,8,256]{3,2,1,0:T(8,128)S(1)}) custom-call(s32[16]{0:T(128)S(1)} %stack.67.place, f32[16,16,32,256]{3,2,1,0:T(8,128)} %probes.3, f32[16,4,8,256]{3,2,1,0:T(8,128)S(1)} %bitcast.29), custom_call_target="tpu_custom_call" | custom-call | bytes 21000000 | tf_op jit(solution)/shard_map/pack0/pallas_call | solution.py:37
  6.6 4.5 %collective-permute-start.2 = (f32[4,36,8,256]{3,2,1,0:T(8,128)S(1)}, f32[4,36,8,256]{3,2,1,0:T(8,128)S(1)}, u32[]{:S(2)}, u32[]{:S(2)}) collective-permute-start(f32[4,36,8,256]{3,2,1,0:T(8,128)S(1)} %get-tuple-element.67), channel_id=1, source_target_pairs={{4,8},{12,16},{20,24},{28,32},{36,40},{44,48},{52,56},{60,64},{68,... | collective-permute-start | bytes 3538952 | tf_op jit(solution)/shard_map/ppermute | solution.py:447
  11.1 1.7 collective-permute-start
  12.8 0.7 collective-permute-start.1
  13.5 4.7 %pack1.1 = (f32[16,32,8,256]{3,2,1,0:T(8,128)S(1)}, f32[4,32,8,256]{3,2,1,0:T(8,128)S(1)}, f32[16,4,8,256]{3,2,1,0:T(8,128)S(1)}, f32[16,4,8,256]{3,2,1,0:T(8,128)S(1)}) custom-call(s32[16]{0:T(128)S(1)} %stack.67.place, f32[16,16,32,256]{3,2,1,0:T(8,128)} %probes.3), custom_call_target="tpu_custom_call" | custom-call | bytes 21000000 | tf_op jit(solution)/shard_map/pack1/pallas_call | solution.py:37
  18.2 7.6 %collective-permute-done.c_in = f32[16,5,8,256]{3,2,1,0:T(8,128)S(1)} collective-permute-done((f32[16,5,8,256]{3,2,1,0:T(8,128)S(1)}, f32[16,5,8,256]{3,2,1,0:T(8,128)S(1)}, u32[]{:S(2)}, u32[]{:S(2)}) %collective-permute-start) | collective-permute-done | bytes 655392 | tf_op jit(solution)/shard_map/ppermute | solution.py:444
  25.7 0.0 collective-permute-done.1.d_in
  25.7 0.0 collective-permute-done.2.b_in
  25.8 1.0 corners.4
  26.7 0.1 collective-permute-start.7
  26.8 4.8 %collective-permute-start.5 = (f32[4,10,8,256]{3,2,1,0:T(8,128)S(1)}, f32[4,10,8,256]{3,2,1,0:T(8,128)S(1)}, u32[]{:S(2)}, u32[]{:S(2)}) collective-permute-start(f32[4,10,8,256]{3,2,1,0:T(8,128)S(1)} %get-tuple-element.78), channel_id=1, source_target_pairs={{4,8},{12,16},{20,24},{28,32},{36,40},{44,48},{52,56},{60,64},{68,... | collective-permute-start | bytes 983048 | tf_op jit(solution)/shard_map/ppermute | solution.py:454
  31.6 5.0 %collective-permute-done.5.e_in = f32[4,10,8,256]{3,2,1,0:T(8,128)S(1)} collective-permute-done((f32[4,10,8,256]{3,2,1,0:T(8,128)S(1)}, f32[4,10,8,256]{3,2,1,0:T(8,128)S(1)}, u32[]{:S(2)}, u32[]{:S(2)}) %collective-permute-start.5) | collective-permute-done | bytes 327712 | tf_op jit(solution)/shard_map/ppermute | solution.py:454
  36.6 3.3 %collective-permute-start.6 = (f32[4,32,8,256]{3,2,1,0:T(8,128)S(1)}, f32[4,32,8,256]{3,2,1,0:T(8,128)S(1)}, u32[]{:S(2)}, u32[]{:S(2)}) collective-permute-start(f32[4,32,8,256]{3,2,1,0:T(8,128)S(1)} %get-tuple-element.82), channel_id=1, source_target_pairs={{4,8},{12,16},{20,24},{28,32},{36,40},{44,48},{52,56},{60,64},{68,... | collective-permute-start | bytes 3145736 | tf_op jit(solution)/shard_map/ppermute | solution.py:447
  40.0 5.1 %collective-permute-start.3 = (f32[16,4,8,256]{3,2,1,0:T(8,128)S(1)}, f32[16,4,8,256]{3,2,1,0:T(8,128)S(1)}, u32[]{:S(2)}, u32[]{:S(2)}) collective-permute-start(f32[16,4,8,256]{3,2,1,0:T(8,128)S(1)} %get-tuple-element.79), channel_id=1, source_target_pairs={{0,1},{2,3},{1,0},{3,2},{4,5},{6,7},{5,4},{7,6},{8,9},{10,11},{9,8... | collective-permute-start | bytes 1572872 | tf_op jit(solution)/shard_map/ppermute | solution.py:444
  45.1 0.7 collective-permute-start.4
  45.8 0.0 collective-permute-done.7.a_in
  45.8 2.9 %coefficients.1.coef = f32[5,24,48,256]{3,2,1,0:T(8,128)S(1)} custom-call(s32[16]{0:T(128)S(1)} %stack.67.place, f32[3]{0:T(128)S(1)} %copy-done.2, f32[16,4,8,256]{3,2,1,0:T(8,128)S(1)} %bitcast.31, f32[4,46,8,256]{3,2,1,0:T(8,128)S(1)} %collective-permute-done.7.a_in, f32[4,36,8,256]{3,2,1,0:T(8,128)S(1)} %collective-permute-done.2.b_in, ...), custom_call_target="tpu_custom_call" | custom-call | bytes 10500000 | tf_op jit(solution)/shard_map/coefficients/pallas_call | solution.py:37
  48.7 15.3 %step0.1 = (f32[16,32,8,256]{3,2,1,0:T(8,128)S(1)}, f32[4,32,8,256]{3,2,1,0:T(8,128)S(1)}, f32[16,4,8,256]{3,2,1,0:T(8,128)S(1)}, f32[16,4,8,256]{3,2,1,0:T(8,128)S(1)}) custom-call(s32[16]{0:T(128)S(1)} %stack.67.place, f32[16,32,8,256]{3,2,1,0:T(8,128)S(1)} %get-tuple-element.74.field, f32[4,46,8,256]{3,2,1,0:T(8,128)S(1)} %collective-permute-done.7.a_in, ...), custom_call_target="tpu_custom_call" | custom-call | bytes 42000000 | tf_op jit(solution)/shard_map/step0/pallas_call | solution.py:37
  64.0 0.0 collective-permute-done.3.c_in
  64.0 0.0 collective-permute-done.4.d_in
  64.0 0.0 collective-permute-done.6.b_in
  64.0 0.9 corners.5
  64.9 2.5 %collective-permute-start.10 = (f32[4,8,8,256]{3,2,1,0:T(8,128)S(1)}, f32[4,8,8,256]{3,2,1,0:T(8,128)S(1)}, u32[]{:S(2)}, u32[]{:S(2)}) collective-permute-start(f32[4,8,8,256]{3,2,1,0:T(8,128)S(1)} %get-tuple-element.94), channel_id=1, source_target_pairs={{4,8},{12,16},{20,24},{28,32},{36,40},{44,48},{52,56},{60,64},{68,... | collective-permute-start | bytes 786440 | tf_op jit(solution)/shard_map/ppermute | solution.py:454
  67.4 0.1 collective-permute-start.12
  67.5 5.1 %collective-permute-done.10.e_in = f32[4,8,8,256]{3,2,1,0:T(8,128)S(1)} collective-permute-done((f32[4,8,8,256]{3,2,1,0:T(8,128)S(1)}, f32[4,8,8,256]{3,2,1,0:T(8,128)S(1)}, u32[]{:S(2)}, u32[]{:S(2)}) %collective-permute-start.10) | collective-permute-done | bytes 262176 | tf_op jit(solution)/shard_map/ppermute | solution.py:454
  72.6 2.5 %collective-permute-start.11 = (f32[4,32,8,256]{3,2,1,0:T(8,128)S(1)}, f32[4,32,8,256]{3,2,1,0:T(8,128)S(1)}, u32[]{:S(2)}, u32[]{:S(2)}) collective-permute-start(f32[4,32,8,256]{3,2,1,0:T(8,128)S(1)} %get-tuple-element.98), channel_id=1, source_target_pairs={{4,8},{12,16},{20,24},{28,32},{36,40},{44,48},{52,56},{60,64},{68,... | collective-permute-start | bytes 3145736 | tf_op jit(solution)/shard_map/ppermute | solution.py:447
  75.1 3.1 %collective-permute-start.8 = (f32[16,4,8,256]{3,2,1,0:T(8,128)S(1)}, f32[16,4,8,256]{3,2,1,0:T(8,128)S(1)}, u32[]{:S(2)}, u32[]{:S(2)}) collective-permute-start(f32[16,4,8,256]{3,2,1,0:T(8,128)S(1)} %get-tuple-element.95), channel_id=1, source_target_pairs={{0,1},{2,3},{1,0},{3,2},{4,5},{6,7},{5,4},{7,6},{8,9},{10,11},{9,8... | collective-permute-start | bytes 1572872 | tf_op jit(solution)/shard_map/ppermute | solution.py:444
  78.2 0.7 collective-permute-start.9
  78.9 0.0 collective-permute-done.12.a_in
  78.9 15.3 %step1.1 = (f32[16,32,8,256]{3,2,1,0:T(8,128)S(1)}, f32[4,32,8,256]{3,2,1,0:T(8,128)S(1)}, f32[16,4,8,256]{3,2,1,0:T(8,128)S(1)}, f32[16,4,8,256]{3,2,1,0:T(8,128)S(1)}) custom-call(s32[16]{0:T(128)S(1)} %stack.67.place, f32[16,32,8,256]{3,2,1,0:T(8,128)S(1)} %get-tuple-element.90.field, f32[4,40,8,256]{3,2,1,0:T(8,128)S(1)} %collective-permute-done.12.a_in, ...), custom_call_target="tpu_custom_call" | custom-call | bytes 42000000 | tf_op jit(solution)/shard_map/step1/pallas_call | solution.py:37
  94.2 0.0 collective-permute-done.8.c_in
  94.2 0.0 collective-permute-done.9.d_in
  94.2 0.0 collective-permute-done.11.b_in
  94.2 0.0 copy-start.1
  94.2 0.9 corners.6
  95.1 0.1 collective-permute-start.17
  95.2 3.7 %collective-permute-start.15 = (f32[4,8,8,256]{3,2,1,0:T(8,128)S(1)}, f32[4,8,8,256]{3,2,1,0:T(8,128)S(1)}, u32[]{:S(2)}, u32[]{:S(2)}) collective-permute-start(f32[4,8,8,256]{3,2,1,0:T(8,128)S(1)} %get-tuple-element.111), channel_id=1, source_target_pairs={{4,8},{12,16},{20,24},{28,32},{36,40},{44,48},{52,56},{60,64},{68,... | collective-permute-start | bytes 786440 | tf_op jit(solution)/shard_map/ppermute | solution.py:454
  98.9 4.3 %collective-permute-done.15.e_in = f32[4,8,8,256]{3,2,1,0:T(8,128)S(1)} collective-permute-done((f32[4,8,8,256]{3,2,1,0:T(8,128)S(1)}, f32[4,8,8,256]{3,2,1,0:T(8,128)S(1)}, u32[]{:S(2)}, u32[]{:S(2)}) %collective-permute-start.15) | collective-permute-done | bytes 262176 | tf_op jit(solution)/shard_map/ppermute | solution.py:454
  103.3 3.3 %collective-permute-start.16 = (f32[4,32,8,256]{3,2,1,0:T(8,128)S(1)}, f32[4,32,8,256]{3,2,1,0:T(8,128)S(1)}, u32[]{:S(2)}, u32[]{:S(2)}) collective-permute-start(f32[4,32,8,256]{3,2,1,0:T(8,128)S(1)} %get-tuple-element.115), channel_id=1, source_target_pairs={{4,8},{12,16},{20,24},{28,32},{36,40},{44,48},{52,56},{60,64},{68,... | collective-permute-start | bytes 3145736 | tf_op jit(solution)/shard_map/ppermute | solution.py:447
  106.6 1.7 collective-permute-start.13
  108.4 0.7 collective-permute-start.14
  109.1 20.1 %last0.1 = (f32[16,16,32,256]{3,2,1,0:T(8,128)}, f32[8,128]{1,0:T(8,128)S(1)}) custom-call(s32[16]{0:T(128)S(1)} %stack.67.place, s32[128]{0:T(128)S(1)} %bitcast.32, f32[16,32,8,256]{3,2,1,0:T(8,128)S(1)} %get-tuple-element.107.field, f32[4,40,8,256]{3,2,1,0:T(8,128)S(1)} %collective-permute-done.17.a_in, ...), custom_call_target="tpu_custom_call" | custom-call | bytes 56000000 | tf_op jit(solution)/shard_map/last0/pallas_call | solution.py:37
  129.2 0.0 collective-permute-done.13.c_in
  129.2 0.0 collective-permute-done.14.d_in
  129.2 0.0 copy-start.5
  129.2 0.9 corners.7
  130.1 0.1 collective-permute-start.18
  130.9 0.2 convert_reduce_fusion
  131.1 3.7 %collective-permute-start.19 = (f32[4,8,8,256]{3,2,1,0:T(8,128)S(1)}, f32[4,8,8,256]{3,2,1,0:T(8,128)S(1)}, u32[]{:S(2)}, u32[]{:S(2)}) collective-permute-start(f32[4,8,8,256]{3,2,1,0:T(8,128)S(1)} %get-tuple-element.122), channel_id=1, source_target_pairs={{4,8},{12,16},{20,24},{28,32},{36,40},{44,48},{52,56},{60,64},{68,... | collective-permute-start | bytes 786440 | tf_op jit(solution)/shard_map/ppermute | solution.py:454
  134.8 0.0 copy-start.4
  134.8 3.9 %collective-permute-done.19.e_in = f32[4,8,8,256]{3,2,1,0:T(8,128)S(1)} collective-permute-done((f32[4,8,8,256]{3,2,1,0:T(8,128)S(1)}, f32[4,8,8,256]{3,2,1,0:T(8,128)S(1)}, u32[]{:S(2)}, u32[]{:S(2)}) %collective-permute-start.19) | collective-permute-done | bytes 262176 | tf_op jit(solution)/shard_map/ppermute | solution.py:454
  138.8 20.1 %last1.1 = (f32[16,16,32,256]{3,2,1,0:T(8,128)}, f32[8,128]{1,0:T(8,128)S(1)}) custom-call(s32[16]{0:T(128)S(1)} %stack.67.place, s32[128]{0:T(128)S(1)} %bitcast.33, f32[16,32,8,256]{3,2,1,0:T(8,128)S(1)} %get-tuple-element.104.field, f32[4,40,8,256]{3,2,1,0:T(8,128)S(1)} %collective-permute-done.18.a_in, ...), custom_call_target="tpu_custom_call", output_to_operand_aliasing={{0}: (9, {})} | custom-call | bytes 56000000 | tf_op jit(solution)/shard_map/last1/pallas_call | solution.py:37
  158.9 0.2 fusion.3
  159.1 29.5 %all_to_all.11 = f32[128,2,32]{2,1,0:T(2,128)S(1)} all-to-all(f32[128,2,32]{2,1,0:T(2,128)S(1)} %bitcast.35), channel_id=1, replica_groups=mesh['gx_0'=4,'gx_1'=4,'gx_2'=2,'gy'=4] {'gx_0','gx_1','gx_2','gy'}, dimensions={0} | all-to-all | bytes 65536 | tf_op jit(solution)/shard_map/all_to_all | solution.py:399
  188.6 0.4 fusion
  189.0 0.2 fusion.11
  189.2 0.1 broadcast_in_dim.4
  189.3 0.1 broadcast_in_dim.5
  189.4 14.1 %all_to_all.12 = f32[128,1,256]{2,1,0:T(1,128)S(1)} all-to-all(f32[128,1,256]{2,1,0:T(1,128)S(1)} %broadcast_in_dim.5), channel_id=1, replica_groups=mesh['gx_0'=4,'gx_1'=4,'gx_2'=2,'gy'=4] {'gx_0','gx_1','gx_2','gy'}, dimensions={0} | all-to-all | bytes 262144 | tf_op jit(solution)/shard_map/all_to_all | solution.py:406
  203.5 0.2 reduce_sum.19
  203.7 0.7 reshape.61
  (13 shorter events, 0.0 us)
Async XLA Ops:
  0.8 1.0 copy-start
  6.6 19.2 %collective-permute-start.2 = (f32[4,36,8,256]{3,2,1,0:T(8,128)S(1)}, f32[4,36,8,256]{3,2,1,0:T(8,128)S(1)}, u32[]{:S(2)}, u32[]{:S(2)}) collective-permute-start(f32[4,36,8,256]{3,2,1,0:T(8,128)S(1)} %get-tuple-element.67), channel_id=1, source_target_pairs={{4,8},{12,16},{20,24},{28,32},{36,40},{44,48},{52,56},{60,64},{68,... | collective-permute-start | bytes 3538952 | tf_op jit(solution)/shard_map/ppermute | solution.py:447
  11.1 14.6 %collective-permute-start = (f32[16,5,8,256]{3,2,1,0:T(8,128)S(1)}, f32[16,5,8,256]{3,2,1,0:T(8,128)S(1)}, u32[]{:S(2)}, u32[]{:S(2)}) collective-permute-start(f32[16,5,8,256]{3,2,1,0:T(8,128)S(1)} %get-tuple-element.65), channel_id=1, source_target_pairs={{0,1},{2,3},{1,0},{3,2},{4,5},{6,7},{5,4},{7,6},{8,9},{10,11},{9,8... | collective-permute-start | bytes 1966088 | tf_op jit(solution)/shard_map/ppermute | solution.py:444
  12.8 12.9 %collective-permute-start.1 = (f32[16,5,8,256]{3,2,1,0:T(8,128)S(1)}, f32[16,5,8,256]{3,2,1,0:T(8,128)S(1)}, u32[]{:S(2)}, u32[]{:S(2)}) collective-permute-start(f32[16,5,8,256]{3,2,1,0:T(8,128)S(1)} %get-tuple-element.66), channel_id=1, source_target_pairs={{1,2},{2,1},{5,6},{6,5},{9,10},{10,9},{13,14},{14,13},{17,18},{18,... | collective-permute-start | bytes 1966088 | tf_op jit(solution)/shard_map/ppermute | solution.py:444
  25.8 20.1 %copy-start.2 = (f32[3]{0:T(128)S(1)}, f32[3]{0:T(128)}, u32[]{:S(2)}) copy-start(f32[3]{0:T(128)} %wind.1) | copy-start | bytes 40
  26.7 19.0 %collective-permute-start.7 = (f32[4,46,8,256]{3,2,1,0:T(8,128)S(1)}, f32[4,46,8,256]{3,2,1,0:T(8,128)S(1)}, u32[]{:S(2)}, u32[]{:S(2)}) collective-permute-start(f32[4,46,8,256]{3,2,1,0:T(8,128)S(1)} %get-tuple-element.77), channel_id=1, source_target_pairs={{0,4},{8,12},{16,20},{24,28},{32,36},{40,44},{48,52},{56,60},{64,6... | collective-permute-start | bytes 4521992 | tf_op jit(solution)/shard_map/ppermute | solution.py:454
  26.8 9.8 %collective-permute-start.5 = (f32[4,10,8,256]{3,2,1,0:T(8,128)S(1)}, f32[4,10,8,256]{3,2,1,0:T(8,128)S(1)}, u32[]{:S(2)}, u32[]{:S(2)}) collective-permute-start(f32[4,10,8,256]{3,2,1,0:T(8,128)S(1)} %get-tuple-element.78), channel_id=1, source_target_pairs={{4,8},{12,16},{20,24},{28,32},{36,40},{44,48},{52,56},{60,64},{68,... | collective-permute-start | bytes 983048 | tf_op jit(solution)/shard_map/ppermute | solution.py:454
  36.6 27.4 %collective-permute-start.6 = (f32[4,32,8,256]{3,2,1,0:T(8,128)S(1)}, f32[4,32,8,256]{3,2,1,0:T(8,128)S(1)}, u32[]{:S(2)}, u32[]{:S(2)}) collective-permute-start(f32[4,32,8,256]{3,2,1,0:T(8,128)S(1)} %get-tuple-element.82), channel_id=1, source_target_pairs={{4,8},{12,16},{20,24},{28,32},{36,40},{44,48},{52,56},{60,64},{68,... | collective-permute-start | bytes 3145736 | tf_op jit(solution)/shard_map/ppermute | solution.py:447
  40.0 24.0 %collective-permute-start.3 = (f32[16,4,8,256]{3,2,1,0:T(8,128)S(1)}, f32[16,4,8,256]{3,2,1,0:T(8,128)S(1)}, u32[]{:S(2)}, u32[]{:S(2)}) collective-permute-start(f32[16,4,8,256]{3,2,1,0:T(8,128)S(1)} %get-tuple-element.79), channel_id=1, source_target_pairs={{0,1},{2,3},{1,0},{3,2},{4,5},{6,7},{5,4},{7,6},{8,9},{10,11},{9,8... | collective-permute-start | bytes 1572872 | tf_op jit(solution)/shard_map/ppermute | solution.py:444
  45.1 18.9 %collective-permute-start.4 = (f32[16,4,8,256]{3,2,1,0:T(8,128)S(1)}, f32[16,4,8,256]{3,2,1,0:T(8,128)S(1)}, u32[]{:S(2)}, u32[]{:S(2)}) collective-permute-start(f32[16,4,8,256]{3,2,1,0:T(8,128)S(1)} %get-tuple-element.80), channel_id=1, source_target_pairs={{1,2},{2,1},{5,6},{6,5},{9,10},{10,9},{13,14},{14,13},{17,18},{18,... | collective-permute-start | bytes 1572872 | tf_op jit(solution)/shard_map/ppermute | solution.py:444
  64.9 7.7 %collective-permute-start.10 = (f32[4,8,8,256]{3,2,1,0:T(8,128)S(1)}, f32[4,8,8,256]{3,2,1,0:T(8,128)S(1)}, u32[]{:S(2)}, u32[]{:S(2)}) collective-permute-start(f32[4,8,8,256]{3,2,1,0:T(8,128)S(1)} %get-tuple-element.94), channel_id=1, source_target_pairs={{4,8},{12,16},{20,24},{28,32},{36,40},{44,48},{52,56},{60,64},{68,... | collective-permute-start | bytes 786440 | tf_op jit(solution)/shard_map/ppermute | solution.py:454
  67.4 11.5 %collective-permute-start.12 = (f32[4,40,8,256]{3,2,1,0:T(8,128)S(1)}, f32[4,40,8,256]{3,2,1,0:T(8,128)S(1)}, u32[]{:S(2)}, u32[]{:S(2)}) collective-permute-start(f32[4,40,8,256]{3,2,1,0:T(8,128)S(1)} %get-tuple-element.93), channel_id=1, source_target_pairs={{0,4},{8,12},{16,20},{24,28},{32,36},{40,44},{48,52},{56,60},{64,6... | collective-permute-start | bytes 3932168 | tf_op jit(solution)/shard_map/ppermute | solution.py:454
  72.6 21.6 %collective-permute-start.11 = (f32[4,32,8,256]{3,2,1,0:T(8,128)S(1)}, f32[4,32,8,256]{3,2,1,0:T(8,128)S(1)}, u32[]{:S(2)}, u32[]{:S(2)}) collective-permute-start(f32[4,32,8,256]{3,2,1,0:T(8,128)S(1)} %get-tuple-element.98), channel_id=1, source_target_pairs={{4,8},{12,16},{20,24},{28,32},{36,40},{44,48},{52,56},{60,64},{68,... | collective-permute-start | bytes 3145736 | tf_op jit(solution)/shard_map/ppermute | solution.py:447
  75.1 19.1 %collective-permute-start.8 = (f32[16,4,8,256]{3,2,1,0:T(8,128)S(1)}, f32[16,4,8,256]{3,2,1,0:T(8,128)S(1)}, u32[]{:S(2)}, u32[]{:S(2)}) collective-permute-start(f32[16,4,8,256]{3,2,1,0:T(8,128)S(1)} %get-tuple-element.95), channel_id=1, source_target_pairs={{0,1},{2,3},{1,0},{3,2},{4,5},{6,7},{5,4},{7,6},{8,9},{10,11},{9,8... | collective-permute-start | bytes 1572872 | tf_op jit(solution)/shard_map/ppermute | solution.py:444
  78.2 16.0 %collective-permute-start.9 = (f32[16,4,8,256]{3,2,1,0:T(8,128)S(1)}, f32[16,4,8,256]{3,2,1,0:T(8,128)S(1)}, u32[]{:S(2)}, u32[]{:S(2)}) collective-permute-start(f32[16,4,8,256]{3,2,1,0:T(8,128)S(1)} %get-tuple-element.96), channel_id=1, source_target_pairs={{1,2},{2,1},{5,6},{6,5},{9,10},{10,9},{13,14},{14,13},{17,18},{18,... | collective-permute-start | bytes 1572872 | tf_op jit(solution)/shard_map/ppermute | solution.py:444
  94.2 14.8 %copy-start.1 = (s32[1,1,128]{2,1,0:T(1,128)S(1)}, s32[1,1,128]{2,1,0:T(1,128)}, u32[]{:S(2)}) copy-start(s32[1,1,128]{2,1,0:T(1,128)} %param.10) | copy-start | bytes 1540
  95.1 13.9 %collective-permute-start.17 = (f32[4,40,8,256]{3,2,1,0:T(8,128)S(1)}, f32[4,40,8,256]{3,2,1,0:T(8,128)S(1)}, u32[]{:S(2)}, u32[]{:S(2)}) collective-permute-start(f32[4,40,8,256]{3,2,1,0:T(8,128)S(1)} %get-tuple-element.110), channel_id=1, source_target_pairs={{0,4},{8,12},{16,20},{24,28},{32,36},{40,44},{48,52},{56,60},{64,6... | collective-permute-start | bytes 3932168 | tf_op jit(solution)/shard_map/ppermute | solution.py:454
  95.2 8.1 %collective-permute-start.15 = (f32[4,8,8,256]{3,2,1,0:T(8,128)S(1)}, f32[4,8,8,256]{3,2,1,0:T(8,128)S(1)}, u32[]{:S(2)}, u32[]{:S(2)}) collective-permute-start(f32[4,8,8,256]{3,2,1,0:T(8,128)S(1)} %get-tuple-element.111), channel_id=1, source_target_pairs={{4,8},{12,16},{20,24},{28,32},{36,40},{44,48},{52,56},{60,64},{68,... | collective-permute-start | bytes 786440 | tf_op jit(solution)/shard_map/ppermute | solution.py:454
  103.3 26.0 %collective-permute-start.16 = (f32[4,32,8,256]{3,2,1,0:T(8,128)S(1)}, f32[4,32,8,256]{3,2,1,0:T(8,128)S(1)}, u32[]{:S(2)}, u32[]{:S(2)}) collective-permute-start(f32[4,32,8,256]{3,2,1,0:T(8,128)S(1)} %get-tuple-element.115), channel_id=1, source_target_pairs={{4,8},{12,16},{20,24},{28,32},{36,40},{44,48},{52,56},{60,64},{68,... | collective-permute-start | bytes 3145736 | tf_op jit(solution)/shard_map/ppermute | solution.py:447
  106.6 22.6 %collective-permute-start.13 = (f32[16,4,8,256]{3,2,1,0:T(8,128)S(1)}, f32[16,4,8,256]{3,2,1,0:T(8,128)S(1)}, u32[]{:S(2)}, u32[]{:S(2)}) collective-permute-start(f32[16,4,8,256]{3,2,1,0:T(8,128)S(1)} %get-tuple-element.112), channel_id=1, source_target_pairs={{0,1},{2,3},{1,0},{3,2},{4,5},{6,7},{5,4},{7,6},{8,9},{10,11},{9,8... | collective-permute-start | bytes 1572872 | tf_op jit(solution)/shard_map/ppermute | solution.py:444
  108.4 20.9 %collective-permute-start.14 = (f32[16,4,8,256]{3,2,1,0:T(8,128)S(1)}, f32[16,4,8,256]{3,2,1,0:T(8,128)S(1)}, u32[]{:S(2)}, u32[]{:S(2)}) collective-permute-start(f32[16,4,8,256]{3,2,1,0:T(8,128)S(1)} %get-tuple-element.113), channel_id=1, source_target_pairs={{1,2},{2,1},{5,6},{6,5},{9,10},{10,9},{13,14},{14,13},{17,18},{18,... | collective-permute-start | bytes 1572872 | tf_op jit(solution)/shard_map/ppermute | solution.py:444
  129.2 1.6 copy-start.5
  130.1 8.6 %collective-permute-start.18 = (f32[4,40,8,256]{3,2,1,0:T(8,128)S(1)}, f32[4,40,8,256]{3,2,1,0:T(8,128)S(1)}, u32[]{:S(2)}, u32[]{:S(2)}) collective-permute-start(f32[4,40,8,256]{3,2,1,0:T(8,128)S(1)} %get-tuple-element.120), channel_id=1, source_target_pairs={{0,4},{8,12},{16,20},{24,28},{32,36},{40,44},{48,52},{56,60},{64,6... | collective-permute-start | bytes 3932168 | tf_op jit(solution)/shard_map/ppermute | solution.py:454
  131.1 7.7 %collective-permute-start.19 = (f32[4,8,8,256]{3,2,1,0:T(8,128)S(1)}, f32[4,8,8,256]{3,2,1,0:T(8,128)S(1)}, u32[]{:S(2)}, u32[]{:S(2)}) collective-permute-start(f32[4,8,8,256]{3,2,1,0:T(8,128)S(1)} %get-tuple-element.122), channel_id=1, source_target_pairs={{4,8},{12,16},{20,24},{28,32},{36,40},{44,48},{52,56},{60,64},{68,... | collective-permute-start | bytes 786440 | tf_op jit(solution)/shard_map/ppermute | solution.py:454
  134.8 24.1 %copy-start.4 = (f32[1,1,128,16]{2,3,1,0:T(8,128)S(1)}, f32[1,1,128,16]{2,3,1,0:T(8,128)}, u32[]{:S(2)}) copy-start(f32[1,1,128,16]{2,3,1,0:T(8,128)} %param.13) | copy-start | bytes 24580
  189.0 15.3 %copy-start.3 = (f32[16,16]{1,0:T(8,128)}, f32[16,16]{1,0:T(8,128)S(1)}, u32[]{:S(2)}) copy-start(f32[16,16]{1,0:T(8,128)S(1)} %fusion) | copy-start | bytes 3076

commit v2 on v1

--- a/solution.py
+++ b/solution.py
@@ -73,17 +73,16 @@
         c.wait()
 
 
-def face_pairs(field, place, x0, y0, b_out, c_out, d_out):
-    return [
-        (field.at[pl.ds(x0 + place[0], H), pl.ds(y0, NY)], b_out.at[:, pl.ds(0, NY)]),
-        (field.at[pl.ds(x0, NX), pl.ds(y0 + place[2], H)], c_out.at[:, pl.ds(0, H)]),
-        (field.at[pl.ds(x0, NX), pl.ds(y0 + place[3], H)], d_out.at[:, pl.ds(0, H)]),
-    ]
+def face_pairs(field, place, x0, y0, outs):
+    planes, all_x, all_y = pl.ds(x0 + place[0], H), pl.ds(x0, NX), pl.ds(y0, NY)
+    c_rows, d_rows = pl.ds(y0 + place[2], H), pl.ds(y0 + place[3], H)
+    taken = [(planes, all_y), (all_x, c_rows), (all_x, d_rows), (planes, c_rows), (planes, d_rows)]
+    return [(field.at[x, y], out.at[:, pl.ds(0, NY if y is all_y else H)]) for (x, y), out in zip(taken, outs)]
 
 
 def face_outs(extra):
     more = 1 if extra else 0
-    faces = [(H, NY + TILES * more, G, NZ), (NX, H + more, G, NZ), (NX, H + more, G, NZ)]
+    faces = [(H, NY + TILES * more, G, NZ)] + [(NX, H + more, G, NZ)] * 2 + [(H, H + more, G, NZ)] * 2
     return [(dims, VMEM) for dims in faces]
 
 
@@ -92,7 +91,8 @@
 
 def pack_kernel(g, place, probes, *rest):
     a_in = rest[0] if g == 0 else None
-    s_out, b_out, c_out, d_out, raw, mat, sem_in, sem_f = rest[-8:]
+    s_out, *outs = rest[-10:-4]
+    raw, mat, sem_in, sem_f = rest[-4:]
 
     def load(i):
         src = probes.at[pl.ds(g * G, G), pl.ds(i * PLANES, PLANES)]
@@ -110,12 +110,15 @@
         return carry
 
     lax.fori_loop(0, NX // PLANES, planes, 0)
-    pairs = face_pairs(s_out, place, 0, 0, b_out, c_out, d_out)
+    pairs = face_pairs(s_out, place, 0, 0, outs)
     if g == 0:
+        planes_out, c_tile, d_tile = pl.ds(place[0], H), pl.ds(place[10], 1), pl.ds(place[11], 1)
         pairs += [
-            (a_in.at[pl.ds(place[0], H)], b_out.at[:, pl.ds(NY, TILES)]),
-            (a_in.at[:, pl.ds(place[10], 1)], c_out.at[:, pl.ds(H, 1)]),
-            (a_in.at[:, pl.ds(place[11], 1)], d_out.at[:, pl.ds(H, 1)]),
+            (a_in.at[planes_out], outs[0].at[:, pl.ds(NY, TILES)]),
+            (a_in.at[:, c_tile], outs[1].at[:, pl.ds(H, 1)]),
+            (a_in.at[:, d_tile], outs[2].at[:, pl.ds(H, 1)]),
+            (a_in.at[planes_out, c_tile], outs[3].at[:, pl.ds(H, 1)]),
+            (a_in.at[planes_out, d_tile], outs[4].at[:, pl.ds(H, 1)]),
         ]
     copy_all(pairs, sem_f)
 
@@ -131,7 +134,7 @@
             pltpu.VMEM((G, NX, NY, NZ), F32),
             pltpu.VMEM((NZ, NZ), jnp.bfloat16),
             DMA((NX // PLANES,)),
-            DMA((6,)),
+            DMA((10,)),
         ],
         [SMEM, ANY] + [VMEM] * len(more),
         6,
@@ -139,45 +142,40 @@
     )
 
 
-def corner_kernel(place, field, c_in, d_in, *rest):
-    a_out, e_out, sems = rest[-3:]
-    inner, outer = pl.ds(place[1], H), pl.ds(place[0], H)
-    rows = pl.ds(0, H)
+def inner_kernel(place, field, c_in, d_in, *rest):
+    out, sems = rest[-2:]
+    inner, rows = pl.ds(place[1], H), pl.ds(0, H)
     pairs = [
-        (field.at[inner], a_out.at[:, pl.ds(H, NY)]),
-        (c_in.at[inner, rows], a_out.at[:, pl.ds(place[4], H)]),
-        (d_in.at[inner, rows], a_out.at[:, pl.ds(place[5], H)]),
-        (c_in.at[outer, rows], e_out.at[:, pl.ds(place[6], H)]),
-        (d_in.at[outer, rows], e_out.at[:, pl.ds(place[7], H)]),
+        (field.at[inner], out.at[:, pl.ds(H, NY)]),
+        (c_in.at[inner, rows], out.at[:, pl.ds(place[4], H)]),
+        (d_in.at[inner, rows], out.at[:, pl.ds(place[5], H)]),
     ]
-    if len(rest) > 3:
+    if len(rest) > 2:
         tile, base = pl.ds(H, 1), NY + 2 * H
         pairs += [
-            (rest[0].at[inner], a_out.at[:, pl.ds(base + 1, TILES)]),
-            (c_in.at[inner, tile], a_out.at[:, pl.ds(base + place[12], 1)]),
-            (d_in.at[inner, tile], a_out.at[:, pl.ds(base + place[13], 1)]),
-            (c_in.at[outer, tile], e_out.at[:, pl.ds(2 * H + place[14], 1)]),
-            (d_in.at[outer, tile], e_out.at[:, pl.ds(2 * H + place[15], 1)]),
+            (rest[0].at[inner], out.at[:, pl.ds(base + 1, TILES)]),
+            (c_in.at[inner, tile], out.at[:, pl.ds(base + place[12], 1)]),
+            (d_in.at[inner, tile], out.at[:, pl.ds(base + place[13], 1)]),
         ]
     copy_all(pairs, sems)
 
 
-def corners(place, field, c_in, d_in, a=None):
+def inner_planes(place, field, c_in, d_in, a=None):
     more = [] if a is None else [a]
     n = len(more)
     return kernel(
-        corner_kernel,
-        "corners",
+        inner_kernel,
+        "inner",
         [place, field, c_in, d_in] + more,
-        [((H, NY + 2 * H + (TILES + 2) * n, G, NZ), VMEM), ((H, 2 * H + 2 * n, G, NZ), VMEM)],
-        [DMA((10,))],
+        [((H, NY + 2 * H + (TILES + 2) * n, G, NZ), VMEM)],
+        [DMA((6,))],
         [SMEM] + [VMEM] * (3 + n),
         1,
         2,
-    )
-
-
-def coefficient_kernel(place, wind, a_own, a_in, b_in, c_in, d_in, e_in, out, wide, mat, sems):
+    )[0]
+
+
+def coefficient_kernel(place, wind, a_own, a_in, b_in, c_in, d_in, f_in, h_in, out, wide, mat, sems):
     base = NY + 2 * H
     outer, own, tile = pl.ds(place[8], H), pl.ds(1, TILES), pl.ds(H, 1)
     copy_all(
@@ -187,8 +185,8 @@
             (b_in.at[:, pl.ds(NY, TILES)], wide.at[outer, own]),
             (c_in.at[:, tile], wide.at[pl.ds(H, NX), pl.ds(place[12], 1)]),
             (d_in.at[:, tile], wide.at[pl.ds(H, NX), pl.ds(place[13], 1)]),
-            (e_in.at[:, pl.ds(2 * H, 1)], wide.at[outer, pl.ds(0, 1)]),
-            (e_in.at[:, pl.ds(2 * H + 1, 1)], wide.at[outer, pl.ds(TILES + 1, 1)]),
+            (f_in.at[:, tile], wide.at[outer, pl.ds(place[12], 1)]),
+            (h_in.at[:, tile], wide.at[outer, pl.ds(place[13], 1)]),
         ],
         sems,
     )
@@ -222,10 +220,10 @@
     return kernel(
         coefficient_kernel,
         "coefficients",
-        [place, wind, a_own] + state[1:6],
+        [place, wind, a_own] + state[1:],
         [((5, NX + 2 * H, 8 * (TILES + 2), NZ), VMEM)],
         [pltpu.VMEM(wide, F32), pltpu.VMEM((NZ, NZ), jnp.bfloat16), DMA((7,))],
-        [SMEM, SMEM] + [VMEM] * 6,
+        [SMEM, SMEM] + [VMEM] * 7,
         3,
         6,
     )[0]
@@ -275,7 +273,7 @@
     lax.fori_loop(0, (nx - 2 * number) // block, planes, 0)
 
 
-def gather_state(place, field, a_in, b_in, c_in, d_in, e_in, u, sems):
+def gather_state(place, field, a_in, b_in, c_in, d_in, f_in, h_in, u, sems):
     outer, own_x, own_y, rows = pl.ds(place[8], H), pl.ds(H, NX), pl.ds(H, NY), pl.ds(0, H)
     copy_all(
         [
@@ -284,8 +282,8 @@
             (b_in.at[:, pl.ds(0, NY)], u.at[outer, own_y]),
             (c_in.at[:, rows], u.at[own_x, pl.ds(place[4], H)]),
             (d_in.at[:, rows], u.at[own_x, pl.ds(place[5], H)]),
-            (e_in.at[:, rows], u.at[outer, rows]),
-            (e_in.at[:, pl.ds(H, H)], u.at[outer, pl.ds(H + NY, H)]),
+            (f_in.at[:, rows], u.at[outer, pl.ds(place[4], H)]),
+            (h_in.at[:, rows], u.at[outer, pl.ds(place[5], H)]),
         ],
         sems,
     )
@@ -297,11 +295,13 @@
         u, v = v, u
 
 
-def step_kernel(place, field, a_in, b_in, c_in, d_in, e_in, coef, s_out, b_out, c_out, d_out, u, v, scaled, sems):
-    gather_state(place, field, a_in, b_in, c_in, d_in, e_in, u, sems)
+def step_kernel(place, *refs):
+    state, coef, s_out, outs = refs[:7], refs[7], refs[8], refs[9:14]
+    u, v, scaled, sems = refs[14:]
+    gather_state(place, *state, u, sems)
     sweeps(u, v, scaled, coef)
     own = u.at[pl.ds(H, NX), pl.ds(H, NY)]
-    copy_all(face_pairs(u, place, H, H, b_out, c_out, d_out) + [(own, s_out)], sems)
+    copy_all(face_pairs(u, place, H, H, outs) + [(own, s_out)], sems)
 
 
 STATE_SCRATCH = [pltpu.VMEM((NX + 2 * H, NY + 2 * H, G, NZ), F32)] * 3
@@ -314,7 +314,7 @@
         [place, *state],
         [((NX, NY, G, NZ), VMEM)] + face_outs(False),
         STATE_SCRATCH + [DMA((8,))],
-        [SMEM] + [VMEM] * 7,
+        [SMEM] + [VMEM] * 8,
         12,
         24,
     )
@@ -333,9 +333,10 @@
     out[...] = lax.fori_loop(0, 128, one, jnp.zeros((G, 128), F32), unroll=8)
 
 
-def last_kernel(g, place, cells, field, a_in, b_in, c_in, d_in, e_in, coef, *rest):
+def last_kernel(g, place, cells, *rest):
+    state, coef = rest[:7], rest[7]
     out, reading, u, v, scaled, stage, mat, sems, sem_out = rest[-9:]
-    gather_state(place, field, a_in, b_in, c_in, d_in, e_in, u, sems)
+    gather_state(place, *state, u, sems)
     mat[...] = sorting(True)
     sweeps(u, v, scaled, coef)
 
@@ -371,10 +372,10 @@
             DMA((8,)),
             DMA((NX // PLANES,)),
         ],
-        [SMEM, SMEM] + [VMEM] * 7 + [ANY] * len(more),
+        [SMEM, SMEM] + [VMEM] * 8 + [ANY] * len(more),
         16,
         30,
-        {9: 0} if more else {},
+        {10: 0} if more else {},
     )
 
 
@@ -422,16 +423,14 @@
             either(odd, 0, NY - H),
             either(odd, NY + H, 0),
             either(odd, 0, NY + H),
-            either(odd, H, 0),
-            either(odd, 0, H),
+            0,
+            0,
             either(core, 0, NX + H),
             either(core, NX + H, 0),
             either(odd, TILES - 1, 0),
             either(odd, 0, TILES - 1),
             either(odd, TILES + 1, 0),
             either(odd, 0, TILES + 1),
-            either(odd, 1, 0),
-            either(odd, 0, 1),
         ]
     ).astype(jnp.int32)
     peers_x, peers_y = lax.axis_size(GX), lax.axis_size("gy")
@@ -440,45 +439,48 @@
     first = both([(i, i + 1) for i in range(0, peers_y - 1, 2)])
     second = both([(i, i + 1) for i in range(1, peers_y - 1, 2)])
 
-    def rows(c, d):
-        return lax.ppermute(c, "gy", first), lax.ppermute(d, "gy", second)
-
-    def planes(b):
-        return lax.ppermute(b, GX, outer)
-
-    def after(values, others):
-        return lax.optimization_barrier((tuple(values), tuple(others)))[0]
-
-    def finish(field, c, d, own=None):
-        a, e = corners(place, field, c, d, own)
-        return lax.ppermute(a, GX, inner), lax.ppermute(e, GX, outer), (a, e)
+    def across(pairs_x, pairs_y):
+        return [(i * peers_y + k, j * peers_y + n) for i, j in pairs_x for k, n in pairs_y]
+
+    def exchange(b, c, d, f, h):
+        return [
+            lax.ppermute(b, GX, outer),
+            lax.ppermute(c, "gy", first),
+            lax.ppermute(d, "gy", second),
+            lax.ppermute(f, ALL, across(outer, first)),
+            lax.ppermute(h, ALL, across(outer, second)),
+        ]
+
+    def after(*values):
+        return list(lax.optimization_barrier(values))
 
     probes = pltpu.with_memory_space_constraint(probes, pltpu.HBM)
     a_own = diffusivity.reshape(NX, TILES, 8, NZ)
     cells = sensor_cell.reshape(-1)
     made = [pack(0, place, probes, a_own), pack(1, place, probes, a_own)]
-    c, d = rows(*made[0][2:])
-    b = planes(made[0][1])
-    c, d, b, *made[1] = after((c, d, b, *made[1]), ())
+    arrived = exchange(*made[0][1:])
+    joined = after(*arrived, *made[1])
+    arrived, made[1] = joined[:5], joined[5:]
     coef = fields = None
     readings = []
     for turn in range(4):
         g, field = turn % 2, made[turn][0]
-        a, e, sent = finish(field, c, d, a_own if turn == 0 else None)
-        state = [field, a, b, c, d, e]
+        a = inner_planes(place, field, *arrived[1:3], *([a_own] if turn == 0 else []))
+        state = [field, lax.ppermute(a, GX, inner), *arrived]
         if turn < 3:
-            c, d = rows(*after(made[turn + 1][2:], sent))
-            b = planes(*after(made[turn + 1][1:2], (e,)))
+            leaving = after(*made[turn + 1][1:], a)[:5]
+            arrived = exchange(*leaving)
         if turn == 0:
             coef = coefficients(place, wind_speed, a_own, state)
         if turn < 2:
-            c, d, b, *out = after((c, d, b, *step(g, place, state + [coef])), ())
-            made.append(out)
+            joined = after(*arrived, *step(g, place, state + [coef]))
+            arrived = joined[:5]
+            made.append(joined[5:])
         else:
             fields, reading = last_step(g, place, cells, state + [coef], fields)
             readings.append(reading)
             if turn == 2:
-                c, d, b, fields = after((c, d, b, fields), ())
+                *arrived, fields = after(*arrived, fields)
     readings = jnp.concatenate(readings, axis=0)
     goal_block, ritz_gram = readings_exchange(readings, sensor_owner, sensor_count, goal_weight)
     return fields, goal_block, ritz_gram

time: 205 us -> 193 us (0.941)
  waiting for transfers between devices: 26 us -> 4.91 us
  starting transfers between devices: 43.1 us -> 55 us
  blocking collectives: 43.6 us -> 40.9 us
    ppermute x20 -> x24, waiting for transfers between devices: 26 us -> 4.91 us  [the longest x4 2.7 us: exchange(): lax.ppermute(f, ALL, across(outer, first))]
    ppermute x20 -> x24, starting transfers between devices: 43.1 us -> 55 us  [the longest x4 18.9 us: exchange(): lax.ppermute(f, ALL, across(outer, first))]
    all_to_all x1, blocking collectives: 29.5 us -> 26.9 us  [readings_exchange(): lax.all_to_all(outgoing, ALL, split_axis=0, concat_axis=0, tiled=True)]
  transfers between devices with their start and end apart: 20 -> 24, of which waited for: 5 -> 2; matrix products, arithmetic and copies ran while one was open for 0% -> 0% of each run, Pallas kernels for 29% -> 30%
where the time goes in v2:
time: 193 us
  Pallas kernels  86.7 us (45%)
  starting transfers between devices  55 us (28%)
  blocking collectives  40.9 us (21%)
  waiting for transfers between devices  4.91 us (3%)
  local copies, waits for them, and re-layouts  2.01 us (1%)
    pallas_call x11, Pallas kernels, kernel(): pl.pallas_call(body, in_specs=in_specs, out_specs=[spec for _, spec in ou...  86.7 us
    all_to_all x1, blocking collectives, readings_exchange(): lax.all_to_all(outgoing, ALL, split_axis=0, concat_axis=0, tiled=True)  26.9 us
    ppermute x4, starting transfers between devices, exchange(): lax.ppermute(f, ALL, across(outer, first))  18.9 us
    ppermute x4, starting transfers between devices, exchange(): lax.ppermute(b, GX, outer)  18.2 us
    all_to_all x1, blocking collectives, readings_exchange(): terms = lax.all_to_all(terms, ALL, split_axis=0, concat_axis=0, tiled=True)  14.1 us
    ppermute x4, starting transfers between devices, exchange(): lax.ppermute(c, 'gy', first)  12 us
  transfers between devices with their start and end apart: 24, of which 2 were waited for; matrix products, arithmetic and copies ran while one was open for 0% of the time, Pallas kernels for 30%

profile of v2, /device:TPU:1, one launch (start us, length us, event | category | flops | bytes accessed | tf_op | source)
XLA Modules:
  0.0 192.6 jit_solution(4237242823697514933)
XLA Ops:
  0.7 0.1 stack.51.place
  0.8 0.0 copy-start
  0.8 1.0 copy-done
  1.8 4.9 %pack0.1 = (f32[16,32,8,256]{3,2,1,0:T(8,128)S(1)}, f32[4,36,8,256]{3,2,1,0:T(8,128)S(1)}, f32[16,5,8,256]{3,2,1,0:T(8,128)S(1)}, f32[16,5,8,256]{3,2,1,0:T(8,12...) custom-call(s32[14]{0:T(128)S(1)} %stack.51.place, f32[16,16,32,256]{3,2,1,0:T(8,128)} %probes.3, ...), custom_call_target="tpu_custom_call" | custom-call | bytes 21000000 | tf_op jit(solution)/shard_map/pack0/pallas_call | solution.py:37
  6.7 4.5 %collective-permute-start = (f32[4,36,8,256]{3,2,1,0:T(8,128)S(1)}, f32[4,36,8,256]{3,2,1,0:T(8,128)S(1)}, u32[]{:S(2)}, u32[]{:S(2)}) collective-permute-start(f32[4,36,8,256]{3,2,1,0:T(8,128)S(1)} %get-tuple-element.85), channel_id=1, source_target_pairs={{4,8},{12,16},{20,24},{28,32},{36,40},{44,48},{52,56},{60,64},{68,... | collective-permute-start | bytes 3538952 | tf_op jit(solution)/shard_map/ppermute | solution.py:447
  11.3 1.7 collective-permute-start.1
  13.0 0.7 collective-permute-start.2
  13.7 6.4 %collective-permute-start.3 = (f32[4,5,8,256]{3,2,1,0:T(8,128)S(1)}, f32[4,5,8,256]{3,2,1,0:T(8,128)S(1)}, u32[]{:S(2)}, u32[]{:S(2)}) collective-permute-start(f32[4,5,8,256]{3,2,1,0:T(8,128)S(1)} %get-tuple-element.88), channel_id=1, source_target_pairs={{4,9},{6,11},{5,8},{7,10},{12,17},{14,19},{13,16},{15,18},{20,25},... | collective-permute-start | bytes 491528 | tf_op jit(solution)/shard_map/ppermute | solution.py:450
  20.1 0.7 collective-permute-start.4
  20.7 4.8 %pack1.1 = (f32[16,32,8,256]{3,2,1,0:T(8,128)S(1)}, f32[4,32,8,256]{3,2,1,0:T(8,128)S(1)}, f32[16,4,8,256]{3,2,1,0:T(8,128)S(1)}, f32[16,4,8,256]{3,2,1,0:T(8,12...) custom-call(s32[14]{0:T(128)S(1)} %stack.51.place, f32[16,16,32,256]{3,2,1,0:T(8,128)} %probes.3), custom_call_target="tpu_custom_call" | custom-call | bytes 21000000 | tf_op jit(solution)/shard_map/pack1/pallas_call | solution.py:37
  25.5 2.7 %collective-permute-done.3.f_in.refs_5_ = f32[4,5,8,256]{3,2,1,0:T(8,128)S(1)} collective-permute-done((f32[4,5,8,256]{3,2,1,0:T(8,128)S(1)}, f32[4,5,8,256]{3,2,1,0:T(8,128)S(1)}, u32[]{:S(2)}, u32[]{:S(2)}) %collective-permute-start.3) | collective-permute-done | bytes 163872 | tf_op jit(solution)/shard_map/ppermute | solution.py:450
  28.3 0.0 collective-permute-done.b_in.refs_2_
  28.3 0.0 copy-start.2
  28.3 0.8 inner.4
  29.1 0.1 collective-permute-start.10
  29.2 5.9 %collective-permute-start.5 = (f32[4,32,8,256]{3,2,1,0:T(8,128)S(1)}, f32[4,32,8,256]{3,2,1,0:T(8,128)S(1)}, u32[]{:S(2)}, u32[]{:S(2)}) collective-permute-start(f32[4,32,8,256]{3,2,1,0:T(8,128)S(1)} %get-tuple-element.104), channel_id=1, source_target_pairs={{4,8},{12,16},{20,24},{28,32},{36,40},{44,48},{52,56},{60,64},{68,... | collective-permute-start | bytes 3145736 | tf_op jit(solution)/shard_map/ppermute | solution.py:447
  35.1 5.1 %collective-permute-start.6 = (f32[16,4,8,256]{3,2,1,0:T(8,128)S(1)}, f32[16,4,8,256]{3,2,1,0:T(8,128)S(1)}, u32[]{:S(2)}, u32[]{:S(2)}) collective-permute-start(f32[16,4,8,256]{3,2,1,0:T(8,128)S(1)} %get-tuple-element.105), channel_id=1, source_target_pairs={{0,1},{2,3},{1,0},{3,2},{4,5},{6,7},{5,4},{7,6},{8,9},{10,11},{9,8... | collective-permute-start | bytes 1572872 | tf_op jit(solution)/shard_map/ppermute | solution.py:448
  40.2 0.7 collective-permute-start.7
  40.9 4.9 %collective-permute-start.8 = (f32[4,4,8,256]{3,2,1,0:T(8,128)S(1)}, f32[4,4,8,256]{3,2,1,0:T(8,128)S(1)}, u32[]{:S(2)}, u32[]{:S(2)}) collective-permute-start(f32[4,4,8,256]{3,2,1,0:T(8,128)S(1)} %get-tuple-element.107), channel_id=1, source_target_pairs={{4,9},{6,11},{5,8},{7,10},{12,17},{14,19},{13,16},{15,18},{20,25},... | collective-permute-start | bytes 393224 | tf_op jit(solution)/shard_map/ppermute | solution.py:450
  45.8 0.0 collective-permute-done.10.a_in.refs_1_
  45.8 0.7 collective-permute-start.9
  46.5 2.9 %coefficients.1.refs_7_.rest_7_ = f32[5,24,48,256]{3,2,1,0:T(8,128)S(1)} custom-call(s32[14]{0:T(128)S(1)} %stack.51.place, f32[3]{0:T(128)S(1)} %copy-done.2, f32[16,4,8,256]{3,2,1,0:T(8,128)S(1)} %bitcast.27, f32[4,46,8,256]{3,2,1,0:T(8,128)S(1)} %collective-permute-done.10.a_in.refs_1_, f32[4,36,8,256]{3,2,1,0:T(8,128)S(1)} %collective-permute-done.b_in.refs_2_, ...), custom_call_target="tpu_custom_call" | custom-call | bytes 10500000 | tf_op jit(solution)/shard_map/coefficients/pallas_call | solution.py:37
  49.4 15.4 %step0.1 = (f32[16,32,8,256]{3,2,1,0:T(8,128)S(1)}, f32[4,32,8,256]{3,2,1,0:T(8,128)S(1)}, f32[16,4,8,256]{3,2,1,0:T(8,128)S(1)}, f32[16,4,8,256]{3,2,1,0:T(8,12...) custom-call(s32[14]{0:T(128)S(1)} %stack.51.place, ...), custom_call_target="tpu_custom_call" | custom-call | bytes 42000000 | tf_op jit(solution)/shard_map/step0/pallas_call | solution.py:37
  64.8 0.0 collective-permute-done.6.c_in.refs_3_
  64.9 0.8 inner.5
  65.6 0.1 collective-permute-start.16
  65.7 4.0 %collective-permute-start.11 = (f32[4,32,8,256]{3,2,1,0:T(8,128)S(1)}, f32[4,32,8,256]{3,2,1,0:T(8,128)S(1)}, u32[]{:S(2)}, u32[]{:S(2)}) collective-permute-start(f32[4,32,8,256]{3,2,1,0:T(8,128)S(1)} %get-tuple-element.126), channel_id=1, source_target_pairs={{4,8},{12,16},{20,24},{28,32},{36,40},{44,48},{52,56},{60,64},{68,... | collective-permute-start | bytes 3145736 | tf_op jit(solution)/shard_map/ppermute | solution.py:447
  69.7 2.5 %collective-permute-start.12 = (f32[16,4,8,256]{3,2,1,0:T(8,128)S(1)}, f32[16,4,8,256]{3,2,1,0:T(8,128)S(1)}, u32[]{:S(2)}, u32[]{:S(2)}) collective-permute-start(f32[16,4,8,256]{3,2,1,0:T(8,128)S(1)} %get-tuple-element.127), channel_id=1, source_target_pairs={{0,1},{2,3},{1,0},{3,2},{4,5},{6,7},{5,4},{7,6},{8,9},{10,11},{9,8... | collective-permute-start | bytes 1572872 | tf_op jit(solution)/shard_map/ppermute | solution.py:448
  72.2 0.7 collective-permute-start.13
  72.9 3.5 %collective-permute-start.14 = (f32[4,4,8,256]{3,2,1,0:T(8,128)S(1)}, f32[4,4,8,256]{3,2,1,0:T(8,128)S(1)}, u32[]{:S(2)}, u32[]{:S(2)}) collective-permute-start(f32[4,4,8,256]{3,2,1,0:T(8,128)S(1)} %get-tuple-element.129), channel_id=1, source_target_pairs={{4,9},{6,11},{5,8},{7,10},{12,17},{14,19},{13,16},{15,18},{20,25},... | collective-permute-start | bytes 393224 | tf_op jit(solution)/shard_map/ppermute | solution.py:450
  76.4 0.0 collective-permute-done.16.refs_1_
  76.4 0.7 collective-permute-start.15
  77.0 15.4 %step1.1 = (f32[16,32,8,256]{3,2,1,0:T(8,128)S(1)}, f32[4,32,8,256]{3,2,1,0:T(8,128)S(1)}, f32[16,4,8,256]{3,2,1,0:T(8,128)S(1)}, f32[16,4,8,256]{3,2,1,0:T(8,12...) custom-call(s32[14]{0:T(128)S(1)} %stack.51.place, ...), custom_call_target="tpu_custom_call" | custom-call | bytes 42000000 | tf_op jit(solution)/shard_map/step1/pallas_call | solution.py:37
  92.4 0.0 collective-permute-done.14.rest_5_
  92.4 0.0 collective-permute-done.12.c_in.rest_3_
  92.4 0.0 collective-permute-done.13.d_in.rest_4_
  92.5 0.0 copy-start.1
  92.5 0.8 inner.6
  93.2 0.1 collective-permute-start.22
  93.3 3.8 %collective-permute-start.17 = (f32[4,32,8,256]{3,2,1,0:T(8,128)S(1)}, f32[4,32,8,256]{3,2,1,0:T(8,128)S(1)}, u32[]{:S(2)}, u32[]{:S(2)}) collective-permute-start(f32[4,32,8,256]{3,2,1,0:T(8,128)S(1)} %get-tuple-element.149), channel_id=1, source_target_pairs={{4,8},{12,16},{20,24},{28,32},{36,40},{44,48},{52,56},{60,64},{68,... | collective-permute-start | bytes 3145736 | tf_op jit(solution)/shard_map/ppermute | solution.py:447
  97.1 2.7 %collective-permute-start.18 = (f32[16,4,8,256]{3,2,1,0:T(8,128)S(1)}, f32[16,4,8,256]{3,2,1,0:T(8,128)S(1)}, u32[]{:S(2)}, u32[]{:S(2)}) collective-permute-start(f32[16,4,8,256]{3,2,1,0:T(8,128)S(1)} %get-tuple-element.150), channel_id=1, source_target_pairs={{0,1},{2,3},{1,0},{3,2},{4,5},{6,7},{5,4},{7,6},{8,9},{10,11},{9,8... | collective-permute-start | bytes 1572872 | tf_op jit(solution)/shard_map/ppermute | solution.py:448
  99.8 0.7 collective-permute-start.19
  100.5 4.2 %collective-permute-start.20 = (f32[4,4,8,256]{3,2,1,0:T(8,128)S(1)}, f32[4,4,8,256]{3,2,1,0:T(8,128)S(1)}, u32[]{:S(2)}, u32[]{:S(2)}) collective-permute-start(f32[4,4,8,256]{3,2,1,0:T(8,128)S(1)} %get-tuple-element.152), channel_id=1, source_target_pairs={{4,9},{6,11},{5,8},{7,10},{12,17},{14,19},{13,16},{15,18},{20,25},... | collective-permute-start | bytes 393224 | tf_op jit(solution)/shard_map/ppermute | solution.py:450
  104.7 0.0 collective-permute-done.22.rest_1_
  104.7 0.7 collective-permute-start.21
  105.4 20.1 %last0.1 = (f32[16,16,32,256]{3,2,1,0:T(8,128)}, f32[8,128]{1,0:T(8,128)S(1)}) custom-call(s32[14]{0:T(128)S(1)} %stack.51.place, s32[128]{0:T(128)S(1)} %bitcast.28, f32[16,32,8,256]{3,2,1,0:T(8,128)S(1)} %get-tuple-element.146.field.rest_0_, f32[4,40,8,256]{3,2,1,0:T(8,128)S(1)} %collective-permute-done.22.rest_1_, ...), custom_call_target="tpu_custom_call" | custom-call | bytes 56000000 | tf_op jit(solution)/shard_map/last0/pallas_call | solution.py:37
  125.5 0.0 collective-permute-done.20.rest_5_
  125.5 0.0 collective-permute-done.21.rest_6_
  125.6 0.0 copy-start.5
  125.6 0.8 inner.7
  126.4 0.3 collective-permute-start.23
  127.3 0.2 convert_reduce_fusion
  127.5 0.0 copy-start.4
  127.5 2.2 %collective-permute-done.23.rest_1_ = f32[4,40,8,256]{3,2,1,0:T(8,128)S(1)} collective-permute-done((f32[4,40,8,256]{3,2,1,0:T(8,128)S(1)}, f32[4,40,8,256]{3,2,1,0:T(8,128)S(1)}, u32[]{:S(2)}, u32[]{:S(2)}) %collective-permute-start.23) | collective-permute-done | bytes 1310752 | tf_op jit(solution)/shard_map/ppermute | solution.py:469
  129.7 20.1 %last1.1 = (f32[16,16,32,256]{3,2,1,0:T(8,128)}, f32[8,128]{1,0:T(8,128)S(1)}) custom-call(s32[14]{0:T(128)S(1)} %stack.51.place, s32[128]{0:T(128)S(1)} %bitcast.29, f32[16,32,8,256]{3,2,1,0:T(8,128)S(1)} %get-tuple-element.140.field.rest_0_, f32[4,40,8,256]{3,2,1,0:T(8,128)S(1)} %collective-permute-done.23.rest_1_, ...), custom_call_target="tpu_custom_call", output_to_operand_aliasing={{0}: (10, {})} | custom-call | bytes 56000000 | tf_op jit(solution)/shard_map/last1/pallas_call | solution.py:37
  149.8 0.2 fusion.3
  150.0 26.9 %all_to_all.11 = f32[128,2,32]{2,1,0:T(2,128)S(1)} all-to-all(f32[128,2,32]{2,1,0:T(2,128)S(1)} %bitcast.31), channel_id=1, replica_groups=mesh['gx_0'=4,'gx_1'=4,'gx_2'=2,'gy'=4] {'gx_0','gx_1','gx_2','gy'}, dimensions={0} | all-to-all | bytes 65536 | tf_op jit(solution)/shard_map/all_to_all | solution.py:400
  176.9 0.4 fusion
  177.3 0.2 fusion.11
  177.5 0.1 broadcast_in_dim.4
  177.6 0.1 broadcast_in_dim.5
  177.7 14.1 %all_to_all.12 = f32[128,1,256]{2,1,0:T(1,128)S(1)} all-to-all(f32[128,1,256]{2,1,0:T(1,128)S(1)} %broadcast_in_dim.5), channel_id=1, replica_groups=mesh['gx_0'=4,'gx_1'=4,'gx_2'=2,'gy'=4] {'gx_0','gx_1','gx_2','gy'}, dimensions={0} | all-to-all | bytes 262144 | tf_op jit(solution)/shard_map/all_to_all | solution.py:407
  191.8 0.2 reduce_sum.19
  192.0 0.7 reshape.61
  (22 shorter events, 0.1 us)
Async XLA Ops:
  0.8 1.0 copy-start
  6.7 21.5 %collective-permute-start = (f32[4,36,8,256]{3,2,1,0:T(8,128)S(1)}, f32[4,36,8,256]{3,2,1,0:T(8,128)S(1)}, u32[]{:S(2)}, u32[]{:S(2)}) collective-permute-start(f32[4,36,8,256]{3,2,1,0:T(8,128)S(1)} %get-tuple-element.85), channel_id=1, source_target_pairs={{4,8},{12,16},{20,24},{28,32},{36,40},{44,48},{52,56},{60,64},{68,... | collective-permute-start | bytes 3538952 | tf_op jit(solution)/shard_map/ppermute | solution.py:447
  11.3 17.0 %collective-permute-start.1 = (f32[16,5,8,256]{3,2,1,0:T(8,128)S(1)}, f32[16,5,8,256]{3,2,1,0:T(8,128)S(1)}, u32[]{:S(2)}, u32[]{:S(2)}) collective-permute-start(f32[16,5,8,256]{3,2,1,0:T(8,128)S(1)} %get-tuple-element.86), channel_id=1, source_target_pairs={{0,1},{2,3},{1,0},{3,2},{4,5},{6,7},{5,4},{7,6},{8,9},{10,11},{9,8... | collective-permute-start | bytes 1966088 | tf_op jit(solution)/shard_map/ppermute | solution.py:448
  13.0 15.3 %collective-permute-start.2 = (f32[16,5,8,256]{3,2,1,0:T(8,128)S(1)}, f32[16,5,8,256]{3,2,1,0:T(8,128)S(1)}, u32[]{:S(2)}, u32[]{:S(2)}) collective-permute-start(f32[16,5,8,256]{3,2,1,0:T(8,128)S(1)} %get-tuple-element.87), channel_id=1, source_target_pairs={{1,2},{2,1},{5,6},{6,5},{9,10},{10,9},{13,14},{14,13},{17,18},{18,... | collective-permute-start | bytes 1966088 | tf_op jit(solution)/shard_map/ppermute | solution.py:449
  13.7 14.6 %collective-permute-start.3 = (f32[4,5,8,256]{3,2,1,0:T(8,128)S(1)}, f32[4,5,8,256]{3,2,1,0:T(8,128)S(1)}, u32[]{:S(2)}, u32[]{:S(2)}) collective-permute-start(f32[4,5,8,256]{3,2,1,0:T(8,128)S(1)} %get-tuple-element.88), channel_id=1, source_target_pairs={{4,9},{6,11},{5,8},{7,10},{12,17},{14,19},{13,16},{15,18},{20,25},... | collective-permute-start | bytes 491528 | tf_op jit(solution)/shard_map/ppermute | solution.py:450
  20.1 8.2 %collective-permute-start.4 = (f32[4,5,8,256]{3,2,1,0:T(8,128)S(1)}, f32[4,5,8,256]{3,2,1,0:T(8,128)S(1)}, u32[]{:S(2)}, u32[]{:S(2)}) collective-permute-start(f32[4,5,8,256]{3,2,1,0:T(8,128)S(1)} %get-tuple-element.89), channel_id=1, source_target_pairs={{5,10},{6,9},{13,18},{14,17},{21,26},{22,25},{29,34},{30,33},{37,4... | collective-permute-start | bytes 491528 | tf_op jit(solution)/shard_map/ppermute | solution.py:451
  28.3 18.3 %copy-start.2 = (f32[3]{0:T(128)S(1)}, f32[3]{0:T(128)}, u32[]{:S(2)}) copy-start(f32[3]{0:T(128)} %wind.1) | copy-start | bytes 40
  29.1 16.7 %collective-permute-start.10 = (f32[4,46,8,256]{3,2,1,0:T(8,128)S(1)}, f32[4,46,8,256]{3,2,1,0:T(8,128)S(1)}, u32[]{:S(2)}, u32[]{:S(2)}) collective-permute-start(f32[4,46,8,256]{3,2,1,0:T(8,128)S(1)} %inner.4), channel_id=1, source_target_pairs={{0,4},{8,12},{16,20},{24,28},{32,36},{40,44},{48,52},{56,60},{64,6... | collective-permute-start | bytes 4521992 | tf_op jit(solution)/shard_map/ppermute | solution.py:469
  29.2 35.7 %collective-permute-start.5 = (f32[4,32,8,256]{3,2,1,0:T(8,128)S(1)}, f32[4,32,8,256]{3,2,1,0:T(8,128)S(1)}, u32[]{:S(2)}, u32[]{:S(2)}) collective-permute-start(f32[4,32,8,256]{3,2,1,0:T(8,128)S(1)} %get-tuple-element.104), channel_id=1, source_target_pairs={{4,8},{12,16},{20,24},{28,32},{36,40},{44,48},{52,56},{60,64},{68,... | collective-permute-start | bytes 3145736 | tf_op jit(solution)/shard_map/ppermute | solution.py:447
  35.1 29.7 %collective-permute-start.6 = (f32[16,4,8,256]{3,2,1,0:T(8,128)S(1)}, f32[16,4,8,256]{3,2,1,0:T(8,128)S(1)}, u32[]{:S(2)}, u32[]{:S(2)}) collective-permute-start(f32[16,4,8,256]{3,2,1,0:T(8,128)S(1)} %get-tuple-element.105), channel_id=1, source_target_pairs={{0,1},{2,3},{1,0},{3,2},{4,5},{6,7},{5,4},{7,6},{8,9},{10,11},{9,8... | collective-permute-start | bytes 1572872 | tf_op jit(solution)/shard_map/ppermute | solution.py:448
  40.2 24.6 %collective-permute-start.7 = (f32[16,4,8,256]{3,2,1,0:T(8,128)S(1)}, f32[16,4,8,256]{3,2,1,0:T(8,128)S(1)}, u32[]{:S(2)}, u32[]{:S(2)}) collective-permute-start(f32[16,4,8,256]{3,2,1,0:T(8,128)S(1)} %get-tuple-element.106), channel_id=1, source_target_pairs={{1,2},{2,1},{5,6},{6,5},{9,10},{10,9},{13,14},{14,13},{17,18},{18,... | collective-permute-start | bytes 1572872 | tf_op jit(solution)/shard_map/ppermute | solution.py:449
  40.9 23.9 %collective-permute-start.8 = (f32[4,4,8,256]{3,2,1,0:T(8,128)S(1)}, f32[4,4,8,256]{3,2,1,0:T(8,128)S(1)}, u32[]{:S(2)}, u32[]{:S(2)}) collective-permute-start(f32[4,4,8,256]{3,2,1,0:T(8,128)S(1)} %get-tuple-element.107), channel_id=1, source_target_pairs={{4,9},{6,11},{5,8},{7,10},{12,17},{14,19},{13,16},{15,18},{20,25},... | collective-permute-start | bytes 393224 | tf_op jit(solution)/shard_map/ppermute | solution.py:450
  45.8 19.0 %collective-permute-start.9 = (f32[4,4,8,256]{3,2,1,0:T(8,128)S(1)}, f32[4,4,8,256]{3,2,1,0:T(8,128)S(1)}, u32[]{:S(2)}, u32[]{:S(2)}) collective-permute-start(f32[4,4,8,256]{3,2,1,0:T(8,128)S(1)} %get-tuple-element.108), channel_id=1, source_target_pairs={{5,10},{6,9},{13,18},{14,17},{21,26},{22,25},{29,34},{30,33},{37,4... | collective-permute-start | bytes 393224 | tf_op jit(solution)/shard_map/ppermute | solution.py:451
  65.6 10.7 %collective-permute-start.16 = (f32[4,40,8,256]{3,2,1,0:T(8,128)S(1)}, f32[4,40,8,256]{3,2,1,0:T(8,128)S(1)}, u32[]{:S(2)}, u32[]{:S(2)}) collective-permute-start(f32[4,40,8,256]{3,2,1,0:T(8,128)S(1)} %inner.5), channel_id=1, source_target_pairs={{0,4},{8,12},{16,20},{24,28},{32,36},{40,44},{48,52},{56,60},{64,6... | collective-permute-start | bytes 3932168 | tf_op jit(solution)/shard_map/ppermute | solution.py:469
  65.7 26.7 %collective-permute-start.11 = (f32[4,32,8,256]{3,2,1,0:T(8,128)S(1)}, f32[4,32,8,256]{3,2,1,0:T(8,128)S(1)}, u32[]{:S(2)}, u32[]{:S(2)}) collective-permute-start(f32[4,32,8,256]{3,2,1,0:T(8,128)S(1)} %get-tuple-element.126), channel_id=1, source_target_pairs={{4,8},{12,16},{20,24},{28,32},{36,40},{44,48},{52,56},{60,64},{68,... | collective-permute-start | bytes 3145736 | tf_op jit(solution)/shard_map/ppermute | solution.py:447
  69.7 22.7 %collective-permute-start.12 = (f32[16,4,8,256]{3,2,1,0:T(8,128)S(1)}, f32[16,4,8,256]{3,2,1,0:T(8,128)S(1)}, u32[]{:S(2)}, u32[]{:S(2)}) collective-permute-start(f32[16,4,8,256]{3,2,1,0:T(8,128)S(1)} %get-tuple-element.127), channel_id=1, source_target_pairs={{0,1},{2,3},{1,0},{3,2},{4,5},{6,7},{5,4},{7,6},{8,9},{10,11},{9,8... | collective-permute-start | bytes 1572872 | tf_op jit(solution)/shard_map/ppermute | solution.py:448
  72.2 20.3 %collective-permute-start.13 = (f32[16,4,8,256]{3,2,1,0:T(8,128)S(1)}, f32[16,4,8,256]{3,2,1,0:T(8,128)S(1)}, u32[]{:S(2)}, u32[]{:S(2)}) collective-permute-start(f32[16,4,8,256]{3,2,1,0:T(8,128)S(1)} %get-tuple-element.128), channel_id=1, source_target_pairs={{1,2},{2,1},{5,6},{6,5},{9,10},{10,9},{13,14},{14,13},{17,18},{18,... | collective-permute-start | bytes 1572872 | tf_op jit(solution)/shard_map/ppermute | solution.py:449
  72.9 19.5 %collective-permute-start.14 = (f32[4,4,8,256]{3,2,1,0:T(8,128)S(1)}, f32[4,4,8,256]{3,2,1,0:T(8,128)S(1)}, u32[]{:S(2)}, u32[]{:S(2)}) collective-permute-start(f32[4,4,8,256]{3,2,1,0:T(8,128)S(1)} %get-tuple-element.129), channel_id=1, source_target_pairs={{4,9},{6,11},{5,8},{7,10},{12,17},{14,19},{13,16},{15,18},{20,25},... | collective-permute-start | bytes 393224 | tf_op jit(solution)/shard_map/ppermute | solution.py:450
  76.4 16.1 %collective-permute-start.15 = (f32[4,4,8,256]{3,2,1,0:T(8,128)S(1)}, f32[4,4,8,256]{3,2,1,0:T(8,128)S(1)}, u32[]{:S(2)}, u32[]{:S(2)}) collective-permute-start(f32[4,4,8,256]{3,2,1,0:T(8,128)S(1)} %get-tuple-element.130), channel_id=1, source_target_pairs={{5,10},{6,9},{13,18},{14,17},{21,26},{22,25},{29,34},{30,33},{37,4... | collective-permute-start | bytes 393224 | tf_op jit(solution)/shard_map/ppermute | solution.py:451
  92.5 12.9 %copy-start.1 = (s32[1,1,128]{2,1,0:T(1,128)S(1)}, s32[1,1,128]{2,1,0:T(1,128)}, u32[]{:S(2)}) copy-start(s32[1,1,128]{2,1,0:T(1,128)} %param.10) | copy-start | bytes 1540
  93.2 11.5 %collective-permute-start.22 = (f32[4,40,8,256]{3,2,1,0:T(8,128)S(1)}, f32[4,40,8,256]{3,2,1,0:T(8,128)S(1)}, u32[]{:S(2)}, u32[]{:S(2)}) collective-permute-start(f32[4,40,8,256]{3,2,1,0:T(8,128)S(1)} %inner.6), channel_id=1, source_target_pairs={{0,4},{8,12},{16,20},{24,28},{32,36},{40,44},{48,52},{56,60},{64,6... | collective-permute-start | bytes 3932168 | tf_op jit(solution)/shard_map/ppermute | solution.py:469
  93.3 32.2 %collective-permute-start.17 = (f32[4,32,8,256]{3,2,1,0:T(8,128)S(1)}, f32[4,32,8,256]{3,2,1,0:T(8,128)S(1)}, u32[]{:S(2)}, u32[]{:S(2)}) collective-permute-start(f32[4,32,8,256]{3,2,1,0:T(8,128)S(1)} %get-tuple-element.149), channel_id=1, source_target_pairs={{4,8},{12,16},{20,24},{28,32},{36,40},{44,48},{52,56},{60,64},{68,... | collective-permute-start | bytes 3145736 | tf_op jit(solution)/shard_map/ppermute | solution.py:447
  97.1 28.4 %collective-permute-start.18 = (f32[16,4,8,256]{3,2,1,0:T(8,128)S(1)}, f32[16,4,8,256]{3,2,1,0:T(8,128)S(1)}, u32[]{:S(2)}, u32[]{:S(2)}) collective-permute-start(f32[16,4,8,256]{3,2,1,0:T(8,128)S(1)} %get-tuple-element.150), channel_id=1, source_target_pairs={{0,1},{2,3},{1,0},{3,2},{4,5},{6,7},{5,4},{7,6},{8,9},{10,11},{9,8... | collective-permute-start | bytes 1572872 | tf_op jit(solution)/shard_map/ppermute | solution.py:448
  99.8 25.7 %collective-permute-start.19 = (f32[16,4,8,256]{3,2,1,0:T(8,128)S(1)}, f32[16,4,8,256]{3,2,1,0:T(8,128)S(1)}, u32[]{:S(2)}, u32[]{:S(2)}) collective-permute-start(f32[16,4,8,256]{3,2,1,0:T(8,128)S(1)} %get-tuple-element.151), channel_id=1, source_target_pairs={{1,2},{2,1},{5,6},{6,5},{9,10},{10,9},{13,14},{14,13},{17,18},{18,... | collective-permute-start | bytes 1572872 | tf_op jit(solution)/shard_map/ppermute | solution.py:449
  100.5 25.0 %collective-permute-start.20 = (f32[4,4,8,256]{3,2,1,0:T(8,128)S(1)}, f32[4,4,8,256]{3,2,1,0:T(8,128)S(1)}, u32[]{:S(2)}, u32[]{:S(2)}) collective-permute-start(f32[4,4,8,256]{3,2,1,0:T(8,128)S(1)} %get-tuple-element.152), channel_id=1, source_target_pairs={{4,9},{6,11},{5,8},{7,10},{12,17},{14,19},{13,16},{15,18},{20,25},... | collective-permute-start | bytes 393224 | tf_op jit(solution)/shard_map/ppermute | solution.py:450
  104.7 20.8 %collective-permute-start.21 = (f32[4,4,8,256]{3,2,1,0:T(8,128)S(1)}, f32[4,4,8,256]{3,2,1,0:T(8,128)S(1)}, u32[]{:S(2)}, u32[]{:S(2)}) collective-permute-start(f32[4,4,8,256]{3,2,1,0:T(8,128)S(1)} %get-tuple-element.153), channel_id=1, source_target_pairs={{5,10},{6,9},{13,18},{14,17},{21,26},{22,25},{29,34},{30,33},{37,4... | collective-permute-start | bytes 393224 | tf_op jit(solution)/shard_map/ppermute | solution.py:451
  125.6 1.7 copy-start.5
  126.4 3.3 %collective-permute-start.23 = (f32[4,40,8,256]{3,2,1,0:T(8,128)S(1)}, f32[4,40,8,256]{3,2,1,0:T(8,128)S(1)}, u32[]{:S(2)}, u32[]{:S(2)}) collective-permute-start(f32[4,40,8,256]{3,2,1,0:T(8,128)S(1)} %inner.7), channel_id=1, source_target_pairs={{0,4},{8,12},{16,20},{24,28},{32,36},{40,44},{48,52},{56,60},{64,6... | collective-permute-start | bytes 3932168 | tf_op jit(solution)/shard_map/ppermute | solution.py:469
  127.5 22.3 %copy-start.4 = (f32[1,1,128,16]{2,3,1,0:T(8,128)S(1)}, f32[1,1,128,16]{2,3,1,0:T(8,128)}, u32[]{:S(2)}) copy-start(f32[1,1,128,16]{2,3,1,0:T(8,128)} %param.13) | copy-start | bytes 24580
  177.3 15.3 %copy-start.3 = (f32[16,16]{1,0:T(8,128)}, f32[16,16]{1,0:T(8,128)S(1)}, u32[]{:S(2)}) copy-start(f32[16,16]{1,0:T(8,128)S(1)} %fusion) | copy-start | bytes 3076

commit v3 on v2

--- a/solution.py
+++ b/solution.py
@@ -65,11 +65,15 @@
     return dot(high, matrix) + (dot(mid, matrix) + dot(low, matrix))
 
 
-def copy_all(pairs, sems):
-    made = [pltpu.make_async_copy(a, b, sems.at[i]) for i, (a, b) in enumerate(pairs)]
+def start_all(pairs, sems, first=0):
+    made = [pltpu.make_async_copy(a, b, sems.at[first + i]) for i, (a, b) in enumerate(pairs)]
     for c in made:
         c.start()
-    for c in made:
+    return made
+
+
+def copy_all(pairs, sems):
+    for c in start_all(pairs, sems):
         c.wait()
 
 
@@ -100,6 +104,17 @@
 
     for i in range(NX // PLANES):
         load(i).start()
+    early = []
+    if g == 0:
+        planes_out, c_tile, d_tile = pl.ds(place[0], H), pl.ds(place[10], 1), pl.ds(place[11], 1)
+        pairs = [
+            (a_in.at[planes_out], outs[0].at[:, pl.ds(NY, TILES)]),
+            (a_in.at[:, c_tile], outs[1].at[:, pl.ds(H, 1)]),
+            (a_in.at[:, d_tile], outs[2].at[:, pl.ds(H, 1)]),
+            (a_in.at[planes_out, c_tile], outs[3].at[:, pl.ds(H, 1)]),
+            (a_in.at[planes_out, d_tile], outs[4].at[:, pl.ds(H, 1)]),
+        ]
+        early = start_all(pairs, sem_f, 5)
     mat[...] = sorting(False)
 
     def planes(i, carry):
@@ -110,21 +125,13 @@
         return carry
 
     lax.fori_loop(0, NX // PLANES, planes, 0)
-    pairs = face_pairs(s_out, place, 0, 0, outs)
-    if g == 0:
-        planes_out, c_tile, d_tile = pl.ds(place[0], H), pl.ds(place[10], 1), pl.ds(place[11], 1)
-        pairs += [
-            (a_in.at[planes_out], outs[0].at[:, pl.ds(NY, TILES)]),
-            (a_in.at[:, c_tile], outs[1].at[:, pl.ds(H, 1)]),
-            (a_in.at[:, d_tile], outs[2].at[:, pl.ds(H, 1)]),
-            (a_in.at[planes_out, c_tile], outs[3].at[:, pl.ds(H, 1)]),
-            (a_in.at[planes_out, d_tile], outs[4].at[:, pl.ds(H, 1)]),
-        ]
-    copy_all(pairs, sem_f)
+    copy_all(face_pairs(s_out, place, 0, 0, outs), sem_f)
+    for c in early:
+        c.wait()
 
 
 def pack(g, place, probes, a):
-    more = [a] if g == 0 else []
+    more = [pltpu.with_memory_space_constraint(a, pltpu.HBM)] if g == 0 else []
     return kernel(
         functools.partial(pack_kernel, g),
         f"pack{g}",
@@ -136,7 +143,7 @@
             DMA((NX // PLANES,)),
             DMA((10,)),
         ],
-        [SMEM, ANY] + [VMEM] * len(more),
+        [SMEM, ANY] + [ANY] * len(more),
         6,
         12,
     )
@@ -235,7 +242,7 @@
 def sweep(number, src, dst, scaled, coef):
     nx, ny = src.shape[:2]
     last = lax.broadcasted_iota(jnp.int32, (G, 128), 1) == 127
-    block = 2
+    block = 2 if (nx - 2 * number) % 4 else 4
 
     def row(ref, x, y, z):
         return ref[x, y, :, z * 128 : (z + 1) * 128]
@@ -459,15 +466,18 @@
     cells = sensor_cell.reshape(-1)
     made = [pack(0, place, probes, a_own), pack(1, place, probes, a_own)]
     arrived = exchange(*made[0][1:])
-    joined = after(*arrived, *made[1])
-    arrived, made[1] = joined[:5], joined[5:]
+    queued = exchange(*made[1][1:4], *after(*made[1][4:], *arrived[3:])[:2])
+    joined = after(*arrived, *made[1], *queued[3:])
+    arrived, made[1], queued[3:] = joined[:5], joined[5:11], joined[11:]
     coef = fields = None
     readings = []
     for turn in range(4):
         g, field = turn % 2, made[turn][0]
         a = inner_planes(place, field, *arrived[1:3], *([a_own] if turn == 0 else []))
         state = [field, lax.ppermute(a, GX, inner), *arrived]
-        if turn < 3:
+        if turn == 0:
+            arrived = queued
+        elif turn < 3:
             leaving = after(*made[turn + 1][1:], a)[:5]
             arrived = exchange(*leaving)
         if turn == 0:

time: 193 us -> 192 us (level)
    ppermute x4, starting transfers between devices: 18.9 us -> 24.6 us  [exchange(): lax.ppermute(f, ALL, across(outer, first))]
    ppermute x4, starting transfers between devices: 18.2 us -> 15.4 us  [exchange(): lax.ppermute(b, GX, outer)]
    ppermute x4, starting transfers between devices: 12 us -> 9.88 us  [exchange(): lax.ppermute(c, 'gy', first)]
  transfers between devices with their start and end apart: 24 -> 24, of which waited for: 2 -> 3; matrix products, arithmetic and copies ran while one was open for 0% -> 0% of each run, Pallas kernels for 30% -> 30%
where the time goes in v3:
time: 192 us
  Pallas kernels  85.8 us (45%)
  starting transfers between devices  56 us (29%)
  blocking collectives  39.1 us (20%)
  waiting for transfers between devices  6.72 us (4%)
    pallas_call x11, Pallas kernels, kernel(): pl.pallas_call(body, in_specs=in_specs, out_specs=[spec for _, spec in ou...  85.8 us
    all_to_all x1, blocking collectives, readings_exchange(): lax.all_to_all(outgoing, ALL, split_axis=0, concat_axis=0, tiled=True)  25 us
    ppermute x4, starting transfers between devices, exchange(): lax.ppermute(f, ALL, across(outer, first))  24.6 us
    ppermute x4, starting transfers between devices, exchange(): lax.ppermute(b, GX, outer)  15.4 us
    all_to_all x1, blocking collectives, readings_exchange(): terms = lax.all_to_all(terms, ALL, split_axis=0, concat_axis=0, tiled=True)  14.1 us
    ppermute x4, starting transfers between devices, exchange(): lax.ppermute(c, 'gy', first)  9.88 us
    ppermute x4, waiting for transfers between devices, exchange(): lax.ppermute(f, ALL, across(outer, first))  4.51 us
  transfers between devices with their start and end apart: 24, of which 3 were waited for; matrix products, arithmetic and copies ran while one was open for 0% of the time, Pallas kernels for 30%

profile of v3, /device:TPU:1, one launch (start us, length us, event | category | flops | bytes accessed | tf_op | source)
XLA Modules:
  0.0 191.6 jit_solution(16033676948030463348)
XLA Ops:
  0.7 0.1 stack.51.place
  0.8 4.9 %pack0.1 = (f32[16,32,8,256]{3,2,1,0:T(8,128)S(1)}, f32[4,36,8,256]{3,2,1,0:T(8,128)S(1)}, f32[16,5,8,256]{3,2,1,0:T(8,128)S(1)}, f32[16,5,8,256]{3,2,1,0:T(8,12...) custom-call(s32[14]{0:T(128)S(1)} %stack.51.place, f32[16,16,32,256]{3,2,1,0:T(8,128)} %probes.3, ...), custom_call_target="tpu_custom_call" | custom-call | bytes 21000000 | tf_op jit(solution)/shard_map/pack0/pallas_call | solution.py:37
  5.7 4.5 %collective-permute-start.3 = (f32[4,36,8,256]{3,2,1,0:T(8,128)S(1)}, f32[4,36,8,256]{3,2,1,0:T(8,128)S(1)}, u32[]{:S(2)}, u32[]{:S(2)}) collective-permute-start(f32[4,36,8,256]{3,2,1,0:T(8,128)S(1)} %get-tuple-element.82), channel_id=1, source_target_pairs={{4,8},{12,16},{20,24},{28,32},{36,40},{44,48},{52,56},{60,64},{68,... | collective-permute-start | bytes 3538952 | tf_op jit(solution)/shard_map/ppermute | solution.py:454
  10.2 1.7 collective-permute-start.4
  11.9 0.7 collective-permute-start.5
  12.6 6.4 %collective-permute-start.6 = (f32[4,5,8,256]{3,2,1,0:T(8,128)S(1)}, f32[4,5,8,256]{3,2,1,0:T(8,128)S(1)}, u32[]{:S(2)}, u32[]{:S(2)}) collective-permute-start(f32[4,5,8,256]{3,2,1,0:T(8,128)S(1)} %get-tuple-element.85), channel_id=1, source_target_pairs={{4,9},{6,11},{5,8},{7,10},{12,17},{14,19},{13,16},{15,18},{20,25},... | collective-permute-start | bytes 491528 | tf_op jit(solution)/shard_map/ppermute | solution.py:457
  19.0 0.0 copy-start
  19.0 0.8 collective-permute-start.7
  19.8 4.8 %pack1.1 = (f32[16,32,8,256]{3,2,1,0:T(8,128)S(1)}, f32[4,32,8,256]{3,2,1,0:T(8,128)S(1)}, f32[16,4,8,256]{3,2,1,0:T(8,128)S(1)}, f32[16,4,8,256]{3,2,1,0:T(8,12...) custom-call(s32[14]{0:T(128)S(1)} %stack.51.place, f32[16,16,32,256]{3,2,1,0:T(8,128)} %probes.3), custom_call_target="tpu_custom_call" | custom-call | bytes 21000000 | tf_op jit(solution)/shard_map/pack1/pallas_call | solution.py:37
  24.6 2.5 %collective-permute-done.6.f_in.refs_5_ = f32[4,5,8,256]{3,2,1,0:T(8,128)S(1)} collective-permute-done((f32[4,5,8,256]{3,2,1,0:T(8,128)S(1)}, f32[4,5,8,256]{3,2,1,0:T(8,128)S(1)}, u32[]{:S(2)}, u32[]{:S(2)}) %collective-permute-start.6) | collective-permute-done | bytes 163872 | tf_op jit(solution)/shard_map/ppermute | solution.py:457
  27.2 0.0 collective-permute-done.7.h_in.refs_6_
  27.2 9.3 %collective-permute-start.8 = (f32[4,4,8,256]{3,2,1,0:T(8,128)S(1)}, f32[4,4,8,256]{3,2,1,0:T(8,128)S(1)}, u32[]{:S(2)}, u32[]{:S(2)}) collective-permute-start(f32[4,4,8,256]{3,2,1,0:T(8,128)S(1)} %get-tuple-element.90), channel_id=1, source_target_pairs={{4,9},{6,11},{5,8},{7,10},{12,17},{14,19},{13,16},{15,18},{20,25},... | collective-permute-start | bytes 393224 | tf_op jit(solution)/shard_map/ppermute | solution.py:457
  36.5 0.7 collective-permute-start.9
  37.1 2.0 %collective-permute-done.8.refs_5_ = f32[4,4,8,256]{3,2,1,0:T(8,128)S(1)} collective-permute-done((f32[4,4,8,256]{3,2,1,0:T(8,128)S(1)}, f32[4,4,8,256]{3,2,1,0:T(8,128)S(1)}, u32[]{:S(2)}, u32[]{:S(2)}) %collective-permute-start.8) | collective-permute-done | bytes 131104 | tf_op jit(solution)/shard_map/ppermute | solution.py:457
  39.1 0.0 collective-permute-done.4.c_in.refs_3_
  39.1 0.0 collective-permute-done.5.d_in.refs_4_
  39.1 0.0 collective-permute-done.3.b_in.refs_2_
  39.1 0.0 copy-start.2
  39.2 0.8 inner.4
  40.0 0.1 collective-permute-start.10
  40.1 3.6 %collective-permute-start = (f32[4,32,8,256]{3,2,1,0:T(8,128)S(1)}, f32[4,32,8,256]{3,2,1,0:T(8,128)S(1)}, u32[]{:S(2)}, u32[]{:S(2)}) collective-permute-start(f32[4,32,8,256]{3,2,1,0:T(8,128)S(1)} %get-tuple-element.79), channel_id=1, source_target_pairs={{4,8},{12,16},{20,24},{28,32},{36,40},{44,48},{52,56},{60,64},{68,... | collective-permute-start | bytes 3145736 | tf_op jit(solution)/shard_map/ppermute | solution.py:454
  43.7 4.5 %collective-permute-start.1 = (f32[16,4,8,256]{3,2,1,0:T(8,128)S(1)}, f32[16,4,8,256]{3,2,1,0:T(8,128)S(1)}, u32[]{:S(2)}, u32[]{:S(2)}) collective-permute-start(f32[16,4,8,256]{3,2,1,0:T(8,128)S(1)} %get-tuple-element.80), channel_id=1, source_target_pairs={{0,1},{2,3},{1,0},{3,2},{4,5},{6,7},{5,4},{7,6},{8,9},{10,11},{9,8... | collective-permute-start | bytes 1572872 | tf_op jit(solution)/shard_map/ppermute | solution.py:455
  48.2 0.7 collective-permute-start.2
  48.9 0.0 collective-permute-done.10.a_in.refs_1_
  48.9 2.9 %coefficients.1.refs_7_.rest_7_ = f32[5,24,48,256]{3,2,1,0:T(8,128)S(1)} custom-call(s32[14]{0:T(128)S(1)} %stack.51.place, f32[3]{0:T(128)S(1)} %copy-done.2, f32[16,4,8,256]{3,2,1,0:T(8,128)S(1)} %bitcast.27, f32[4,46,8,256]{3,2,1,0:T(8,128)S(1)} %collective-permute-done.10.a_in.refs_1_, f32[4,36,8,256]{3,2,1,0:T(8,128)S(1)} %collective-permute-done.3.b_in.refs_2_, ...), custom_call_target="tpu_custom_call" | custom-call | bytes 10500000 | tf_op jit(solution)/shard_map/coefficients/pallas_call | solution.py:37
  51.8 15.1 %step0.1 = (f32[16,32,8,256]{3,2,1,0:T(8,128)S(1)}, f32[4,32,8,256]{3,2,1,0:T(8,128)S(1)}, f32[16,4,8,256]{3,2,1,0:T(8,128)S(1)}, f32[16,4,8,256]{3,2,1,0:T(8,12...) custom-call(s32[14]{0:T(128)S(1)} %stack.51.place, ...), custom_call_target="tpu_custom_call" | custom-call | bytes 42000000 | tf_op jit(solution)/shard_map/step0/pallas_call | solution.py:37
  67.0 0.0 collective-permute-done.1.c_in.refs_3_
  67.0 0.8 inner.5
  67.8 0.1 collective-permute-start.16
  67.9 3.7 %collective-permute-start.11 = (f32[4,32,8,256]{3,2,1,0:T(8,128)S(1)}, f32[4,32,8,256]{3,2,1,0:T(8,128)S(1)}, u32[]{:S(2)}, u32[]{:S(2)}) collective-permute-start(f32[4,32,8,256]{3,2,1,0:T(8,128)S(1)} %get-tuple-element.114), channel_id=1, source_target_pairs={{4,8},{12,16},{20,24},{28,32},{36,40},{44,48},{52,56},{60,64},{68,... | collective-permute-start | bytes 3145736 | tf_op jit(solution)/shard_map/ppermute | solution.py:454
  71.6 1.3 collective-permute-start.12
  72.9 0.7 collective-permute-start.13
  73.6 4.6 %collective-permute-start.14 = (f32[4,4,8,256]{3,2,1,0:T(8,128)S(1)}, f32[4,4,8,256]{3,2,1,0:T(8,128)S(1)}, u32[]{:S(2)}, u32[]{:S(2)}) collective-permute-start(f32[4,4,8,256]{3,2,1,0:T(8,128)S(1)} %get-tuple-element.117), channel_id=1, source_target_pairs={{4,9},{6,11},{5,8},{7,10},{12,17},{14,19},{13,16},{15,18},{20,25},... | collective-permute-start | bytes 393224 | tf_op jit(solution)/shard_map/ppermute | solution.py:457
  78.2 0.0 collective-permute-done.16.refs_1_
  78.2 0.7 collective-permute-start.15
  78.9 15.1 %step1.1 = (f32[16,32,8,256]{3,2,1,0:T(8,128)S(1)}, f32[4,32,8,256]{3,2,1,0:T(8,128)S(1)}, f32[16,4,8,256]{3,2,1,0:T(8,128)S(1)}, f32[16,4,8,256]{3,2,1,0:T(8,12...) custom-call(s32[14]{0:T(128)S(1)} %stack.51.place, ...), custom_call_target="tpu_custom_call" | custom-call | bytes 42000000 | tf_op jit(solution)/shard_map/step1/pallas_call | solution.py:37
  94.0 0.0 collective-permute-done.15.rest_6_
  94.1 0.0 collective-permute-done.12.c_in.rest_3_
  94.1 0.0 collective-permute-done.11.rest_2_
  94.1 0.0 copy-start.1
  94.1 0.8 inner.6
  94.9 0.1 collective-permute-start.22
  95.0 3.6 %collective-permute-start.17 = (f32[4,32,8,256]{3,2,1,0:T(8,128)S(1)}, f32[4,32,8,256]{3,2,1,0:T(8,128)S(1)}, u32[]{:S(2)}, u32[]{:S(2)}) collective-permute-start(f32[4,32,8,256]{3,2,1,0:T(8,128)S(1)} %get-tuple-element.137), channel_id=1, source_target_pairs={{4,8},{12,16},{20,24},{28,32},{36,40},{44,48},{52,56},{60,64},{68,... | collective-permute-start | bytes 3145736 | tf_op jit(solution)/shard_map/ppermute | solution.py:454
  98.6 2.3 %collective-permute-start.18 = (f32[16,4,8,256]{3,2,1,0:T(8,128)S(1)}, f32[16,4,8,256]{3,2,1,0:T(8,128)S(1)}, u32[]{:S(2)}, u32[]{:S(2)}) collective-permute-start(f32[16,4,8,256]{3,2,1,0:T(8,128)S(1)} %get-tuple-element.138), channel_id=1, source_target_pairs={{0,1},{2,3},{1,0},{3,2},{4,5},{6,7},{5,4},{7,6},{8,9},{10,11},{9,8... | collective-permute-start | bytes 1572872 | tf_op jit(solution)/shard_map/ppermute | solution.py:455
  100.9 0.7 collective-permute-start.19
  101.6 4.3 %collective-permute-start.20 = (f32[4,4,8,256]{3,2,1,0:T(8,128)S(1)}, f32[4,4,8,256]{3,2,1,0:T(8,128)S(1)}, u32[]{:S(2)}, u32[]{:S(2)}) collective-permute-start(f32[4,4,8,256]{3,2,1,0:T(8,128)S(1)} %get-tuple-element.140), channel_id=1, source_target_pairs={{4,9},{6,11},{5,8},{7,10},{12,17},{14,19},{13,16},{15,18},{20,25},... | collective-permute-start | bytes 393224 | tf_op jit(solution)/shard_map/ppermute | solution.py:457
  106.0 0.8 collective-permute-start.21
  106.9 19.9 %last0.1 = (f32[16,16,32,256]{3,2,1,0:T(8,128)}, f32[8,128]{1,0:T(8,128)S(1)}) custom-call(s32[14]{0:T(128)S(1)} %stack.51.place, s32[128]{0:T(128)S(1)} %bitcast.28, f32[16,32,8,256]{3,2,1,0:T(8,128)S(1)} %get-tuple-element.134.field.rest_0_, f32[4,40,8,256]{3,2,1,0:T(8,128)S(1)} %collective-permute-done.22.rest_1_, ...), custom_call_target="tpu_custom_call" | custom-call | bytes 56000000 | tf_op jit(solution)/shard_map/last0/pallas_call | solution.py:37
  126.8 0.0 copy-start.5
  126.8 0.8 inner.7
  127.6 0.1 collective-permute-start.23
  128.4 0.2 convert_reduce_fusion
  128.6 0.0 copy-start.4
  128.6 2.2 %collective-permute-done.23.rest_1_ = f32[4,40,8,256]{3,2,1,0:T(8,128)S(1)} collective-permute-done((f32[4,40,8,256]{3,2,1,0:T(8,128)S(1)}, f32[4,40,8,256]{3,2,1,0:T(8,128)S(1)}, u32[]{:S(2)}, u32[]{:S(2)}) %collective-permute-start.23) | collective-permute-done | bytes 1310752 | tf_op jit(solution)/shard_map/ppermute | solution.py:477
  130.7 19.9 %last1.1 = (f32[16,16,32,256]{3,2,1,0:T(8,128)}, f32[8,128]{1,0:T(8,128)S(1)}) custom-call(s32[14]{0:T(128)S(1)} %stack.51.place, s32[128]{0:T(128)S(1)} %bitcast.29, f32[16,32,8,256]{3,2,1,0:T(8,128)S(1)} %get-tuple-element.128.field.rest_0_, f32[4,40,8,256]{3,2,1,0:T(8,128)S(1)} %collective-permute-done.23.rest_1_, ...), custom_call_target="tpu_custom_call", output_to_operand_aliasing={{0}: (10, {})} | custom-call | bytes 56000000 | tf_op jit(solution)/shard_map/last1/pallas_call | solution.py:37
  150.7 0.2 fusion.3
  150.9 25.0 %all_to_all.11 = f32[128,2,32]{2,1,0:T(2,128)S(1)} all-to-all(f32[128,2,32]{2,1,0:T(2,128)S(1)} %bitcast.31), channel_id=1, replica_groups=mesh['gx_0'=4,'gx_1'=4,'gx_2'=2,'gy'=4] {'gx_0','gx_1','gx_2','gy'}, dimensions={0} | all-to-all | bytes 65536 | tf_op jit(solution)/shard_map/all_to_all | solution.py:407
  175.9 0.4 fusion
  176.3 0.2 fusion.11
  176.5 0.1 broadcast_in_dim.4
  176.6 0.1 broadcast_in_dim.5
  176.7 14.1 %all_to_all.12 = f32[128,1,256]{2,1,0:T(1,128)S(1)} all-to-all(f32[128,1,256]{2,1,0:T(1,128)S(1)} %broadcast_in_dim.5), channel_id=1, replica_groups=mesh['gx_0'=4,'gx_1'=4,'gx_2'=2,'gy'=4] {'gx_0','gx_1','gx_2','gy'}, dimensions={0} | all-to-all | bytes 262144 | tf_op jit(solution)/shard_map/all_to_all | solution.py:414
  190.8 0.2 reduce_sum.19
  190.9 0.7 reshape.61
  (22 shorter events, 0.1 us)
Async XLA Ops:
  5.7 33.4 %collective-permute-start.3 = (f32[4,36,8,256]{3,2,1,0:T(8,128)S(1)}, f32[4,36,8,256]{3,2,1,0:T(8,128)S(1)}, u32[]{:S(2)}, u32[]{:S(2)}) collective-permute-start(f32[4,36,8,256]{3,2,1,0:T(8,128)S(1)} %get-tuple-element.82), channel_id=1, source_target_pairs={{4,8},{12,16},{20,24},{28,32},{36,40},{44,48},{52,56},{60,64},{68,... | collective-permute-start | bytes 3538952 | tf_op jit(solution)/shard_map/ppermute | solution.py:454
  10.2 28.9 %collective-permute-start.4 = (f32[16,5,8,256]{3,2,1,0:T(8,128)S(1)}, f32[16,5,8,256]{3,2,1,0:T(8,128)S(1)}, u32[]{:S(2)}, u32[]{:S(2)}) collective-permute-start(f32[16,5,8,256]{3,2,1,0:T(8,128)S(1)} %get-tuple-element.83), channel_id=1, source_target_pairs={{0,1},{2,3},{1,0},{3,2},{4,5},{6,7},{5,4},{7,6},{8,9},{10,11},{9,8... | collective-permute-start | bytes 1966088 | tf_op jit(solution)/shard_map/ppermute | solution.py:455
  11.9 27.2 %collective-permute-start.5 = (f32[16,5,8,256]{3,2,1,0:T(8,128)S(1)}, f32[16,5,8,256]{3,2,1,0:T(8,128)S(1)}, u32[]{:S(2)}, u32[]{:S(2)}) collective-permute-start(f32[16,5,8,256]{3,2,1,0:T(8,128)S(1)} %get-tuple-element.84), channel_id=1, source_target_pairs={{1,2},{2,1},{5,6},{6,5},{9,10},{10,9},{13,14},{14,13},{17,18},{18,... | collective-permute-start | bytes 1966088 | tf_op jit(solution)/shard_map/ppermute | solution.py:456
  12.6 14.6 %collective-permute-start.6 = (f32[4,5,8,256]{3,2,1,0:T(8,128)S(1)}, f32[4,5,8,256]{3,2,1,0:T(8,128)S(1)}, u32[]{:S(2)}, u32[]{:S(2)}) collective-permute-start(f32[4,5,8,256]{3,2,1,0:T(8,128)S(1)} %get-tuple-element.85), channel_id=1, source_target_pairs={{4,9},{6,11},{5,8},{7,10},{12,17},{14,19},{13,16},{15,18},{20,25},... | collective-permute-start | bytes 491528 | tf_op jit(solution)/shard_map/ppermute | solution.py:457
  19.0 20.1 %copy-start = (f32[16,32,256]{2,1,0:T(8,128)S(1)}, f32[16,32,256]{2,1,0:T(8,128)}, u32[]{:S(2)}) copy-start(f32[16,32,256]{2,1,0:T(8,128)} %param.8) | copy-start | bytes 1572868
  19.0 8.2 %collective-permute-start.7 = (f32[4,5,8,256]{3,2,1,0:T(8,128)S(1)}, f32[4,5,8,256]{3,2,1,0:T(8,128)S(1)}, u32[]{:S(2)}, u32[]{:S(2)}) collective-permute-start(f32[4,5,8,256]{3,2,1,0:T(8,128)S(1)} %get-tuple-element.86), channel_id=1, source_target_pairs={{5,10},{6,9},{13,18},{14,17},{21,26},{22,25},{29,34},{30,33},{37,4... | collective-permute-start | bytes 491528 | tf_op jit(solution)/shard_map/ppermute | solution.py:458
  27.2 11.9 %collective-permute-start.8 = (f32[4,4,8,256]{3,2,1,0:T(8,128)S(1)}, f32[4,4,8,256]{3,2,1,0:T(8,128)S(1)}, u32[]{:S(2)}, u32[]{:S(2)}) collective-permute-start(f32[4,4,8,256]{3,2,1,0:T(8,128)S(1)} %get-tuple-element.90), channel_id=1, source_target_pairs={{4,9},{6,11},{5,8},{7,10},{12,17},{14,19},{13,16},{15,18},{20,25},... | collective-permute-start | bytes 393224 | tf_op jit(solution)/shard_map/ppermute | solution.py:457
  36.5 2.6 %collective-permute-start.9 = (f32[4,4,8,256]{3,2,1,0:T(8,128)S(1)}, f32[4,4,8,256]{3,2,1,0:T(8,128)S(1)}, u32[]{:S(2)}, u32[]{:S(2)}) collective-permute-start(f32[4,4,8,256]{3,2,1,0:T(8,128)S(1)} %get-tuple-element.91), channel_id=1, source_target_pairs={{5,10},{6,9},{13,18},{14,17},{21,26},{22,25},{29,34},{30,33},{37,4... | collective-permute-start | bytes 393224 | tf_op jit(solution)/shard_map/ppermute | solution.py:458
  39.1 9.8 %copy-start.2 = (f32[3]{0:T(128)S(1)}, f32[3]{0:T(128)}, u32[]{:S(2)}) copy-start(f32[3]{0:T(128)} %wind.1) | copy-start | bytes 40
  40.0 8.9 %collective-permute-start.10 = (f32[4,46,8,256]{3,2,1,0:T(8,128)S(1)}, f32[4,46,8,256]{3,2,1,0:T(8,128)S(1)}, u32[]{:S(2)}, u32[]{:S(2)}) collective-permute-start(f32[4,46,8,256]{3,2,1,0:T(8,128)S(1)} %inner.4), channel_id=1, source_target_pairs={{0,4},{8,12},{16,20},{24,28},{32,36},{40,44},{48,52},{56,60},{64,6... | collective-permute-start | bytes 4521992 | tf_op jit(solution)/shard_map/ppermute | solution.py:477
  40.1 26.9 %collective-permute-start = (f32[4,32,8,256]{3,2,1,0:T(8,128)S(1)}, f32[4,32,8,256]{3,2,1,0:T(8,128)S(1)}, u32[]{:S(2)}, u32[]{:S(2)}) collective-permute-start(f32[4,32,8,256]{3,2,1,0:T(8,128)S(1)} %get-tuple-element.79), channel_id=1, source_target_pairs={{4,8},{12,16},{20,24},{28,32},{36,40},{44,48},{52,56},{60,64},{68,... | collective-permute-start | bytes 3145736 | tf_op jit(solution)/shard_map/ppermute | solution.py:454
  43.7 23.3 %collective-permute-start.1 = (f32[16,4,8,256]{3,2,1,0:T(8,128)S(1)}, f32[16,4,8,256]{3,2,1,0:T(8,128)S(1)}, u32[]{:S(2)}, u32[]{:S(2)}) collective-permute-start(f32[16,4,8,256]{3,2,1,0:T(8,128)S(1)} %get-tuple-element.80), channel_id=1, source_target_pairs={{0,1},{2,3},{1,0},{3,2},{4,5},{6,7},{5,4},{7,6},{8,9},{10,11},{9,8... | collective-permute-start | bytes 1572872 | tf_op jit(solution)/shard_map/ppermute | solution.py:455
  48.2 18.8 %collective-permute-start.2 = (f32[16,4,8,256]{3,2,1,0:T(8,128)S(1)}, f32[16,4,8,256]{3,2,1,0:T(8,128)S(1)}, u32[]{:S(2)}, u32[]{:S(2)}) collective-permute-start(f32[16,4,8,256]{3,2,1,0:T(8,128)S(1)} %get-tuple-element.81), channel_id=1, source_target_pairs={{1,2},{2,1},{5,6},{6,5},{9,10},{10,9},{13,14},{14,13},{17,18},{18,... | collective-permute-start | bytes 1572872 | tf_op jit(solution)/shard_map/ppermute | solution.py:456
  67.8 10.4 %collective-permute-start.16 = (f32[4,40,8,256]{3,2,1,0:T(8,128)S(1)}, f32[4,40,8,256]{3,2,1,0:T(8,128)S(1)}, u32[]{:S(2)}, u32[]{:S(2)}) collective-permute-start(f32[4,40,8,256]{3,2,1,0:T(8,128)S(1)} %inner.5), channel_id=1, source_target_pairs={{0,4},{8,12},{16,20},{24,28},{32,36},{40,44},{48,52},{56,60},{64,6... | collective-permute-start | bytes 3932168 | tf_op jit(solution)/shard_map/ppermute | solution.py:477
  67.9 26.2 %collective-permute-start.11 = (f32[4,32,8,256]{3,2,1,0:T(8,128)S(1)}, f32[4,32,8,256]{3,2,1,0:T(8,128)S(1)}, u32[]{:S(2)}, u32[]{:S(2)}) collective-permute-start(f32[4,32,8,256]{3,2,1,0:T(8,128)S(1)} %get-tuple-element.114), channel_id=1, source_target_pairs={{4,8},{12,16},{20,24},{28,32},{36,40},{44,48},{52,56},{60,64},{68,... | collective-permute-start | bytes 3145736 | tf_op jit(solution)/shard_map/ppermute | solution.py:454
  71.6 22.5 %collective-permute-start.12 = (f32[16,4,8,256]{3,2,1,0:T(8,128)S(1)}, f32[16,4,8,256]{3,2,1,0:T(8,128)S(1)}, u32[]{:S(2)}, u32[]{:S(2)}) collective-permute-start(f32[16,4,8,256]{3,2,1,0:T(8,128)S(1)} %get-tuple-element.115), channel_id=1, source_target_pairs={{0,1},{2,3},{1,0},{3,2},{4,5},{6,7},{5,4},{7,6},{8,9},{10,11},{9,8... | collective-permute-start | bytes 1572872 | tf_op jit(solution)/shard_map/ppermute | solution.py:455
  72.9 21.2 %collective-permute-start.13 = (f32[16,4,8,256]{3,2,1,0:T(8,128)S(1)}, f32[16,4,8,256]{3,2,1,0:T(8,128)S(1)}, u32[]{:S(2)}, u32[]{:S(2)}) collective-permute-start(f32[16,4,8,256]{3,2,1,0:T(8,128)S(1)} %get-tuple-element.116), channel_id=1, source_target_pairs={{1,2},{2,1},{5,6},{6,5},{9,10},{10,9},{13,14},{14,13},{17,18},{18,... | collective-permute-start | bytes 1572872 | tf_op jit(solution)/shard_map/ppermute | solution.py:456
  73.6 20.5 %collective-permute-start.14 = (f32[4,4,8,256]{3,2,1,0:T(8,128)S(1)}, f32[4,4,8,256]{3,2,1,0:T(8,128)S(1)}, u32[]{:S(2)}, u32[]{:S(2)}) collective-permute-start(f32[4,4,8,256]{3,2,1,0:T(8,128)S(1)} %get-tuple-element.117), channel_id=1, source_target_pairs={{4,9},{6,11},{5,8},{7,10},{12,17},{14,19},{13,16},{15,18},{20,25},... | collective-permute-start | bytes 393224 | tf_op jit(solution)/shard_map/ppermute | solution.py:457
  78.2 15.8 %collective-permute-start.15 = (f32[4,4,8,256]{3,2,1,0:T(8,128)S(1)}, f32[4,4,8,256]{3,2,1,0:T(8,128)S(1)}, u32[]{:S(2)}, u32[]{:S(2)}) collective-permute-start(f32[4,4,8,256]{3,2,1,0:T(8,128)S(1)} %get-tuple-element.118), channel_id=1, source_target_pairs={{5,10},{6,9},{13,18},{14,17},{21,26},{22,25},{29,34},{30,33},{37,4... | collective-permute-start | bytes 393224 | tf_op jit(solution)/shard_map/ppermute | solution.py:458
  94.1 12.8 %copy-start.1 = (s32[1,1,128]{2,1,0:T(1,128)S(1)}, s32[1,1,128]{2,1,0:T(1,128)}, u32[]{:S(2)}) copy-start(s32[1,1,128]{2,1,0:T(1,128)} %param.10) | copy-start | bytes 1540
  94.9 11.1 %collective-permute-start.22 = (f32[4,40,8,256]{3,2,1,0:T(8,128)S(1)}, f32[4,40,8,256]{3,2,1,0:T(8,128)S(1)}, u32[]{:S(2)}, u32[]{:S(2)}) collective-permute-start(f32[4,40,8,256]{3,2,1,0:T(8,128)S(1)} %inner.6), channel_id=1, source_target_pairs={{0,4},{8,12},{16,20},{24,28},{32,36},{40,44},{48,52},{56,60},{64,6... | collective-permute-start | bytes 3932168 | tf_op jit(solution)/shard_map/ppermute | solution.py:477
  95.0 31.9 %collective-permute-start.17 = (f32[4,32,8,256]{3,2,1,0:T(8,128)S(1)}, f32[4,32,8,256]{3,2,1,0:T(8,128)S(1)}, u32[]{:S(2)}, u32[]{:S(2)}) collective-permute-start(f32[4,32,8,256]{3,2,1,0:T(8,128)S(1)} %get-tuple-element.137), channel_id=1, source_target_pairs={{4,8},{12,16},{20,24},{28,32},{36,40},{44,48},{52,56},{60,64},{68,... | collective-permute-start | bytes 3145736 | tf_op jit(solution)/shard_map/ppermute | solution.py:454
  98.6 28.2 %collective-permute-start.18 = (f32[16,4,8,256]{3,2,1,0:T(8,128)S(1)}, f32[16,4,8,256]{3,2,1,0:T(8,128)S(1)}, u32[]{:S(2)}, u32[]{:S(2)}) collective-permute-start(f32[16,4,8,256]{3,2,1,0:T(8,128)S(1)} %get-tuple-element.138), channel_id=1, source_target_pairs={{0,1},{2,3},{1,0},{3,2},{4,5},{6,7},{5,4},{7,6},{8,9},{10,11},{9,8... | collective-permute-start | bytes 1572872 | tf_op jit(solution)/shard_map/ppermute | solution.py:455
  100.9 25.9 %collective-permute-start.19 = (f32[16,4,8,256]{3,2,1,0:T(8,128)S(1)}, f32[16,4,8,256]{3,2,1,0:T(8,128)S(1)}, u32[]{:S(2)}, u32[]{:S(2)}) collective-permute-start(f32[16,4,8,256]{3,2,1,0:T(8,128)S(1)} %get-tuple-element.139), channel_id=1, source_target_pairs={{1,2},{2,1},{5,6},{6,5},{9,10},{10,9},{13,14},{14,13},{17,18},{18,... | collective-permute-start | bytes 1572872 | tf_op jit(solution)/shard_map/ppermute | solution.py:456
  101.6 25.2 %collective-permute-start.20 = (f32[4,4,8,256]{3,2,1,0:T(8,128)S(1)}, f32[4,4,8,256]{3,2,1,0:T(8,128)S(1)}, u32[]{:S(2)}, u32[]{:S(2)}) collective-permute-start(f32[4,4,8,256]{3,2,1,0:T(8,128)S(1)} %get-tuple-element.140), channel_id=1, source_target_pairs={{4,9},{6,11},{5,8},{7,10},{12,17},{14,19},{13,16},{15,18},{20,25},... | collective-permute-start | bytes 393224 | tf_op jit(solution)/shard_map/ppermute | solution.py:457
  106.0 20.8 %collective-permute-start.21 = (f32[4,4,8,256]{3,2,1,0:T(8,128)S(1)}, f32[4,4,8,256]{3,2,1,0:T(8,128)S(1)}, u32[]{:S(2)}, u32[]{:S(2)}) collective-permute-start(f32[4,4,8,256]{3,2,1,0:T(8,128)S(1)} %get-tuple-element.141), channel_id=1, source_target_pairs={{5,10},{6,9},{13,18},{14,17},{21,26},{22,25},{29,34},{30,33},{37,4... | collective-permute-start | bytes 393224 | tf_op jit(solution)/shard_map/ppermute | solution.py:458
  126.8 1.5 copy-start.5
  127.6 3.1 %collective-permute-start.23 = (f32[4,40,8,256]{3,2,1,0:T(8,128)S(1)}, f32[4,40,8,256]{3,2,1,0:T(8,128)S(1)}, u32[]{:S(2)}, u32[]{:S(2)}) collective-permute-start(f32[4,40,8,256]{3,2,1,0:T(8,128)S(1)} %inner.7), channel_id=1, source_target_pairs={{0,4},{8,12},{16,20},{24,28},{32,36},{40,44},{48,52},{56,60},{64,6... | collective-permute-start | bytes 3932168 | tf_op jit(solution)/shard_map/ppermute | solution.py:477
  128.6 22.1 %copy-start.4 = (f32[1,1,128,16]{2,3,1,0:T(8,128)S(1)}, f32[1,1,128,16]{2,3,1,0:T(8,128)}, u32[]{:S(2)}) copy-start(f32[1,1,128,16]{2,3,1,0:T(8,128)} %param.13) | copy-start | bytes 24580
  176.3 15.3 %copy-start.3 = (f32[16,16]{1,0:T(8,128)}, f32[16,16]{1,0:T(8,128)S(1)}, u32[]{:S(2)}) copy-start(f32[16,16]{1,0:T(8,128)S(1)} %fusion) | copy-start | bytes 3076

commit v4 on v3

--- a/solution.py
+++ b/solution.py
@@ -449,14 +449,14 @@
     def across(pairs_x, pairs_y):
         return [(i * peers_y + k, j * peers_y + n) for i, j in pairs_x for k, n in pairs_y]
 
+    def sides(b, c, d):
+        return [lax.ppermute(b, GX, outer), lax.ppermute(c, "gy", first), lax.ppermute(d, "gy", second)]
+
+    def diagonals(f, h):
+        return [lax.ppermute(f, ALL, across(outer, first)), lax.ppermute(h, ALL, across(outer, second))]
+
     def exchange(b, c, d, f, h):
-        return [
-            lax.ppermute(b, GX, outer),
-            lax.ppermute(c, "gy", first),
-            lax.ppermute(d, "gy", second),
-            lax.ppermute(f, ALL, across(outer, first)),
-            lax.ppermute(h, ALL, across(outer, second)),
-        ]
+        return sides(b, c, d) + diagonals(f, h)
 
     def after(*values):
         return list(lax.optimization_barrier(values))
@@ -465,10 +465,11 @@
     a_own = diffusivity.reshape(NX, TILES, 8, NZ)
     cells = sensor_cell.reshape(-1)
     made = [pack(0, place, probes, a_own), pack(1, place, probes, a_own)]
-    arrived = exchange(*made[0][1:])
-    queued = exchange(*made[1][1:4], *after(*made[1][4:], *arrived[3:])[:2])
-    joined = after(*arrived, *made[1], *queued[3:])
-    arrived, made[1], queued[3:] = joined[:5], joined[5:11], joined[11:]
+    corner_pairs = zip(made[0][4:], made[1][4:])
+    cornered = diagonals(*[jnp.concatenate(pair, axis=1) for pair in corner_pairs])
+    arrived = sides(*made[0][1:4]) + cornered
+    joined = after(*arrived, *made[1])
+    arrived, made[1] = joined[:5], joined[5:]
     coef = fields = None
     readings = []
     for turn in range(4):
@@ -476,7 +477,7 @@
         a = inner_planes(place, field, *arrived[1:3], *([a_own] if turn == 0 else []))
         state = [field, lax.ppermute(a, GX, inner), *arrived]
         if turn == 0:
-            arrived = queued
+            arrived = sides(*after(*made[1][1:4], a)[:3]) + [x[:, H + 1 :] for x in arrived[3:]]
         elif turn < 3:
             leaving = after(*made[turn + 1][1:], a)[:5]
             arrived = exchange(*leaving)

time: 192 us -> 187 us (0.974)
  starting transfers between devices: 56 us -> 51.2 us
    ppermute x20 -> x18, starting transfers between devices: 55.7 us -> 50.9 us  [the longest x4 18.9 us: sides(): lax.ppermute(b, GX, outer)]
    ppermute x20 -> x18, waiting for transfers between devices: 4.55 us -> 4.06 us  [the longest x3 4.02 us: diagonals(): lax.ppermute(f, ALL, across(outer, first))]
  transfers between devices with their start and end apart: 24 -> 22, of which waited for: 3 -> 2; matrix products, arithmetic and copies ran while one was open for 0% -> 0% of each run, Pallas kernels for 30% -> 31%
where the time goes in v4:
time: 187 us; the launch traced here: 186 us
  Pallas kernels  85.8 us (46%)
  starting transfers between devices  51.2 us (27%)
  blocking collectives  39.2 us (21%)
  waiting for transfers between devices  6.22 us (3%)
  between operations  1.87 us (1%)
    pallas_call x11, Pallas kernels, kernel(): pl.pallas_call(body, in_specs=in_specs, out_specs=[spec for _, spec in ou...  85.8 us
    all_to_all x1, blocking collectives, readings_exchange(): lax.all_to_all(outgoing, ALL, split_axis=0, concat_axis=0, tiled=True)  25.1 us
    ppermute x4, starting transfers between devices, sides(): lax.ppermute(b, GX, outer)  18.9 us
    ppermute x3, starting transfers between devices, diagonals(): lax.ppermute(f, ALL, across(outer, first))  15.2 us
    all_to_all x1, blocking collectives, readings_exchange(): terms = lax.all_to_all(terms, ALL, split_axis=0, concat_axis=0, tiled=True)  14.1 us
    ppermute x4, starting transfers between devices, sides(): lax.ppermute(c, 'gy', first)  11.9 us
    ppermute x3, waiting for transfers between devices, diagonals(): lax.ppermute(f, ALL, across(outer, first))  4.02 us
  transfers between devices with their start and end apart: 22, of which 2 were waited for; matrix products, arithmetic and copies ran while one was open for 0% of the time, Pallas kernels for 31%

profile of v4, /device:TPU:1, one launch (start us, length us, event | category | flops | bytes accessed | tf_op | source)
XLA Modules:
  0.0 186.5 jit_solution(8407949516956096366)
XLA Ops:
  0.7 0.1 stack.51.place
  0.8 4.9 %pack0.1 = (f32[16,32,8,256]{3,2,1,0:T(8,128)S(1)}, f32[4,36,8,256]{3,2,1,0:T(8,128)S(1)}, f32[16,5,8,256]{3,2,1,0:T(8,128)S(1)}, f32[16,5,8,256]{3,2,1,0:T(8,12...) custom-call(s32[14]{0:T(128)S(1)} %stack.51.place, f32[16,16,32,256]{3,2,1,0:T(8,128)} %probes.3, ...), custom_call_target="tpu_custom_call" | custom-call | bytes 21000000 | tf_op jit(solution)/shard_map/pack0/pallas_call | solution.py:37
  5.7 4.5 %collective-permute-start = (f32[4,36,8,256]{3,2,1,0:T(8,128)S(1)}, f32[4,36,8,256]{3,2,1,0:T(8,128)S(1)}, u32[]{:S(2)}, u32[]{:S(2)}) collective-permute-start(f32[4,36,8,256]{3,2,1,0:T(8,128)S(1)} %get-tuple-element.81), channel_id=1, source_target_pairs={{4,8},{12,16},{20,24},{28,32},{36,40},{44,48},{52,56},{60,64},{68,... | collective-permute-start | bytes 3538952 | tf_op jit(solution)/shard_map/ppermute | solution.py:453
  10.2 1.7 collective-permute-start.1
  11.9 0.7 collective-permute-start.2
  12.6 4.8 %pack1.1 = (f32[16,32,8,256]{3,2,1,0:T(8,128)S(1)}, f32[4,32,8,256]{3,2,1,0:T(8,128)S(1)}, f32[16,4,8,256]{3,2,1,0:T(8,128)S(1)}, f32[16,4,8,256]{3,2,1,0:T(8,12...) custom-call(s32[14]{0:T(128)S(1)} %stack.51.place, f32[16,16,32,256]{3,2,1,0:T(8,128)} %probes.3), custom_call_target="tpu_custom_call" | custom-call | bytes 21000000 | tf_op jit(solution)/shard_map/pack1/pallas_call | solution.py:37
  17.4 0.0 copy-start
  17.5 6.5 %collective-permute-start.3 = (f32[4,9,8,256]{3,2,1,0:T(8,128)S(1)}, f32[4,9,8,256]{3,2,1,0:T(8,128)S(1)}, u32[]{:S(2)}, u32[]{:S(2)}) collective-permute-start(f32[4,9,8,256]{3,2,1,0:T(8,128)S(1)} %pad_maximum_fusion), channel_id=1, source_target_pairs={{4,9},{6,11},{5,8},{7,10},{12,17},{14,19},{13,16},{15,18},{20,25},... | collective-permute-start | bytes 884744 | tf_op jit(solution)/shard_map/ppermute | solution.py:456
  24.0 0.7 collective-permute-start.4
  24.7 4.0 %collective-permute-done.3.f_in.refs_5_ = f32[4,9,8,256]{3,2,1,0:T(8,128)S(1)} collective-permute-done((f32[4,9,8,256]{3,2,1,0:T(8,128)S(1)}, f32[4,9,8,256]{3,2,1,0:T(8,128)S(1)}, u32[]{:S(2)}, u32[]{:S(2)}) %collective-permute-start.3) | collective-permute-done | bytes 294944 | tf_op jit(solution)/shard_map/ppermute | solution.py:456
  28.7 0.0 collective-permute-done.4.h_in.refs_6_
  28.7 0.0 collective-permute-done.1.c_in.refs_3_
  28.7 0.0 collective-permute-done.2.d_in.refs_4_
  28.7 0.0 collective-permute-done.b_in.refs_2_
  28.7 0.0 copy-start.2
  28.7 0.8 inner.4
  29.6 0.1 collective-permute-start.8
  29.7 7.2 %collective-permute-start.5 = (f32[4,32,8,256]{3,2,1,0:T(8,128)S(1)}, f32[4,32,8,256]{3,2,1,0:T(8,128)S(1)}, u32[]{:S(2)}, u32[]{:S(2)}) collective-permute-start(f32[4,32,8,256]{3,2,1,0:T(8,128)S(1)} %get-tuple-element.98), channel_id=1, source_target_pairs={{4,8},{12,16},{20,24},{28,32},{36,40},{44,48},{52,56},{60,64},{68,... | collective-permute-start | bytes 3145736 | tf_op jit(solution)/shard_map/ppermute | solution.py:453
  36.9 6.4 %collective-permute-start.6 = (f32[16,4,8,256]{3,2,1,0:T(8,128)S(1)}, f32[16,4,8,256]{3,2,1,0:T(8,128)S(1)}, u32[]{:S(2)}, u32[]{:S(2)}) collective-permute-start(f32[16,4,8,256]{3,2,1,0:T(8,128)S(1)} %get-tuple-element.99), channel_id=1, source_target_pairs={{0,1},{2,3},{1,0},{3,2},{4,5},{6,7},{5,4},{7,6},{8,9},{10,11},{9,8... | collective-permute-start | bytes 1572872 | tf_op jit(solution)/shard_map/ppermute | solution.py:453
  43.3 0.7 collective-permute-start.7
  44.1 0.0 collective-permute-done.8.a_in.refs_1_
  44.1 2.9 %coefficients.1.refs_7_.rest_7_ = f32[5,24,48,256]{3,2,1,0:T(8,128)S(1)} custom-call(s32[14]{0:T(128)S(1)} %stack.51.place, f32[3]{0:T(128)S(1)} %copy-done.2, f32[16,4,8,256]{3,2,1,0:T(8,128)S(1)} %bitcast.27, f32[4,46,8,256]{3,2,1,0:T(8,128)S(1)} %collective-permute-done.8.a_in.refs_1_, f32[4,36,8,256]{3,2,1,0:T(8,128)S(1)} %collective-permute-done.b_in.refs_2_, ...), custom_call_target="tpu_custom_call" | custom-call | bytes 10500000 | tf_op jit(solution)/shard_map/coefficients/pallas_call | solution.py:37
  47.0 15.1 %step0.1 = (f32[16,32,8,256]{3,2,1,0:T(8,128)S(1)}, f32[4,32,8,256]{3,2,1,0:T(8,128)S(1)}, f32[16,4,8,256]{3,2,1,0:T(8,128)S(1)}, f32[16,4,8,256]{3,2,1,0:T(8,12...) custom-call(s32[14]{0:T(128)S(1)} %stack.51.place, ...), custom_call_target="tpu_custom_call" | custom-call | bytes 42000000 | tf_op jit(solution)/shard_map/step0/pallas_call | solution.py:37
  62.1 0.0 collective-permute-done.6.c_in.refs_3_
  62.2 0.0 collective-permute-done.5.refs_2_
  62.2 0.8 inner.5
  62.9 0.1 collective-permute-start.14
  63.0 3.6 %collective-permute-start.9 = (f32[4,32,8,256]{3,2,1,0:T(8,128)S(1)}, f32[4,32,8,256]{3,2,1,0:T(8,128)S(1)}, u32[]{:S(2)}, u32[]{:S(2)}) collective-permute-start(f32[4,32,8,256]{3,2,1,0:T(8,128)S(1)} %get-tuple-element.118), channel_id=1, source_target_pairs={{4,8},{12,16},{20,24},{28,32},{36,40},{44,48},{52,56},{60,64},{68,... | collective-permute-start | bytes 3145736 | tf_op jit(solution)/shard_map/ppermute | solution.py:453
  66.6 1.8 collective-permute-start.10
  68.5 0.7 collective-permute-start.11
  69.2 4.1 %collective-permute-start.12 = (f32[4,4,8,256]{3,2,1,0:T(8,128)S(1)}, f32[4,4,8,256]{3,2,1,0:T(8,128)S(1)}, u32[]{:S(2)}, u32[]{:S(2)}) collective-permute-start(f32[4,4,8,256]{3,2,1,0:T(8,128)S(1)} %get-tuple-element.121), channel_id=1, source_target_pairs={{4,9},{6,11},{5,8},{7,10},{12,17},{14,19},{13,16},{15,18},{20,25},... | collective-permute-start | bytes 393224 | tf_op jit(solution)/shard_map/ppermute | solution.py:456
  73.3 0.7 collective-permute-start.13
  74.0 15.1 %step1.1 = (f32[16,32,8,256]{3,2,1,0:T(8,128)S(1)}, f32[4,32,8,256]{3,2,1,0:T(8,128)S(1)}, f32[16,4,8,256]{3,2,1,0:T(8,128)S(1)}, f32[16,4,8,256]{3,2,1,0:T(8,12...) custom-call(s32[14]{0:T(128)S(1)} %stack.51.place, ...), custom_call_target="tpu_custom_call" | custom-call | bytes 42000000 | tf_op jit(solution)/shard_map/step1/pallas_call | solution.py:37
  89.1 0.0 collective-permute-done.12.rest_5_
  89.2 0.0 collective-permute-done.11.d_in.rest_4_
  89.2 0.0 copy-start.1
  89.2 0.8 inner.6
  90.0 0.1 collective-permute-start.20
  90.1 3.6 %collective-permute-start.15 = (f32[4,32,8,256]{3,2,1,0:T(8,128)S(1)}, f32[4,32,8,256]{3,2,1,0:T(8,128)S(1)}, u32[]{:S(2)}, u32[]{:S(2)}) collective-permute-start(f32[4,32,8,256]{3,2,1,0:T(8,128)S(1)} %get-tuple-element.141), channel_id=1, source_target_pairs={{4,8},{12,16},{20,24},{28,32},{36,40},{44,48},{52,56},{60,64},{68,... | collective-permute-start | bytes 3145736 | tf_op jit(solution)/shard_map/ppermute | solution.py:453
  93.7 1.9 collective-permute-start.16
  95.5 0.7 collective-permute-start.17
  96.2 4.5 %collective-permute-start.18 = (f32[4,4,8,256]{3,2,1,0:T(8,128)S(1)}, f32[4,4,8,256]{3,2,1,0:T(8,128)S(1)}, u32[]{:S(2)}, u32[]{:S(2)}) collective-permute-start(f32[4,4,8,256]{3,2,1,0:T(8,128)S(1)} %get-tuple-element.144), channel_id=1, source_target_pairs={{4,9},{6,11},{5,8},{7,10},{12,17},{14,19},{13,16},{15,18},{20,25},... | collective-permute-start | bytes 393224 | tf_op jit(solution)/shard_map/ppermute | solution.py:456
  100.8 0.8 collective-permute-start.19
  101.7 19.9 %last0.1 = (f32[16,16,32,256]{3,2,1,0:T(8,128)}, f32[8,128]{1,0:T(8,128)S(1)}) custom-call(s32[14]{0:T(128)S(1)} %stack.51.place, s32[128]{0:T(128)S(1)} %bitcast.28, f32[16,32,8,256]{3,2,1,0:T(8,128)S(1)} %get-tuple-element.138.field.rest_0_, f32[4,40,8,256]{3,2,1,0:T(8,128)S(1)} %collective-permute-done.20.rest_1_, ...), custom_call_target="tpu_custom_call" | custom-call | bytes 56000000 | tf_op jit(solution)/shard_map/last0/pallas_call | solution.py:37
  121.6 0.0 collective-permute-done.18.rest_5_
  121.6 0.0 collective-permute-done.19.rest_6_
  121.6 0.0 collective-permute-done.17.d_in.rest_4_
  121.6 0.0 collective-permute-done.15.rest_2_
  121.6 0.0 copy-start.5
  121.6 0.8 inner.7
  122.4 0.1 collective-permute-start.21
  123.2 0.2 convert_reduce_fusion
  123.4 0.0 copy-start.4
  123.4 2.2 %collective-permute-done.21.rest_1_ = f32[4,40,8,256]{3,2,1,0:T(8,128)S(1)} collective-permute-done((f32[4,40,8,256]{3,2,1,0:T(8,128)S(1)}, f32[4,40,8,256]{3,2,1,0:T(8,128)S(1)}, u32[]{:S(2)}, u32[]{:S(2)}) %collective-permute-start.21) | collective-permute-done | bytes 1310752 | tf_op jit(solution)/shard_map/ppermute | solution.py:478
  125.5 19.9 %last1.1 = (f32[16,16,32,256]{3,2,1,0:T(8,128)}, f32[8,128]{1,0:T(8,128)S(1)}) custom-call(s32[14]{0:T(128)S(1)} %stack.51.place, s32[128]{0:T(128)S(1)} %bitcast.29, f32[16,32,8,256]{3,2,1,0:T(8,128)S(1)} %get-tuple-element.132.field.rest_0_, f32[4,40,8,256]{3,2,1,0:T(8,128)S(1)} %collective-permute-done.21.rest_1_, ...), custom_call_target="tpu_custom_call", output_to_operand_aliasing={{0}: (10, {})} | custom-call | bytes 56000000 | tf_op jit(solution)/shard_map/last1/pallas_call | solution.py:37
  145.5 0.2 fusion.3
  145.7 25.1 %all_to_all.11 = f32[128,2,32]{2,1,0:T(2,128)S(1)} all-to-all(f32[128,2,32]{2,1,0:T(2,128)S(1)} %bitcast.31), channel_id=1, replica_groups=mesh['gx_0'=4,'gx_1'=4,'gx_2'=2,'gy'=4] {'gx_0','gx_1','gx_2','gy'}, dimensions={0} | all-to-all | bytes 65536 | tf_op jit(solution)/shard_map/all_to_all | solution.py:407
  170.7 0.4 fusion
  171.2 0.2 fusion.11
  171.4 0.1 broadcast_in_dim.4
  171.5 0.1 broadcast_in_dim.5
  171.6 14.1 %all_to_all.12 = f32[128,1,256]{2,1,0:T(1,128)S(1)} all-to-all(f32[128,1,256]{2,1,0:T(1,128)S(1)} %broadcast_in_dim.5), channel_id=1, replica_groups=mesh['gx_0'=4,'gx_1'=4,'gx_2'=2,'gy'=4] {'gx_0','gx_1','gx_2','gy'}, dimensions={0} | all-to-all | bytes 262144 | tf_op jit(solution)/shard_map/all_to_all | solution.py:414
  185.6 0.2 reduce_sum.19
  185.8 0.7 reshape.61
  (22 shorter events, 0.1 us)
Async XLA Ops:
  5.7 23.0 %collective-permute-start = (f32[4,36,8,256]{3,2,1,0:T(8,128)S(1)}, f32[4,36,8,256]{3,2,1,0:T(8,128)S(1)}, u32[]{:S(2)}, u32[]{:S(2)}) collective-permute-start(f32[4,36,8,256]{3,2,1,0:T(8,128)S(1)} %get-tuple-element.81), channel_id=1, source_target_pairs={{4,8},{12,16},{20,24},{28,32},{36,40},{44,48},{52,56},{60,64},{68,... | collective-permute-start | bytes 3538952 | tf_op jit(solution)/shard_map/ppermute | solution.py:453
  10.2 18.5 %collective-permute-start.1 = (f32[16,5,8,256]{3,2,1,0:T(8,128)S(1)}, f32[16,5,8,256]{3,2,1,0:T(8,128)S(1)}, u32[]{:S(2)}, u32[]{:S(2)}) collective-permute-start(f32[16,5,8,256]{3,2,1,0:T(8,128)S(1)} %get-tuple-element.82), channel_id=1, source_target_pairs={{0,1},{2,3},{1,0},{3,2},{4,5},{6,7},{5,4},{7,6},{8,9},{10,11},{9,8... | collective-permute-start | bytes 1966088 | tf_op jit(solution)/shard_map/ppermute | solution.py:453
  11.9 16.8 %collective-permute-start.2 = (f32[16,5,8,256]{3,2,1,0:T(8,128)S(1)}, f32[16,5,8,256]{3,2,1,0:T(8,128)S(1)}, u32[]{:S(2)}, u32[]{:S(2)}) collective-permute-start(f32[16,5,8,256]{3,2,1,0:T(8,128)S(1)} %get-tuple-element.83), channel_id=1, source_target_pairs={{1,2},{2,1},{5,6},{6,5},{9,10},{10,9},{13,14},{14,13},{17,18},{18,... | collective-permute-start | bytes 1966088 | tf_op jit(solution)/shard_map/ppermute | solution.py:453
  17.4 11.3 %copy-start = (f32[16,32,256]{2,1,0:T(8,128)S(1)}, f32[16,32,256]{2,1,0:T(8,128)}, u32[]{:S(2)}) copy-start(f32[16,32,256]{2,1,0:T(8,128)} %param.8) | copy-start | bytes 1572868
  17.5 11.3 %collective-permute-start.3 = (f32[4,9,8,256]{3,2,1,0:T(8,128)S(1)}, f32[4,9,8,256]{3,2,1,0:T(8,128)S(1)}, u32[]{:S(2)}, u32[]{:S(2)}) collective-permute-start(f32[4,9,8,256]{3,2,1,0:T(8,128)S(1)} %pad_maximum_fusion), channel_id=1, source_target_pairs={{4,9},{6,11},{5,8},{7,10},{12,17},{14,19},{13,16},{15,18},{20,25},... | collective-permute-start | bytes 884744 | tf_op jit(solution)/shard_map/ppermute | solution.py:456
  24.0 4.7 %collective-permute-start.4 = (f32[4,9,8,256]{3,2,1,0:T(8,128)S(1)}, f32[4,9,8,256]{3,2,1,0:T(8,128)S(1)}, u32[]{:S(2)}, u32[]{:S(2)}) collective-permute-start(f32[4,9,8,256]{3,2,1,0:T(8,128)S(1)} %pad_maximum_fusion.1), channel_id=1, source_target_pairs={{5,10},{6,9},{13,18},{14,17},{21,26},{22,25},{29,34},{30,33},{37,4... | collective-permute-start | bytes 884744 | tf_op jit(solution)/shard_map/ppermute | solution.py:456
  28.7 15.3 %copy-start.2 = (f32[3]{0:T(128)S(1)}, f32[3]{0:T(128)}, u32[]{:S(2)}) copy-start(f32[3]{0:T(128)} %wind.1) | copy-start | bytes 40
  29.6 14.5 %collective-permute-start.8 = (f32[4,46,8,256]{3,2,1,0:T(8,128)S(1)}, f32[4,46,8,256]{3,2,1,0:T(8,128)S(1)}, u32[]{:S(2)}, u32[]{:S(2)}) collective-permute-start(f32[4,46,8,256]{3,2,1,0:T(8,128)S(1)} %inner.4), channel_id=1, source_target_pairs={{0,4},{8,12},{16,20},{24,28},{32,36},{40,44},{48,52},{56,60},{64,6... | collective-permute-start | bytes 4521992 | tf_op jit(solution)/shard_map/ppermute | solution.py:478
  29.7 32.5 %collective-permute-start.5 = (f32[4,32,8,256]{3,2,1,0:T(8,128)S(1)}, f32[4,32,8,256]{3,2,1,0:T(8,128)S(1)}, u32[]{:S(2)}, u32[]{:S(2)}) collective-permute-start(f32[4,32,8,256]{3,2,1,0:T(8,128)S(1)} %get-tuple-element.98), channel_id=1, source_target_pairs={{4,8},{12,16},{20,24},{28,32},{36,40},{44,48},{52,56},{60,64},{68,... | collective-permute-start | bytes 3145736 | tf_op jit(solution)/shard_map/ppermute | solution.py:453
  36.9 25.3 %collective-permute-start.6 = (f32[16,4,8,256]{3,2,1,0:T(8,128)S(1)}, f32[16,4,8,256]{3,2,1,0:T(8,128)S(1)}, u32[]{:S(2)}, u32[]{:S(2)}) collective-permute-start(f32[16,4,8,256]{3,2,1,0:T(8,128)S(1)} %get-tuple-element.99), channel_id=1, source_target_pairs={{0,1},{2,3},{1,0},{3,2},{4,5},{6,7},{5,4},{7,6},{8,9},{10,11},{9,8... | collective-permute-start | bytes 1572872 | tf_op jit(solution)/shard_map/ppermute | solution.py:453
  43.3 18.8 %collective-permute-start.7 = (f32[16,4,8,256]{3,2,1,0:T(8,128)S(1)}, f32[16,4,8,256]{3,2,1,0:T(8,128)S(1)}, u32[]{:S(2)}, u32[]{:S(2)}) collective-permute-start(f32[16,4,8,256]{3,2,1,0:T(8,128)S(1)} %get-tuple-element.100), channel_id=1, source_target_pairs={{1,2},{2,1},{5,6},{6,5},{9,10},{10,9},{13,14},{14,13},{17,18},{18,... | collective-permute-start | bytes 1572872 | tf_op jit(solution)/shard_map/ppermute | solution.py:453
  62.9 10.4 %collective-permute-start.14 = (f32[4,40,8,256]{3,2,1,0:T(8,128)S(1)}, f32[4,40,8,256]{3,2,1,0:T(8,128)S(1)}, u32[]{:S(2)}, u32[]{:S(2)}) collective-permute-start(f32[4,40,8,256]{3,2,1,0:T(8,128)S(1)} %inner.5), channel_id=1, source_target_pairs={{0,4},{8,12},{16,20},{24,28},{32,36},{40,44},{48,52},{56,60},{64,6... | collective-permute-start | bytes 3932168 | tf_op jit(solution)/shard_map/ppermute | solution.py:478
  63.0 26.2 %collective-permute-start.9 = (f32[4,32,8,256]{3,2,1,0:T(8,128)S(1)}, f32[4,32,8,256]{3,2,1,0:T(8,128)S(1)}, u32[]{:S(2)}, u32[]{:S(2)}) collective-permute-start(f32[4,32,8,256]{3,2,1,0:T(8,128)S(1)} %get-tuple-element.118), channel_id=1, source_target_pairs={{4,8},{12,16},{20,24},{28,32},{36,40},{44,48},{52,56},{60,64},{68,... | collective-permute-start | bytes 3145736 | tf_op jit(solution)/shard_map/ppermute | solution.py:453
  66.6 22.5 %collective-permute-start.10 = (f32[16,4,8,256]{3,2,1,0:T(8,128)S(1)}, f32[16,4,8,256]{3,2,1,0:T(8,128)S(1)}, u32[]{:S(2)}, u32[]{:S(2)}) collective-permute-start(f32[16,4,8,256]{3,2,1,0:T(8,128)S(1)} %get-tuple-element.119), channel_id=1, source_target_pairs={{0,1},{2,3},{1,0},{3,2},{4,5},{6,7},{5,4},{7,6},{8,9},{10,11},{9,8... | collective-permute-start | bytes 1572872 | tf_op jit(solution)/shard_map/ppermute | solution.py:453
  68.5 20.7 %collective-permute-start.11 = (f32[16,4,8,256]{3,2,1,0:T(8,128)S(1)}, f32[16,4,8,256]{3,2,1,0:T(8,128)S(1)}, u32[]{:S(2)}, u32[]{:S(2)}) collective-permute-start(f32[16,4,8,256]{3,2,1,0:T(8,128)S(1)} %get-tuple-element.120), channel_id=1, source_target_pairs={{1,2},{2,1},{5,6},{6,5},{9,10},{10,9},{13,14},{14,13},{17,18},{18,... | collective-permute-start | bytes 1572872 | tf_op jit(solution)/shard_map/ppermute | solution.py:453
  69.2 20.0 %collective-permute-start.12 = (f32[4,4,8,256]{3,2,1,0:T(8,128)S(1)}, f32[4,4,8,256]{3,2,1,0:T(8,128)S(1)}, u32[]{:S(2)}, u32[]{:S(2)}) collective-permute-start(f32[4,4,8,256]{3,2,1,0:T(8,128)S(1)} %get-tuple-element.121), channel_id=1, source_target_pairs={{4,9},{6,11},{5,8},{7,10},{12,17},{14,19},{13,16},{15,18},{20,25},... | collective-permute-start | bytes 393224 | tf_op jit(solution)/shard_map/ppermute | solution.py:456
  73.3 15.8 %collective-permute-start.13 = (f32[4,4,8,256]{3,2,1,0:T(8,128)S(1)}, f32[4,4,8,256]{3,2,1,0:T(8,128)S(1)}, u32[]{:S(2)}, u32[]{:S(2)}) collective-permute-start(f32[4,4,8,256]{3,2,1,0:T(8,128)S(1)} %get-tuple-element.122), channel_id=1, source_target_pairs={{5,10},{6,9},{13,18},{14,17},{21,26},{22,25},{29,34},{30,33},{37,4... | collective-permute-start | bytes 393224 | tf_op jit(solution)/shard_map/ppermute | solution.py:456
  89.2 12.4 %copy-start.1 = (s32[1,1,128]{2,1,0:T(1,128)S(1)}, s32[1,1,128]{2,1,0:T(1,128)}, u32[]{:S(2)}) copy-start(s32[1,1,128]{2,1,0:T(1,128)} %param.10) | copy-start | bytes 1540
  90.0 10.8 %collective-permute-start.20 = (f32[4,40,8,256]{3,2,1,0:T(8,128)S(1)}, f32[4,40,8,256]{3,2,1,0:T(8,128)S(1)}, u32[]{:S(2)}, u32[]{:S(2)}) collective-permute-start(f32[4,40,8,256]{3,2,1,0:T(8,128)S(1)} %inner.6), channel_id=1, source_target_pairs={{0,4},{8,12},{16,20},{24,28},{32,36},{40,44},{48,52},{56,60},{64,6... | collective-permute-start | bytes 3932168 | tf_op jit(solution)/shard_map/ppermute | solution.py:478
  90.1 31.5 %collective-permute-start.15 = (f32[4,32,8,256]{3,2,1,0:T(8,128)S(1)}, f32[4,32,8,256]{3,2,1,0:T(8,128)S(1)}, u32[]{:S(2)}, u32[]{:S(2)}) collective-permute-start(f32[4,32,8,256]{3,2,1,0:T(8,128)S(1)} %get-tuple-element.141), channel_id=1, source_target_pairs={{4,8},{12,16},{20,24},{28,32},{36,40},{44,48},{52,56},{60,64},{68,... | collective-permute-start | bytes 3145736 | tf_op jit(solution)/shard_map/ppermute | solution.py:453
  93.7 27.9 %collective-permute-start.16 = (f32[16,4,8,256]{3,2,1,0:T(8,128)S(1)}, f32[16,4,8,256]{3,2,1,0:T(8,128)S(1)}, u32[]{:S(2)}, u32[]{:S(2)}) collective-permute-start(f32[16,4,8,256]{3,2,1,0:T(8,128)S(1)} %get-tuple-element.142), channel_id=1, source_target_pairs={{0,1},{2,3},{1,0},{3,2},{4,5},{6,7},{5,4},{7,6},{8,9},{10,11},{9,8... | collective-permute-start | bytes 1572872 | tf_op jit(solution)/shard_map/ppermute | solution.py:453
  95.5 26.1 %collective-permute-start.17 = (f32[16,4,8,256]{3,2,1,0:T(8,128)S(1)}, f32[16,4,8,256]{3,2,1,0:T(8,128)S(1)}, u32[]{:S(2)}, u32[]{:S(2)}) collective-permute-start(f32[16,4,8,256]{3,2,1,0:T(8,128)S(1)} %get-tuple-element.143), channel_id=1, source_target_pairs={{1,2},{2,1},{5,6},{6,5},{9,10},{10,9},{13,14},{14,13},{17,18},{18,... | collective-permute-start | bytes 1572872 | tf_op jit(solution)/shard_map/ppermute | solution.py:453
  96.2 25.3 %collective-permute-start.18 = (f32[4,4,8,256]{3,2,1,0:T(8,128)S(1)}, f32[4,4,8,256]{3,2,1,0:T(8,128)S(1)}, u32[]{:S(2)}, u32[]{:S(2)}) collective-permute-start(f32[4,4,8,256]{3,2,1,0:T(8,128)S(1)} %get-tuple-element.144), channel_id=1, source_target_pairs={{4,9},{6,11},{5,8},{7,10},{12,17},{14,19},{13,16},{15,18},{20,25},... | collective-permute-start | bytes 393224 | tf_op jit(solution)/shard_map/ppermute | solution.py:456
  100.8 20.8 %collective-permute-start.19 = (f32[4,4,8,256]{3,2,1,0:T(8,128)S(1)}, f32[4,4,8,256]{3,2,1,0:T(8,128)S(1)}, u32[]{:S(2)}, u32[]{:S(2)}) collective-permute-start(f32[4,4,8,256]{3,2,1,0:T(8,128)S(1)} %get-tuple-element.145), channel_id=1, source_target_pairs={{5,10},{6,9},{13,18},{14,17},{21,26},{22,25},{29,34},{30,33},{37,4... | collective-permute-start | bytes 393224 | tf_op jit(solution)/shard_map/ppermute | solution.py:456
  121.6 1.5 copy-start.5
  122.4 3.1 %collective-permute-start.21 = (f32[4,40,8,256]{3,2,1,0:T(8,128)S(1)}, f32[4,40,8,256]{3,2,1,0:T(8,128)S(1)}, u32[]{:S(2)}, u32[]{:S(2)}) collective-permute-start(f32[4,40,8,256]{3,2,1,0:T(8,128)S(1)} %inner.7), channel_id=1, source_target_pairs={{0,4},{8,12},{16,20},{24,28},{32,36},{40,44},{48,52},{56,60},{64,6... | collective-permute-start | bytes 3932168 | tf_op jit(solution)/shard_map/ppermute | solution.py:478
  123.4 22.1 %copy-start.4 = (f32[1,1,128,16]{2,3,1,0:T(8,128)S(1)}, f32[1,1,128,16]{2,3,1,0:T(8,128)}, u32[]{:S(2)}) copy-start(f32[1,1,128,16]{2,3,1,0:T(8,128)} %param.13) | copy-start | bytes 24580
  171.2 15.3 %copy-start.3 = (f32[16,16]{1,0:T(8,128)}, f32[16,16]{1,0:T(8,128)S(1)}, u32[]{:S(2)}) copy-start(f32[16,16]{1,0:T(8,128)S(1)} %fusion) | copy-start | bytes 3076
